TPU v7x, 256 devices: a whole 4x4x8 slice. The times are simulated.
256 devices in a mesh: dom: 128 (over z, x, y), feat: 2 (over core).
Axes of the slice: x: 4, y: 4, z: 8, core: 2. Of those that a mesh axis runs over, the one named last changes fastest.
Arguments:
- features: bfloat16 [524288, 256], P('dom', 'feat'), may hold values from -6 to 6
- self_weight: bfloat16 [256, 256], P('feat'), may hold values from -0.375 to 0.375
- neighbor_weight: bfloat16 [256, 256], P('feat'), may hold values from -0.375 to 0.375
- tile_values: bfloat16 [20480, 128, 128], P('dom'), may hold values from 0 to 1
- tile_row: int32 [20480], P('dom'), may hold values from 0 to 31
- tile_owner: int32 [20480], P('dom'), may hold values from 0 to 127
- send_tile: int32 [16384], P('dom'), may hold values from 0 to 31
- tile_count: int32 [128], P('dom'), may hold values from 26 to 160, as said below
- hub_panel: bfloat16 [524288, 256], P('dom'), may hold values from 0 to 1
- hub_rows: int32 [256], P('dom'), may hold values from 0 to 4095
- cotangent: bfloat16 [524288, 256], P('dom', 'feat'), may hold values from -6 to 6
Outputs:
- layer_out: bfloat16 [524288, 256], P('dom', 'feat')
- self_grad: float32 [256, 256], P('feat')
- neighbor_grad: float32 [256, 256], P('feat')
- input_grad: float32 [524288, 256], P('dom', 'feat')
Inputs may be any that keep to these rules, and one draw needn't show every extreme that they name: `tile_count`: one partition has exactly 160 live slots in every draw.
All inputs are finite; a program needn't handle non-finite values.
Results may differ from a plain program's by a relative error of at most 0.011.
The roundings to bfloat16 on the way count: a program that leaves them out, or rounds other values in their place, can miss the bound.
Values may be sent and summed in bfloat16 or wider, within the bound.
No kernel may reach another device: no remote copies, remote signals or barrier semaphores. Data moves between devices by JAX's collectives and lax.ppermute only.
A program may use at most 128 MiB of HBM per device.

v0:
```python
import math

import jax
import jax.numpy as jnp
from jax import lax
from jax.sharding import PartitionSpec as P


def shards(
    features,
    self_weight,
    neighbor_weight,
    tile_values,
    tile_row,
    tile_owner,
    send_tile,
    tile_count,
    hub_panel,
    hub_rows,
    cotangent,
):
    rows_dev, half_width = features.shape
    tile_cap, tile_edge = (tile_values.shape[0], tile_values.shape[1])
    tiles_dev = rows_dev // tile_edge
    dom_size = lax.axis_size("dom")
    local_tiles = features.reshape(tiles_dev, tile_edge, half_width)
    outgoing = local_tiles[send_tile]
    hub_local = features[hub_rows]
    incoming = lax.all_to_all(outgoing, "dom", split_axis=0, concat_axis=0, tiled=True)
    hub_feats = lax.all_gather(hub_local, "dom", axis=0, tiled=True)
    live_mask = (jnp.arange(tile_cap) < tile_count[0]).astype(jnp.float32)
    columns = incoming[tile_owner]
    products = (
        jnp.einsum("kij,kjf->kif", tile_values, columns, preferred_element_type=jnp.float32)
        * live_mask[:, None, None]
    )
    neighbor_sums = jax.ops.segment_sum(products, tile_row, num_segments=tiles_dev).reshape(
        rows_dev, half_width
    )
    neighbor_sums = neighbor_sums + jnp.dot(
        hub_panel, hub_feats, preferred_element_type=jnp.float32
    )
    wide_values = tile_values.astype(jnp.float32)
    tile_squares = jnp.sum(wide_values * wide_values, axis=2) * live_mask[:, None]
    squares = jax.ops.segment_sum(tile_squares, tile_row, num_segments=tiles_dev).reshape(rows_dev)
    wide_panel = hub_panel.astype(jnp.float32)
    squares = squares + jnp.sum(wide_panel * wide_panel, axis=1)
    inverse_norm = lax.rsqrt(1.0 + squares)
    aggregate = (neighbor_sums * inverse_norm[:, None]).astype(jnp.bfloat16)
    partial_sums = jnp.dot(features, self_weight, preferred_element_type=jnp.float32) + jnp.dot(
        aggregate, neighbor_weight, preferred_element_type=jnp.float32
    )
    preact = lax.psum_scatter(partial_sums, "feat", scatter_dimension=1, tiled=True)
    layer_out = jnp.maximum(preact, 0.0).astype(jnp.bfloat16)
    slopes = jnp.where(preact > 0, cotangent.astype(jnp.float32), 0.0).astype(jnp.bfloat16)
    slopes_full = lax.all_gather(slopes, "feat", axis=1, tiled=True)
    self_term = jnp.einsum("vi,vo->io", features, slopes_full, preferred_element_type=jnp.float32)
    neighbor_term = jnp.einsum(
        "vi,vo->io", aggregate, slopes_full, preferred_element_type=jnp.float32
    )
    self_sum, neighbor_sum = lax.psum((self_term, neighbor_term), "dom")
    factor = 1.0 / math.sqrt(rows_dev * dom_size)
    direct = jnp.einsum("vo,io->vi", slopes_full, self_weight, preferred_element_type=jnp.float32)
    agg_slopes = (
        jnp.einsum("vo,io->vi", slopes_full, neighbor_weight, preferred_element_type=jnp.float32)
        * inverse_norm[:, None]
    ).astype(jnp.bfloat16)
    slope_tiles = agg_slopes.reshape(tiles_dev, tile_edge, half_width)[tile_row]
    tile_back = (
        jnp.einsum("kji,kjf->kif", tile_values, slope_tiles, preferred_element_type=jnp.float32)
        * live_mask[:, None, None]
    )
    owner_terms = jax.ops.segment_sum(tile_back, tile_owner, num_segments=dom_size).astype(
        jnp.bfloat16
    )
    hub_term = jnp.einsum("vh,vf->hf", hub_panel, agg_slopes, preferred_element_type=jnp.float32)
    returned = lax.all_to_all(owner_terms, "dom", split_axis=0, concat_axis=0, tiled=True)
    hub_grad = lax.psum_scatter(hub_term, "dom", scatter_dimension=0, tiled=True)
    owner_back = jax.ops.segment_sum(
        returned.astype(jnp.float32), send_tile, num_segments=tiles_dev
    ).reshape(rows_dev, half_width)
    input_grad = (direct + owner_back).at[hub_rows].add(hub_grad)
    return (layer_out, self_sum * factor, neighbor_sum * factor, input_grad)


def solution(mesh):
    placed = (
        P("dom", "feat"),
        P("feat", None),
        P("feat", None),
        P("dom", None, None),
        P("dom"),
        P("dom"),
        P("dom"),
        P("dom"),
        P("dom", None),
        P("dom"),
        P("dom", "feat"),
    )
    return jax.shard_map(
        shards,
        mesh=mesh,
        in_specs=placed,
        out_specs=(P("dom", "feat"), P("feat", None), P("feat", None), P("dom", "feat")),
        check_vma=False,
    )
```

profile of v0, /device:TPU:2, one launch (start us, length us, event | category | flops | bytes accessed | tf_op | source)
XLA Modules:
  0.0 917.0 jit_solution(794628782129374157)
XLA Ops:
  8.4 3.0 gather_fusion
  11.4 16.0 %all-to-all-start = ((bf16[128,128,128]{2,1,0:T(8,128)(2,1)}), bf16[128,128,128]{2,1,0:T(8,128)(2,1)}, u32[]{:S(2)}, u32[]{:S(2)}) async-start(bf16[128,128,128]{2,1,0:T(8,128)(2,1)} %gather_fusion), calls=%async_computation | async-start | bytes 8388608 | tf_op jit(solution)/shard_map/all_to_all | solution.py:29
  29.0 5.3 multiply_reduce_fusion
  35.4 404.6 %all-gather.1 = bf16[128,2,128]{2,1,0:T(2,128)(2,1)S(1)} all-gather(bf16[1,2,128]{2,1,0:T(2,128)(2,1)S(1)} %bitcast.58), channel_id=2, replica_groups=mesh['dom'=128,'feat'=2] {'dom'}, dimensions={0}, use_global_device_ids=true | all-gather | bytes 66048 | tf_op jit(solution)/shard_map/all_gather | solution.py:30
  440.7 2.7 fusion.10
  443.4 9.8 %gather_fusion.1 = bf16[160,128,128]{2,1,0:T(8,128)(2,1)} fusion(bf16[128,128,128]{2,1,0:T(8,128)(2,1)} %all-to-all-done, s32[1024]{0:T(1024)S(1)} %pad_clamp_fusion.2), kind=kCustom, calls=%fused_computation.1 | custom fusion | bytes 10486400 | tf_op jit(solution)/shard_map/gather | solution.py:32
  453.2 11.9 %multiply_bitcast_fusion.1 = f32[160,128,128]{1,2,0:T(8,128)} fusion(f32[160]{0:T(256)S(1)} %compare_convert_fusion, bf16[160,128,128]{2,1,0:T(8,128)(2,1)} %gather_fusion.1, bf16[160,128,128]{2,1,0:T(8,128)(2,1)} %param.14), kind=kOutput, calls=%fused_computation.11 | convolution fusion | flops 673710080 | bytes 20972160 | tf_op jit(solution)/shard_map/kij,kjf->kif/dot_general | solution.py:34
  465.1 11.7 %copy.35 = f32[160,128,128]{2,1,0:T(8,128)} copy(f32[160,128,128]{1,2,0:T(8,128)} %multiply_bitcast_fusion.1) | data formatting | bytes 20971520 | tf_op jit(solution)/shard_map/mul | solution.py:34
  477.1 21.2 %scatter_fusion = f32[32,128,128]{2,1,0:T(8,128)S(1)} fusion(f32[32,128,128]{2,1,0:T(8,128)S(1)} %broadcast.32.clone, s32[160]{0:T(256)S(1)} %copy-done.9, f32[160,128,128]{2,1,0:T(8,128)} %copy.35), kind=kCustom, calls=%fused_computation.4 | custom fusion | flops 2621440 | bytes 31457920 | tf_op jit(solution)/shard_map/scatter-add | solution.py:37
  498.3 1.8 copy.49
  500.1 3.2 fusion.2
  504.3 2.7 convolution_add_fusion
  507.3 23.7 %reduce-scatter.3.cloned.1.call-done = f32[4096,128]{1,0:T(8,128)} async-done(((f32[4096,256]{1,0:T(8,128)}), f32[4096,128]{1,0:T(8,128)}) %reduce-scatter.3.cloned.1.call-update) | async-done | bytes 2097168 | tf_op jit(solution)/shard_map/reduce_scatter | solution.py:53
  531.0 2.8 select_convert_fusion
  533.9 17.1 %all-gather.4.cloned.1.call-done = bf16[4096,256]{1,0:T(8,128)(2,1)} async-done(((bf16[4096,128]{1,0:T(8,128)(2,1)}), bf16[4096,256]{1,0:T(8,128)(2,1)}) %all-gather.4.cloned.1.call-update) | async-done | bytes 2097168 | tf_op jit(solution)/shard_map/all_gather | solution.py:56
  551.0 2.4 fusion.3
  554.1 7.7 gather_fusion.3
  561.8 10.4 %multiply_bitcast_fusion = f32[160,128,128]{1,2,0:T(8,128)} fusion(f32[160]{0:T(256)S(1)} %compare_convert_fusion, bf16[160,128,128]{2,1,0:T(8,128)(2,1)} %gather_fusion.3, bf16[160,128,128]{2,1,0:T(8,128)(2,1)} %param.14), kind=kOutput, calls=%fused_computation.9 | convolution fusion | flops 673710080 | bytes 20972160 | tf_op jit(solution)/shard_map/kji,kjf->kif/dot_general | solution.py:70
  572.2 11.7 %copy.41 = f32[160,128,128]{2,1,0:T(8,128)} copy(f32[160,128,128]{1,2,0:T(8,128)} %multiply_bitcast_fusion) | data formatting | bytes 20971520 | tf_op jit(solution)/shard_map/mul | solution.py:70
  583.9 4.4 broadcast_in_dim.42
  588.3 33.5 %scatter_fusion.1 = f32[128,128,128]{2,1,0:T(8,128)} fusion(f32[128,128,128]{2,1,0:T(8,128)} %broadcast_in_dim.42, s32[160]{0:T(256)S(1)} %copy-done.10, f32[160,128,128]{2,1,0:T(8,128)} %copy.41), kind=kCustom, calls=%fused_computation.6 | custom fusion | flops 2621440 | bytes 31457920 | tf_op jit(solution)/shard_map/scatter-add | solution.py:73
  621.8 6.3 convert_element_type.46
  628.1 14.2 %all-to-all-start.1 = ((bf16[128,128,128]{2,1,0:T(8,128)(2,1)}), bf16[128,128,128]{2,1,0:T(8,128)(2,1)}, u32[]{:S(2)}, u32[]{:S(2)}) async-start(bf16[128,128,128]{2,1,0:T(8,128)(2,1)} %convert_element_type.46), calls=%async_computation.2 | async-start | bytes 8388608 | tf_op jit(solution)/shard_map/all_to_all | solution.py:77
  643.9 3.0 convolution_bitcast_fusion.1
  646.9 2.8 fusion.11
  649.7 1.4 convolution_bitcast_fusion.2
  651.2 2.7 maximum_convert_fusion
  653.9 222.2 %all-reduce.4.cloned.1.call-done = (f32[128,256]{0,1:T(8,128)}, f32[128,256]{0,1:T(8,128)}, f32[256,128]{0,1:T(8,128)}) async-done(((f32[128,256]{0,1:T(8,128)}, f32[128,256]{0,1:T(8,128)}, f32[256,128]{0,1:T(8,128)}), (f32[128,256]{0,1:T(8,128)}, f32[128,256]{0,1:T(8,128)}, f32[256,128]{0,1:T(8,128)})) %all-reduce.4.cloned.1.call-update) | async-done | bytes 393232 | tf_op jit(solution)/shard_map/psum | solution.py:61
  879.5 6.5 convert_element_type.47
  886.3 17.1 %scatter_fusion.2 = f32[32,128,128]{2,1,0:T(8,128)S(1)} fusion(f32[32,128,128]{2,1,0:T(8,128)S(1)} %broadcast.32, s32[128]{0:T(128)S(1)} %copy-done.11, f32[128,128,128]{2,1,0:T(8,128)} %convert_element_type.47), kind=kCustom, calls=%fused_computation.7 | custom fusion | flops 2097152 | bytes 25166336 | tf_op jit(solution)/shard_map/scatter-add | solution.py:79
  903.4 3.6 convolution_add_fusion.1
  907.0 3.5 scatter_fusion.3
  (58 shorter events, 10.5 us)
Async XLA Ops:
  7.2 1.2 copy-start
  11.4 16.9 %copy-start.12 = (s32[2]{0:T(128)S(1)}, s32[2]{0:T(128)}, u32[]{:S(2)}) copy-start(s32[2]{0:T(128)} %param.20) | copy-start | bytes 28
  11.4 431.9 %all-to-all-start = ((bf16[128,128,128]{2,1,0:T(8,128)(2,1)}), bf16[128,128,128]{2,1,0:T(8,128)(2,1)}, u32[]{:S(2)}, u32[]{:S(2)}) async-start(bf16[128,128,128]{2,1,0:T(8,128)(2,1)} %gather_fusion), calls=%async_computation | async-start | bytes 8388608 | tf_op jit(solution)/shard_map/all_to_all | solution.py:29
  27.5 6.8 copy-start.9
  27.5 412.5 %copy-start.10 = (s32[160]{0:T(256)S(1)}, s32[160]{0:T(256)}, u32[]{:S(2)}) copy-start(s32[160]{0:T(256)} %param.16) | copy-start | bytes 1924
  27.5 412.5 %copy-start.3 = (bf16[4096,256]{1,0:T(8,128)(2,1)S(1)}, bf16[4096,256]{1,0:T(8,128)(2,1)}, u32[]{:S(2)}) copy-start(bf16[4096,256]{1,0:T(8,128)(2,1)} %param.19) | copy-start | bytes 6291460
  27.5 413.2 %copy-start.8 = (bf16[128,256]{1,0:T(8,128)(2,1)S(1)}, bf16[128,256]{1,0:T(8,128)(2,1)}, u32[]{:S(2)}) copy-start(bf16[128,256]{1,0:T(8,128)(2,1)} %param.12) | copy-start | bytes 196612
  27.5 503.5 %reduce-scatter.3.cloned.1.call-start = ((), (), s32[]{:S(2)}) async-start(), calls=%async_computation.3 | async-start | bytes 6291456 | tf_op jit(solution)/shard_map/reduce_scatter | solution.py:53
  498.3 6.0 copy-start.7
  500.1 4.2 copy-start.2
  503.3 1.0 copy-start.5
  507.0 24.0 %copy-start.6 = (bf16[4096,128]{1,0:T(8,128)(2,1)S(1)}, bf16[4096,128]{1,0:T(8,128)(2,1)}, u32[]{:S(2)}) copy-start(bf16[4096,128]{1,0:T(8,128)(2,1)} %param.21) | copy-start | bytes 3145732
  507.0 44.0 %all-gather.4.cloned.1.call-start = ((), (), s32[]{:S(2)}) async-start(), calls=%async_computation.4 | async-start | bytes 3145728 | tf_op jit(solution)/shard_map/all_gather | solution.py:56
  553.4 8.4 copy-start.4
  628.1 14.6 %copy-start.13 = (u32[256]{0:T(256)S(1)}, u32[256]{0:T(256)}, u32[]{:S(2)}) copy-start(u32[256]{0:T(256)} %constant.28) | copy-start | bytes 3076
  628.1 18.8 %copy-start.1 = (bf16[4096,256]{1,0:T(8,128)(2,1)S(1)}, bf16[4096,256]{1,0:T(8,128)(2,1)}, u32[]{:S(2)}) copy-start(bf16[4096,256]{1,0:T(8,128)(2,1)} %all-gather.4.cloned.1.call-done) | copy-start | bytes 6291460
  628.1 251.4 %all-to-all-start.1 = ((bf16[128,128,128]{2,1,0:T(8,128)(2,1)}), bf16[128,128,128]{2,1,0:T(8,128)(2,1)}, u32[]{:S(2)}, u32[]{:S(2)}) async-start(bf16[128,128,128]{2,1,0:T(8,128)(2,1)} %convert_element_type.46), calls=%async_computation.2 | async-start | bytes 8388608 | tf_op jit(solution)/shard_map/all_to_all | solution.py:77
  642.4 233.7 %all-reduce.4.cloned.1.call-start = ((), (), s32[]{:S(2)}) async-start(), calls=%async_computation.5 | async-start | bytes 786432 | tf_op jit(solution)/shard_map/psum | solution.py:61
  879.5 6.8 copy-start.11
Sparse Core Ops, SparseCore 0:
  507.1 23.8 reduce-scatter.2
  534.0 16.9 all-gather.3
  651.3 224.6 all-reduce.3
where the time goes:
time: 919 us; the launch traced here: 917 us
  blocking collectives  405 us (44%)
  waiting for transfers between devices  263 us (29%)
  other arithmetic  102 us (11%)
  local copies, waits for them, and re-layouts  56.5 us (6%)
  matrix products  44.1 us (5%)
  starting transfers between devices  30.9 us (3%)
  between operations  15.5 us (2%)
    all_gather x1, blocking collectives, shards(): hub_feats = lax.all_gather(hub_local, 'dom', axis=0, tiled=True)  405 us
    psum x1, waiting for transfers between devices, shards(): self_sum, neighbor_sum = lax.psum((self_term, neighbor_term), 'dom')  222 us
    scatter-add x1, other arithmetic, shards(): jax.ops.segment_sum(tile_back, tile_owner, num_segments=dom_size)  33.5 us
    reduce_scatter x1, waiting for transfers between devices, shards(): lax.psum_scatter(partial_sums, 'feat', scatter_dimension=1, tiled=True)  23.7 us
    scatter-add x1, other arithmetic, shards(): jax.ops.segment_sum(products, tile_row, num_segments=tiles_dev)  21.2 us
  transfers between devices with their start and end apart: 5, of which 3 were waited for; matrix products, arithmetic and copies ran while one was open for 3% of the time, Pallas kernels for 0%

commit v1 on v0

v1 whole, which is shorter than its diff:
```python
import math

import jax
import jax.numpy as jnp
from jax import lax
from jax.experimental import pallas as pl
from jax.experimental.pallas import tpu as pltpu
from jax.sharding import PartitionSpec as P

F32 = jnp.float32
BF16 = jnp.bfloat16
MIB = 1 << 20


def dot(a, b, dims):
    return lax.dot_general(a, b, (dims, ((), ())), preferred_element_type=F32)


NN = ((1,), (0,))
NT = ((1,), (1,))
TN = ((0,), (0,))


def params(mib, steps):
    return pltpu.CompilerParams(
        dimension_semantics=("arbitrary",) * steps, vmem_limit_bytes=mib * MIB
    )


def pack_kernel(send, hubs, feat, out, hub_rows):
    step = pl.program_id(0)
    per_step, edge = out.shape[0], out.shape[1] - 8

    @pl.when(step == 0)
    def _():
        hub_rows[...] = jnp.zeros_like(hub_rows)
        for j in range(2):
            row = hubs[j]
            base = pl.multiple_of((row // 16) * 16, 16)
            block = feat[pl.ds(base, 16), :].astype(F32)
            here = lax.broadcasted_iota(jnp.int32, block.shape, 0) == row - base
            hub_rows[j : j + 1, :] = jnp.sum(
                jnp.where(here, block, 0.0), axis=0, keepdims=True
            )

    extra = hub_rows[...].astype(BF16)
    for i in range(per_step):
        start = pl.multiple_of(send[step * per_step + i] * edge, edge)
        out[i, :edge, :] = feat[pl.ds(start, edge), :]
        out[i, edge:, :] = extra


def pack(features, send_tile, hub_rows, edge):
    rows, width = features.shape
    parts = send_tile.shape[0]
    per_step = 16
    return pl.pallas_call(
        pack_kernel,
        name="pack",
        out_shape=jax.ShapeDtypeStruct((parts, edge + 8, width), BF16),
        grid_spec=pltpu.PrefetchScalarGridSpec(
            num_scalar_prefetch=2,
            grid=(parts // per_step,),
            in_specs=[pl.BlockSpec((rows, width), lambda g, *_: (0, 0))],
            out_specs=pl.BlockSpec((per_step, edge + 8, width), lambda g, *_: (g, 0, 0)),
            scratch_shapes=[pltpu.VMEM((8, width), F32)],
        ),
        compiler_params=params(16, 1),
    )(send_tile, hub_rows, features)


def prepare_kernel(
    row, count, order, first, second, kinds, values, panel, inv, flipped, pairs, squares
):
    step, steps = pl.program_id(0), pl.num_programs(0)
    edge = values.shape[1]
    slots, duos = flipped.shape[0], pairs.shape[0]

    @pl.when(step == 0)
    def _():
        squares[...] = jnp.zeros_like(squares)

    @pl.loop(0, slots)
    def _(i):
        k = step * slots + i
        flipped[i] = values[order[k]].T
        tile = values[k].astype(F32)
        live = (k < count[0]).astype(F32)
        start = pl.multiple_of(row[k] * edge, edge)
        squares[pl.ds(start, edge), :] += tile * tile * live

    @pl.loop(0, duos)
    def _(i):
        p = step * duos + i
        has_first = (kinds[p] > 0).astype(BF16)
        has_second = (kinds[p] > 1).astype(BF16)
        pairs[i, :, :edge] = values[first[p]] * has_first
        pairs[i, :, edge:] = values[second[p]] * has_second

    @pl.when(step == steps - 1)
    def _():
        @pl.loop(0, squares.shape[0] // edge)
        def _(t):
            at = pl.ds(pl.multiple_of(t * edge, edge), edge)
            wide = panel[at, :].astype(F32)
            wide = wide * wide
            half = wide.shape[1] // 2
            total = jnp.sum(
                squares[at, :] + wide[:, :half] + wide[:, half:], axis=1, keepdims=True
            )
            inv[at, :] = jnp.broadcast_to(lax.rsqrt(1.0 + total), (edge, inv.shape[1]))


def prepare(row, count, order, first, second, kinds, values, panel, duos):
    slots, edge, _ = values.shape
    rows, hubs = panel.shape
    steps = 4
    whole = lambda g, *_: (0, 0)
    return pl.pallas_call(
        prepare_kernel,
        name="prepare",
        out_shape=(
            jax.ShapeDtypeStruct((rows, edge), F32),
            jax.ShapeDtypeStruct((slots, edge, edge), BF16),
            jax.ShapeDtypeStruct((duos, edge, 2 * edge), BF16),
        ),
        grid_spec=pltpu.PrefetchScalarGridSpec(
            num_scalar_prefetch=6,
            grid=(steps,),
            in_specs=[
                pl.BlockSpec((slots, edge, edge), lambda g, *_: (0, 0, 0)),
                pl.BlockSpec((rows, hubs), whole),
            ],
            out_specs=(
                pl.BlockSpec((rows, edge), whole),
                pl.BlockSpec((slots // steps, edge, edge), lambda g, *_: (g, 0, 0)),
                pl.BlockSpec((duos // steps, edge, 2 * edge), lambda g, *_: (g, 0, 0)),
            ),
            scratch_shapes=[pltpu.VMEM((rows, edge), F32)],
        ),
        compiler_params=params(40, 1),
        cost_estimate=pl.CostEstimate(
            flops=60_000_000_000, bytes_accessed=40_000_000, transcendentals=0
        ),
    )(row, count, order, first, second, kinds, values, panel)


def gather_kernel(row, owner_a, owner_b, n_duos, pairs, incoming, panel, inv, out, sums):
    step, steps = pl.program_id(0), pl.num_programs(0)
    duos, edge, _ = pairs.shape
    parts = incoming.shape[0]

    @pl.when(step == 0)
    def _():
        tail = incoming[:, edge:, :].reshape(parts * 8, incoming.shape[2])
        h = lax.broadcasted_iota(jnp.int32, (2 * parts, parts * 8), 0)
        r = lax.broadcasted_iota(jnp.int32, (2 * parts, parts * 8), 1)
        pick = (r == (h // 2) * 8 + h % 2).astype(F32).astype(BF16)
        hub_feats = dot(pick, tail, NN).astype(BF16)

        @pl.loop(0, sums.shape[0] // 512)
        def _(t):
            at = pl.ds(pl.multiple_of(t * 512, 512), 512)
            sums[at, :] = dot(panel[at, :], hub_feats, NN)

    @pl.when(step * duos < n_duos[0])
    def _():
        products = []
        for i in range(duos):
            p = step * duos + i
            columns = jnp.concatenate(
                [incoming[owner_a[p], :edge, :], incoming[owner_b[p], :edge, :]], axis=0
            )
            products.append(dot(pairs[i], columns, NN))
        for i in range(duos):
            start = pl.multiple_of(row[step * duos + i] * edge, edge)
            sums[pl.ds(start, edge), :] += products[i]

    @pl.when(step == steps - 1)
    def _():
        @pl.loop(0, sums.shape[0] // 512)
        def _(t):
            at = pl.ds(pl.multiple_of(t * 512, 512), 512)
            out[at, :] = (sums[at, :] * inv[at, :]).astype(BF16)


def gather(row, owner_a, owner_b, n_duos, pairs, incoming, panel, inv):
    duos, edge, _ = pairs.shape
    rows, hubs = panel.shape
    per_step = 8
    whole = lambda g, *_: (0, 0)

    def block(g, row, owner_a, owner_b, n_duos):
        return (jnp.minimum(g, (n_duos[0] - 1) // per_step), 0, 0)

    return pl.pallas_call(
        gather_kernel,
        name="gather",
        out_shape=jax.ShapeDtypeStruct((rows, edge), BF16),
        grid_spec=pltpu.PrefetchScalarGridSpec(
            num_scalar_prefetch=4,
            grid=(duos // per_step,),
            in_specs=[
                pl.BlockSpec((per_step, edge, 2 * edge), block),
                pl.BlockSpec(incoming.shape, lambda g, *_: (0, 0, 0)),
                pl.BlockSpec((rows, hubs), whole),
                pl.BlockSpec((rows, edge), whole),
            ],
            out_specs=pl.BlockSpec((rows, edge), whole),
            scratch_shapes=[pltpu.VMEM((rows, edge), F32)],
        ),
        compiler_params=params(40, 1),
    )(row, owner_a, owner_b, n_duos, pairs, incoming, panel, inv)


def middle_kernel(
    feat, feat_peer, agg, agg_peer, cot, cot_peer, inv, panel, own_w, nbr_w,
    layer, slopes_out, agg_slopes_out, extra, hub_acc, grad_acc,
):
    step, steps = pl.program_id(0), pl.num_programs(0)
    half = feat.shape[1]
    x = feat[...]
    a = agg[...]
    preact = dot(jnp.concatenate([x, feat_peer[...]], axis=1), own_w[...], NN) + dot(
        jnp.concatenate([a, agg_peer[...]], axis=1), nbr_w[...], NN
    )
    layer[...] = jnp.maximum(preact[:, :half], 0.0).astype(BF16)
    cotangent = jnp.concatenate([cot[...], cot_peer[...]], axis=1).astype(F32)
    slopes = jnp.where(preact > 0, cotangent, 0.0).astype(BF16)
    slopes_out[...] = slopes
    agg_slopes = (dot(slopes, nbr_w[:half, :], NT) * inv[...]).astype(BF16)
    agg_slopes_out[...] = agg_slopes
    hub = dot(panel[...], agg_slopes, TN)
    grads = dot(jnp.concatenate([x, a], axis=1), slopes, TN)

    @pl.when(step == 0)
    def _():
        hub_acc[...] = hub
        grad_acc[...] = grads

    @pl.when(step > 0)
    def _():
        hub_acc[...] += hub
        grad_acc[...] += grads

    @pl.when(step == steps - 1)
    def _():
        n = half
        extra[...] = jnp.zeros_like(extra)
        for j in range(2):
            extra[pl.ds(j, n, stride=8), :] = hub_acc[pl.ds(j, n, stride=2), :]
            for c in range(2):
                extra[pl.ds(2 + 2 * j + c, n, stride=8), :] = grad_acc[
                    j * n : (j + 1) * n, c * n : (c + 1) * n
                ]


def middle(feat, feat_peer, agg, agg_peer, cot, cot_peer, inv, panel, own_w, nbr_w):
    rows, half = feat.shape
    hubs = panel.shape[1]
    block = 512
    by_row = lambda width: pl.BlockSpec((block, width), lambda g: (g, 0))
    whole = lambda shape: pl.BlockSpec(shape, lambda g: (0, 0))
    return pl.pallas_call(
        middle_kernel,
        name="middle",
        out_shape=(
            jax.ShapeDtypeStruct((rows, half), BF16),
            jax.ShapeDtypeStruct((rows, 2 * half), BF16),
            jax.ShapeDtypeStruct((rows, half), BF16),
            jax.ShapeDtypeStruct((8 * half, half), F32),
        ),
        grid=(rows // block,),
        in_specs=[by_row(half)] * 7
        + [by_row(hubs), whole(own_w.shape), whole(nbr_w.shape)],
        out_specs=(by_row(half), by_row(2 * half), by_row(half), whole((8 * half, half))),
        scratch_shapes=[
            pltpu.VMEM((hubs, half), F32),
            pltpu.VMEM((2 * half, 2 * half), F32),
        ],
        compiler_params=params(32, 1),
    )(feat, feat_peer, agg, agg_peer, cot, cot_peer, inv, panel, own_w, nbr_w)


def back_kernel(order_row, order_owner, same, live, count, flipped, slopes, *rest):
    extra = rest[0] if len(rest) == 3 else None
    out, carry = rest[-2:]
    step = pl.program_id(0)
    slots, part, edge = flipped.shape

    @pl.when(step == 0)
    def _():
        out[:, :part, :] = jnp.zeros((out.shape[0], part, out.shape[2]), out.dtype)
        carry[...] = jnp.zeros_like(carry)
        if extra is not None:
            out[:, part:, :] = extra[...].astype(BF16)

    @pl.when(step * slots < count[0])
    def _():
        products = []
        for i in range(slots):
            start = pl.multiple_of(order_row[step * slots + i] * edge, edge)
            products.append(dot(flipped[i], slopes[pl.ds(start, edge), :], NN))
        total = carry[...]
        for i in range(slots):
            k = step * slots + i
            total = products[i] * live[k].astype(F32) + total * same[k].astype(F32)
            out[order_owner[k], :part, :] = total.astype(BF16)
        carry[...] = total


def back(order_row, order_owner, same, live, count, flipped, slopes, extra, side):
    slots, edge, _ = flipped.shape
    rows, half = slopes.shape
    part = edge // 2
    parts = 128 if extra is None else extra.shape[0]
    per_step = 16

    def block(g, order_row, order_owner, same, live, count):
        return (jnp.minimum(g, (count[0] - 1) // per_step), side, 0)

    height = part + (8 if extra is not None else 0)
    in_specs = [
        pl.BlockSpec((per_step, part, edge), block),
        pl.BlockSpec((rows, half), lambda g, *_: (0, 0)),
    ]
    args = [flipped, slopes]
    if extra is not None:
        in_specs.append(pl.BlockSpec(extra.shape, lambda g, *_: (0, 0, 0)))
        args.append(extra)
    return pl.pallas_call(
        back_kernel,
        name=f"back_{side}",
        out_shape=jax.ShapeDtypeStruct((parts, height, half), BF16),
        grid_spec=pltpu.PrefetchScalarGridSpec(
            num_scalar_prefetch=5,
            grid=(slots // per_step,),
            in_specs=in_specs,
            out_specs=pl.BlockSpec((parts, height, half), lambda g, *_: (0, 0, 0)),
            scratch_shapes=[pltpu.VMEM((part, half), F32)],
        ),
        compiler_params=params(32, 1),
    )(order_row, order_owner, same, live, count, *args)


def finish_first_kernel(send, hubs, slopes, own_w, returned, out, share):
    parts, height, half = returned.shape
    tiles, edge = out.shape[0], out.shape[1]
    part = height - 8

    @pl.loop(0, tiles)
    def _(t):
        at = pl.ds(pl.multiple_of(t * edge, edge), edge)
        out[t] = dot(slopes[at, :], own_w[...], NT)

    total = jnp.zeros((8, half), F32)
    for p in range(parts):
        out[send[p], :part, :] += returned[p, :part, :].astype(F32)
        total = total + returned[p, part:, :].astype(F32)
    share[...] = total
    for j in range(2):
        row = hubs[j]
        tile, inside = row // edge, row % edge
        base = pl.multiple_of((inside // 8) * 8, 8)
        here = lax.broadcasted_iota(jnp.int32, (8, half), 0) == inside - base
        out[tile, pl.ds(base, 8), :] += jnp.where(here, total[j : j + 1, :], 0.0)


def finish_first(send_tile, hub_rows, slopes, own_w, returned, edge):
    rows = slopes.shape[0]
    half = returned.shape[2]
    smem = pl.BlockSpec(memory_space=pltpu.SMEM)
    vmem = pl.BlockSpec(memory_space=pltpu.VMEM)
    return pl.pallas_call(
        finish_first_kernel,
        name="finish_first",
        out_shape=(
            jax.ShapeDtypeStruct((rows // edge, edge, half), F32),
            jax.ShapeDtypeStruct((8, half), F32),
        ),
        in_specs=[smem, smem, vmem, vmem, vmem],
        out_specs=(vmem, vmem),
        compiler_params=pltpu.CompilerParams(vmem_limit_bytes=24 * MIB),
    )(send_tile, hub_rows, slopes, own_w, returned)


def finish_second_kernel(send, returned, before, out):
    out[...] = before[...]
    for p in range(returned.shape[0]):
        out[send[p]] += returned[p].astype(F32)


def finish_second(send_tile, returned, before):
    tiles, edge, half = before.shape
    spec = pl.BlockSpec((tiles, edge // 2, half), lambda g, *_: (0, 1, 0))
    return pl.pallas_call(
        finish_second_kernel,
        name="finish_second",
        out_shape=jax.ShapeDtypeStruct(before.shape, F32),
        grid_spec=pltpu.PrefetchScalarGridSpec(
            num_scalar_prefetch=1,
            grid=(1,),
            in_specs=[pl.BlockSpec(returned.shape, lambda g, *_: (0, 0, 0)), spec],
            out_specs=spec,
        ),
        input_output_aliases={2: 0},
        compiler_params=params(24, 1),
    )(send_tile, returned, before)


def plan(tile_row, tile_owner, tile_count, tiles, parts):
    slots = tile_row.shape[0]
    index = jnp.arange(slots, dtype=jnp.int32)
    live = index < tile_count[0]
    earlier = index[None, :] < index[:, None]
    pick = lambda where, what: jnp.sum(jnp.where(where, what, 0), axis=1, dtype=jnp.int32)

    key = jnp.where(live, tile_owner, parts)
    before = (key[None, :] < key[:, None]) | ((key[None, :] == key[:, None]) & earlier)
    rank = jnp.sum(before, axis=1, dtype=jnp.int32)
    last = jnp.minimum(index, tile_count[0] - 1)
    at = rank[None, :] == last[:, None]
    order = pick(at, index[None, :])
    order_row = pick(at, tile_row[None, :])
    order_owner = pick(at, tile_owner[None, :])
    same = jnp.concatenate([jnp.zeros((1,), jnp.int32), (order_owner[1:] == order_owner[:-1]).astype(jnp.int32)])
    live_int = live.astype(jnp.int32)

    mates = live[None, :] & (tile_row[None, :] == tile_row[:, None])
    inside = jnp.sum(mates & earlier, axis=1, dtype=jnp.int32)
    rows = jnp.arange(tiles, dtype=jnp.int32)
    per_row = jnp.sum(live[None, :] & (tile_row[None, :] == rows[:, None]), axis=1, dtype=jnp.int32)
    row_pairs = (per_row + 1) // 2
    lower = jnp.sum(
        jnp.where(rows[None, :] < tile_row[:, None], row_pairs[None, :], 0), axis=1, dtype=jnp.int32
    )
    pair = jnp.where(live, lower + inside // 2, -1)
    duos = (slots + tiles) // 2
    p = jnp.arange(duos, dtype=jnp.int32)
    is_first = (pair[None, :] == p[:, None]) & (inside[None, :] % 2 == 0)
    is_second = (pair[None, :] == p[:, None]) & (inside[None, :] % 2 == 1)
    first = pick(is_first, index[None, :])
    second = pick(is_second, index[None, :])
    owner_a = pick(is_first, tile_owner[None, :])
    owner_b = pick(is_second, tile_owner[None, :])
    pair_row = pick(is_first, tile_row[None, :])
    kinds = pick(is_first, 1) + pick(is_second, 1)
    n_duos = jnp.sum(row_pairs, dtype=jnp.int32).reshape(1)
    return (
        (order, order_row, order_owner, same, live_int),
        (first, second, kinds, pair_row, owner_a, owner_b, n_duos),
        duos,
    )


def exchange(block):
    return lax.all_to_all(block, "dom", split_axis=0, concat_axis=0, tiled=True)


def swap(block):
    return lax.ppermute(block, "feat", [(0, 1), (1, 0)])


def shards(
    features,
    self_weight,
    neighbor_weight,
    tile_values,
    tile_row,
    tile_owner,
    send_tile,
    tile_count,
    hub_panel,
    hub_rows,
    cotangent,
):
    rows_dev, half = features.shape
    tile_edge = tile_values.shape[1]
    tiles_dev = rows_dev // tile_edge
    dom_size = lax.axis_size("dom")
    core = lax.axis_index("feat")

    outgoing = pack(features, send_tile, hub_rows, tile_edge)
    incoming = exchange(outgoing)

    def own_first(w):
        return jnp.where(core == 0, w, jnp.concatenate([w[:, half:], w[:, :half]], axis=1))

    weights = own_first(jnp.concatenate([self_weight, neighbor_weight], axis=0))
    peer_weights = swap(weights)
    peer_weights = jnp.concatenate([peer_weights[:, half:], peer_weights[:, :half]], axis=1)
    own_w = jnp.concatenate([weights[:half], peer_weights[:half]], axis=0)
    nbr_w = jnp.concatenate([weights[half:], peer_weights[half:]], axis=0)
    feat_peer = swap(features)
    cot_peer = swap(cotangent)

    by_owner, by_row, duos = plan(tile_row, tile_owner, tile_count, tiles_dev, dom_size)
    order, order_row, order_owner, same, live = by_owner
    first, second, kinds, pair_row, owner_a, owner_b, n_duos = by_row
    inv, flipped, pairs = prepare(
        tile_row, tile_count, order, first, second, kinds, tile_values, hub_panel, duos
    )

    aggregate = gather(pair_row, owner_a, owner_b, n_duos, pairs, incoming, hub_panel, inv)
    agg_peer = swap(aggregate)
    layer_out, slopes, agg_slopes, extra = middle(
        features, feat_peer, aggregate, agg_peer, cotangent, cot_peer, inv, hub_panel, own_w, nbr_w
    )
    extra = extra.reshape(dom_size, 8, half)
    back_args = (order_row, order_owner, same, live, tile_count, flipped, agg_slopes)
    returned_a = exchange(back(*back_args, extra, 0))
    returned_b = exchange(back(*back_args, None, 1))

    partial_grad, share = finish_first(
        send_tile, hub_rows, slopes, own_w[:half], returned_a, tile_edge
    )
    grads = exchange(jnp.broadcast_to(share[None, 2:6], (dom_size, 4, half)))
    input_grad = finish_second(send_tile, returned_b, partial_grad).reshape(rows_dev, half)

    grads = grads * (1.0 / math.sqrt(rows_dev * dom_size))
    sides = [jnp.concatenate([grads[:, 2 * j], grads[:, 2 * j + 1]], axis=1) for j in range(2)]
    self_grad, neighbor_grad = (own_first(side) for side in sides)
    return (layer_out, self_grad, neighbor_grad, input_grad)


def solution(mesh):
    placed = (
        P("dom", "feat"),
        P("feat", None),
        P("feat", None),
        P("dom", None, None),
        P("dom"),
        P("dom"),
        P("dom"),
        P("dom"),
        P("dom", None),
        P("dom"),
        P("dom", "feat"),
    )
    return jax.shard_map(
        shards,
        mesh=mesh,
        in_specs=placed,
        out_specs=(P("dom", "feat"), P("feat", None), P("feat", None), P("dom", "feat")),
        check_vma=False,
    )
```

time: 919 us -> 306 us (0.33)
  blocking collectives: 405 us -> 0 us
  other arithmetic: 102 us -> 2.6 us
  waiting for transfers between devices: 263 us -> 178 us
  Pallas kernels: 0 us -> 57.2 us
  matrix products: 44.1 us -> 0 us
  local copies, waits for them, and re-layouts: 56.5 us -> 19.7 us
  starting transfers between devices: 30.9 us -> 45.4 us
  between operations: 15.5 us -> 1.68 us
    all_gather x1 -> x0, blocking collectives: 405 us -> none  [shards(): hub_feats = lax.all_gather(hub_local, 'dom', axis=0, tiled=True)]
    psum x1 -> x0, waiting for transfers between devices: 222 us -> none  [shards(): self_sum, neighbor_sum = lax.psum((self_term, neighbor_term), 'dom')]
    all_to_all x2 -> x4, waiting for transfers between devices: 0.01 us -> 176 us  [exchange(): return lax.all_to_all(block, 'dom', split_axis=0, concat_axis=0, tiled=True)]
    scatter-add x5 -> x0, other arithmetic: 76.4 us -> none  [the longest x1 33.5 us: shards(): jax.ops.segment_sum(tile_back, tile_owner, num_segments=dom_size)]
    pallas_call x0 -> x8, Pallas kernels: none -> 57.2 us  [the longest x1 21.9 us: prepare(): pl.pallas_call(prepare_kernel, name='prepare', out_shape=(jax.ShapeDtypeS...]
    dot_general x10 -> x0, matrix products: 44.1 us -> none  [the longest x1 11.9 us: shards(): jnp.einsum('kij,kjf->kif', tile_values, columns, preferred_element_type=j...]
    reduce_scatter x1 -> x0, waiting for transfers between devices: 23.7 us -> none  [shards(): lax.psum_scatter(partial_sums, 'feat', scatter_dimension=1, tiled=True)]
    mul x2 -> x0, local copies, waits for them, and re-layouts: 23.5 us -> none  [the longest x1 11.7 us: shards(): jnp.einsum('kij,kjf->kif', tile_values, columns, preferred_element_type=j...]
  transfers between devices with their start and end apart: 5 -> 8, of which waited for: 3 -> 5; matrix products, arithmetic and copies ran while one was open for 3% -> 1% of each run, Pallas kernels for 0% -> 15%
where the time goes in v1:
time: 306 us; the launch traced here: 304 us
  waiting for transfers between devices  178 us (58%)
  Pallas kernels  57.2 us (19%)
  starting transfers between devices  45.4 us (15%)
  local copies, waits for them, and re-layouts  19.7 us (6%)
    all_to_all x4, waiting for transfers between devices, exchange(): return lax.all_to_all(block, 'dom', split_axis=0, concat_axis=0, tiled=True)  176 us
    all_to_all x4, starting transfers between devices, exchange(): return lax.all_to_all(block, 'dom', split_axis=0, concat_axis=0, tiled=True)  44.6 us
    pallas_call x1, Pallas kernels, prepare(): pl.pallas_call(prepare_kernel, name='prepare', out_shape=(jax.ShapeDtypeS...  21.9 us
    unnamed x51, local copies, waits for them, and re-layouts  18 us
    pallas_call x1, Pallas kernels, gather(): pl.pallas_call(gather_kernel, name='gather', out_shape=jax.ShapeDtypeStru...  8.61 us
    pallas_call x1, Pallas kernels, middle(): pl.pallas_call(middle_kernel, name='middle', out_shape=(jax.ShapeDtypeStr...  8.56 us
    pallas_call x1, Pallas kernels, finish_first(): pl.pallas_call(finish_first_kernel, name='finish_first', out_shape=(jax.S...  7.94 us
  transfers between devices with their start and end apart: 8, of which 5 were waited for; matrix products, arithmetic and copies ran while one was open for 1% of the time, Pallas kernels for 15%

profile of v1, /device:TPU:2, one launch (start us, length us, event | category | flops | bytes accessed | tf_op | source)
XLA Modules:
  0.0 304.1 jit_solution(5562919251217880031)
XLA Ops:
  0.6 1.2 copy-done.9
  1.9 0.7 copy-done.16
  2.5 0.7 copy-done.18
  3.2 1.0 pack.1
  4.2 2.0 copy-done.2
  6.3 16.1 %all-to-all-start = ((bf16[128,136,128]{2,1,0:T(8,128)(2,1)}), bf16[128,136,128]{2,1,0:T(8,128)(2,1)}, u32[]{:S(2)}, u32[]{:S(2)}) async-start(bf16[128,136,128]{2,1,0:T(8,128)(2,1)} %copy-done.2), calls=%async_computation | async-start | bytes 8912896 | tf_op jit(solution)/shard_map/all_to_all | solution.py:457
  25.6 21.9 %prepare.1 = (f32[4096,128]{1,0:T(8,128)S(1)}, bf16[160,128,128]{2,1,0:T(8,128)(2,1)S(1)}, bf16[96,128,256]{2,1,0:T(8,128)(2,1)}) custom-call(s32[160]{0:T(256)S(1)} %copy-done.15, s32[1]{0:T(128)} %copy.26.count, s32[160]{0:T(256)S(1)} %get-tuple-element.24.order, s32[96]{0:T(128)S(1)} %get-tuple-element.28.first, s32[96]{0:T(128)S(1)} %get-tuple-element.31.second, ...), custom_call_target="tpu_custom_call" | custom-call | flops 60000002048 | bytes 40000000 | tf_op jit(solution)/shard_map/prepare/pallas_call | solution.py:119
  47.6 2.4 copy-done
  50.0 1.3 copy-done.5
  51.3 72.2 %all-to-all-done.incoming = bf16[128,136,128]{2,1,0:T(8,128)(2,1)} async-done(((bf16[128,136,128]{2,1,0:T(8,128)(2,1)}), bf16[128,136,128]{2,1,0:T(8,128)(2,1)}, u32[]{:S(2)}, u32[]{:S(2)}) %all-to-all-start) | async-done | bytes 4456480 | tf_op jit(solution)/shard_map/all_to_all | solution.py:457
  123.4 1.6 copy-done.6
  125.0 8.6 %gather.1.agg = bf16[4096,128]{1,0:T(8,128)(2,1)S(1)} custom-call(s32[96]{0:T(128)S(1)} %get-tuple-element.29.row, s32[96]{0:T(128)S(1)} %get-tuple-element.26.owner_a, s32[96]{0:T(128)S(1)} %get-tuple-element.25.owner_b, s32[1]{0:T(128)} %bitcast.1.n_duos, bf16[96,128,256]{2,1,0:T(8,128)(2,1)} %get-tuple-element.13.pairs, ...), custom_call_target="tpu_custom_call" | custom-call | tf_op jit(solution)/shard_map/gather/pallas_call | solution.py:196
  133.9 0.9 fusion.19
  134.9 1.5 collective-permute-done.1.agg_peer
  136.4 8.6 %middle.1 = (bf16[4096,128]{1,0:T(8,128)(2,1)}, bf16[4096,256]{1,0:T(8,128)(2,1)S(1)}, bf16[4096,128]{1,0:T(8,128)(2,1)S(1)}, f32[1024,128]{1,0:T(8,128)S(1)}) custom-call(bf16[4096,128]{1,0:T(8,128)(2,1)S(1)} %copy-done.11, bf16[4096,128]{1,0:T(8,128)(2,1)} %collective-permute-done.feat_peer, bf16[4096,128]{1,0:T(8,128)(2,1)S(1)} %gather.1.agg, ...), custom_call_target="tpu_custom_call" | custom-call | tf_op jit(solution)/shard_map/middle/pallas_call | solution.py:264
  145.0 1.3 copy-done.12
  146.3 2.6 back_0.1
  148.9 1.4 copy-done.3
  150.3 13.0 %all-to-all-start.1 = ((bf16[128,72,128]{2,1,0:T(8,128)(2,1)}), bf16[128,72,128]{2,1,0:T(8,128)(2,1)S(1)}, u32[]{:S(2)}, u32[]{:S(2)}) async-start(bf16[128,72,128]{2,1,0:T(8,128)(2,1)} %copy-done.3), calls=%async_computation.1 | async-start | bytes 4718592 | tf_op jit(solution)/shard_map/all_to_all | solution.py:457
  163.3 2.5 copy-done.1
  165.8 2.5 back_1.1
  168.3 1.3 copy-done.8
  169.6 51.8 %all-to-all-done.1.returned = bf16[128,72,128]{2,1,0:T(8,128)(2,1)S(1)} async-done(((bf16[128,72,128]{2,1,0:T(8,128)(2,1)}), bf16[128,72,128]{2,1,0:T(8,128)(2,1)S(1)}, u32[]{:S(2)}, u32[]{:S(2)}) %all-to-all-start.1) | async-done | bytes 2359328 | tf_op jit(solution)/shard_map/all_to_all | solution.py:457
  221.4 8.4 %all-to-all-start.3 = ((bf16[128,64,128]{2,1,0:T(8,128)(2,1)}), bf16[128,64,128]{2,1,0:T(8,128)(2,1)}, u32[]{:S(2)}, u32[]{:S(2)}) async-start(bf16[128,64,128]{2,1,0:T(8,128)(2,1)} %copy-done.8), calls=%async_computation.3 | async-start | bytes 4194304 | tf_op jit(solution)/shard_map/all_to_all | solution.py:457
  229.9 1.6 copy-done.13
  231.5 7.9 %finish_first.1 = (f32[32,128,128]{2,1,0:T(8,128)}, f32[8,128]{1,0:T(8,128)S(1)}) custom-call(s32[128]{0:T(128)S(1)} %copy-done.17, s32[2]{0:T(128)S(1)} %copy-done.19, bf16[4096,256]{1,0:T(8,128)(2,1)S(1)} %copy-done.13, bf16[128,256]{1,0:T(8,128)(2,1)S(1)} %get-tuple-element.42.own_w, bf16[128,72,128]{2,1,0:T(8,128)(2,1)S(1)} %all-to-all-done.1.returned), custom_call_target="tpu_custom_call" | custom-call | tf_op jit(solution)/shard_map/finish_first/pallas_call | solution.py:374
  239.4 42.4 %all-to-all-done.3.returned = bf16[128,64,128]{2,1,0:T(8,128)(2,1)} async-done(((bf16[128,64,128]{2,1,0:T(8,128)(2,1)}), bf16[128,64,128]{2,1,0:T(8,128)(2,1)}, u32[]{:S(2)}, u32[]{:S(2)}) %all-to-all-start.3) | async-done | bytes 2097184 | tf_op jit(solution)/shard_map/all_to_all | solution.py:457
  281.9 0.7 broadcast_in_dim.127
  282.6 7.1 %all-to-all-start.2 = ((f32[128,4,128]{2,1,0:T(4,128)}), f32[128,4,128]{2,1,0:T(4,128)S(1)}, u32[]{:S(2)}, u32[]{:S(2)}) async-start(f32[128,4,128]{2,1,0:T(4,128)} %broadcast_in_dim.127), calls=%async_computation.2 | async-start | bytes 524288 | tf_op jit(solution)/shard_map/all_to_all | solution.py:457
  289.7 4.0 %finish_second.1 = f32[32,128,128]{2,1,0:T(8,128)} custom-call(s32[128]{0:T(128)S(1)} %copy-done.17, bf16[128,64,128]{2,1,0:T(8,128)(2,1)} %all-to-all-done.3.returned, f32[32,128,128]{2,1,0:T(8,128)} %get-tuple-element.21.before), custom_call_target="tpu_custom_call", output_to_operand_aliasing={{}: (2, {})} | custom-call | tf_op jit(solution)/shard_map/finish_second/pallas_call | solution.py:396
  293.7 9.7 %all-to-all-done.2 = f32[128,4,128]{2,1,0:T(4,128)S(1)} async-done(((f32[128,4,128]{2,1,0:T(4,128)}), f32[128,4,128]{2,1,0:T(4,128)S(1)}, u32[]{:S(2)}, u32[]{:S(2)}) %all-to-all-start.2) | async-done | bytes 262176 | tf_op jit(solution)/shard_map/all_to_all | solution.py:457
  303.4 0.7 maximum_select_fusion.1
  (73 shorter events, 2.9 us)
Async XLA Ops:
  0.6 1.2 copy-start.9
  1.9 0.7 copy-start.16
  4.2 2.0 copy-start.2
  6.2 16.2 %copy-start.10 = (bf16[4096,128]{1,0:T(8,128)(2,1)S(1)}, bf16[4096,128]{1,0:T(8,128)(2,1)}, u32[]{:S(2)}) copy-start(bf16[4096,128]{1,0:T(8,128)(2,1)} %feat.3) | copy-start | bytes 3145732
  6.2 16.3 %copy-start.20 = (bf16[128,256]{1,0:T(8,128)(2,1)S(1)}, bf16[128,256]{1,0:T(8,128)(2,1)}, u32[]{:S(2)}) copy-start(bf16[128,256]{1,0:T(8,128)(2,1)} %param.12) | copy-start | bytes 196612
  6.2 16.3 %copy-start.21 = (bf16[128,256]{1,0:T(8,128)(2,1)S(1)}, bf16[128,256]{1,0:T(8,128)(2,1)}, u32[]{:S(2)}) copy-start(bf16[128,256]{1,0:T(8,128)(2,1)} %param.13) | copy-start | bytes 196612
  6.2 17.7 %copy-start.15 = (s32[160]{0:T(256)S(1)}, s32[160]{0:T(256)}, u32[]{:S(2)}) copy-start(s32[160]{0:T(256)} %row.1) | copy-start | bytes 1924
  6.2 18.6 %copy-start.22 = (s32[160]{0:T(256)S(1)}, s32[160]{0:T(256)}, u32[]{:S(2)}) copy-start(s32[160]{0:T(256)} %param.16) | copy-start | bytes 1924
  6.3 19.4 %copy-start.4 = (bf16[4096,256]{1,0:T(8,128)(2,1)S(1)}, bf16[4096,256]{1,0:T(8,128)(2,1)}, u32[]{:S(2)}) copy-start(bf16[4096,256]{1,0:T(8,128)(2,1)} %panel.5) | copy-start | bytes 6291460
  6.3 117.2 %all-to-all-start = ((bf16[128,136,128]{2,1,0:T(8,128)(2,1)}), bf16[128,136,128]{2,1,0:T(8,128)(2,1)}, u32[]{:S(2)}, u32[]{:S(2)}) async-start(bf16[128,136,128]{2,1,0:T(8,128)(2,1)} %copy-done.2), calls=%async_computation | async-start | bytes 8912896 | tf_op jit(solution)/shard_map/all_to_all | solution.py:457
  22.4 112.5 %collective-permute-start = (bf16[4096,128]{1,0:T(8,128)(2,1)S(1)}, bf16[4096,128]{1,0:T(8,128)(2,1)}, u32[]{:S(2)}, u32[]{:S(2)}) collective-permute-start(bf16[4096,128]{1,0:T(8,128)(2,1)S(1)} %copy-done.10), channel_id=1, source_target_pairs={{0,1},{1,0},{2,3},{3,2},{4,5},{5,4},{6,7},{7,6},{8,9},{9,8},{10,11... | collective-permute-start | bytes 3145736 | tf_op jit(solution)/shard_map/ppermute | solution.py:461
  22.6 111.3 %collective-permute-start.3 = (bf16[256,256]{1,0:T(8,128)(2,1)S(1)}, bf16[256,256]{1,0:T(8,128)(2,1)}, u32[]{:S(2)}, u32[]{:S(2)}) collective-permute-start(bf16[256,256]{1,0:T(8,128)(2,1)S(1)} %maximum_select_fusion), channel_id=1, source_target_pairs={{0,1},{1,0},{2,3},{3,2},{4,5},{5,4},{6,7},{7,6},{8,9},{9,8},{10,11... | collective-permute-start | bytes 393224 | tf_op jit(solution)/shard_map/ppermute | solution.py:461
  23.2 111.7 %collective-permute-start.2 = (bf16[4096,128]{1,0:T(8,128)(2,1)}, bf16[4096,128]{1,0:T(8,128)(2,1)}, u32[]{:S(2)}, u32[]{:S(2)}) collective-permute-start(bf16[4096,128]{1,0:T(8,128)(2,1)} %cot.1), channel_id=1, source_target_pairs={{0,1},{1,0},{2,3},{3,2},{4,5},{5,4},{6,7},{7,6},{8,9},{9,8},{10,11... | collective-permute-start | bytes 3145736 | tf_op jit(solution)/shard_map/ppermute | solution.py:461
  47.6 2.4 copy-start
  50.0 1.3 copy-start.5
  123.4 1.6 copy-start.6
  125.0 11.4 %copy-start.7 = (f32[4096,128]{1,0:T(8,128)S(1)}, f32[4096,128]{1,0:T(8,128)}, u32[]{:S(2)}) copy-start(f32[4096,128]{1,0:T(8,128)} %copy-done.5) | copy-start | bytes 6291460
  125.0 11.4 %copy-start.11 = (bf16[4096,128]{1,0:T(8,128)(2,1)S(1)}, bf16[4096,128]{1,0:T(8,128)(2,1)}, u32[]{:S(2)}) copy-start(bf16[4096,128]{1,0:T(8,128)(2,1)} %feat.3) | copy-start | bytes 3145732
  125.0 11.4 %copy-start.14 = (bf16[4096,128]{1,0:T(8,128)(2,1)S(1)}, bf16[4096,128]{1,0:T(8,128)(2,1)}, u32[]{:S(2)}) copy-start(bf16[4096,128]{1,0:T(8,128)(2,1)} %cot.1) | copy-start | bytes 3145732
  133.7 2.7 collective-permute-start.1
  134.9 11.4 %slice-start = ((s8[5242880]{0:T(1024)(128)(4,1)}), s8[4194304]{0:T(1024)(128)(4,1)S(1)}, s32[]{:S(2)}) async-start(s8[5242880]{0:T(1024)(128)(4,1)} %bitcast.17), calls=%async_computation.4 | async-start | bytes 8388608
  134.9 11.4 %slice-start.1 = ((s8[5242880]{0:T(1024)(128)(4,1)}), s8[1048576]{0:T(1024)(128)(4,1)S(1)}, s32[]{:S(2)}) async-start(s8[5242880]{0:T(1024)(128)(4,1)} %bitcast.17), calls=%async_computation.5 | async-start | bytes 2097152
  145.0 1.3 copy-start.12
  148.9 1.4 copy-start.3
  150.3 71.1 %all-to-all-start.1 = ((bf16[128,72,128]{2,1,0:T(8,128)(2,1)}), bf16[128,72,128]{2,1,0:T(8,128)(2,1)S(1)}, u32[]{:S(2)}, u32[]{:S(2)}) async-start(bf16[128,72,128]{2,1,0:T(8,128)(2,1)} %copy-done.3), calls=%async_computation.1 | async-start | bytes 4718592 | tf_op jit(solution)/shard_map/all_to_all | solution.py:457
  163.3 2.5 copy-start.1
  168.3 1.3 copy-start.8
  169.6 60.3 %copy-start.17 = (s32[128]{0:T(128)S(1)}, s32[128]{0:T(128)}, u32[]{:S(2)}) copy-start(s32[128]{0:T(128)} %send.5) | copy-start | bytes 1540
  169.6 60.3 %copy-start.19 = (s32[2]{0:T(128)S(1)}, s32[2]{0:T(128)}, u32[]{:S(2)}) copy-start(s32[2]{0:T(128)} %hubs.3) | copy-start | bytes 28
  221.4 60.4 %all-to-all-start.3 = ((bf16[128,64,128]{2,1,0:T(8,128)(2,1)}), bf16[128,64,128]{2,1,0:T(8,128)(2,1)}, u32[]{:S(2)}, u32[]{:S(2)}) async-start(bf16[128,64,128]{2,1,0:T(8,128)(2,1)} %copy-done.8), calls=%async_computation.3 | async-start | bytes 4194304 | tf_op jit(solution)/shard_map/all_to_all | solution.py:457
  229.9 1.6 copy-start.13
  282.6 20.8 %all-to-all-start.2 = ((f32[128,4,128]{2,1,0:T(4,128)}), f32[128,4,128]{2,1,0:T(4,128)S(1)}, u32[]{:S(2)}, u32[]{:S(2)}) async-start(f32[128,4,128]{2,1,0:T(4,128)} %broadcast_in_dim.127), calls=%async_computation.2 | async-start | bytes 524288 | tf_op jit(solution)/shard_map/all_to_all | solution.py:457
  (1 other events, 0.7 us)

commit v2 on v1

--- a/solution.py
+++ b/solution.py
@@ -65,7 +65,7 @@
             out_specs=pl.BlockSpec((per_step, edge + 8, width), lambda g, *_: (g, 0, 0)),
             scratch_shapes=[pltpu.VMEM((8, width), F32)],
         ),
-        compiler_params=params(16, 1),
+        compiler_params=params(58, 1),
     )(send_tile, hub_rows, features)
 
 
@@ -187,7 +187,7 @@
 def gather(row, owner_a, owner_b, n_duos, pairs, incoming, panel, inv):
     duos, edge, _ = pairs.shape
     rows, hubs = panel.shape
-    per_step = 8
+    per_step = 16
     whole = lambda g, *_: (0, 0)
 
     def block(g, row, owner_a, owner_b, n_duos):
@@ -215,14 +215,12 @@
 
 def middle_kernel(
     feat, feat_peer, agg, agg_peer, cot, cot_peer, inv, panel, own_w, nbr_w,
-    layer, slopes_out, agg_slopes_out, extra, hub_acc, grad_acc,
+    layer, slopes_out, agg_slopes_out, extra, hub_acc,
 ):
     step, steps = pl.program_id(0), pl.num_programs(0)
     half = feat.shape[1]
-    x = feat[...]
-    a = agg[...]
-    preact = dot(jnp.concatenate([x, feat_peer[...]], axis=1), own_w[...], NN) + dot(
-        jnp.concatenate([a, agg_peer[...]], axis=1), nbr_w[...], NN
+    preact = dot(jnp.concatenate([feat[...], feat_peer[...]], axis=1), own_w[...], NN) + dot(
+        jnp.concatenate([agg[...], agg_peer[...]], axis=1), nbr_w[...], NN
     )
     layer[...] = jnp.maximum(preact[:, :half], 0.0).astype(BF16)
     cotangent = jnp.concatenate([cot[...], cot_peer[...]], axis=1).astype(F32)
@@ -231,28 +229,21 @@
     agg_slopes = (dot(slopes, nbr_w[:half, :], NT) * inv[...]).astype(BF16)
     agg_slopes_out[...] = agg_slopes
     hub = dot(panel[...], agg_slopes, TN)
-    grads = dot(jnp.concatenate([x, a], axis=1), slopes, TN)
 
     @pl.when(step == 0)
     def _():
         hub_acc[...] = hub
-        grad_acc[...] = grads
 
     @pl.when(step > 0)
     def _():
         hub_acc[...] += hub
-        grad_acc[...] += grads
 
     @pl.when(step == steps - 1)
     def _():
-        n = half
+        owners = hub_acc.shape[0] // 2
         extra[...] = jnp.zeros_like(extra)
         for j in range(2):
-            extra[pl.ds(j, n, stride=8), :] = hub_acc[pl.ds(j, n, stride=2), :]
-            for c in range(2):
-                extra[pl.ds(2 + 2 * j + c, n, stride=8), :] = grad_acc[
-                    j * n : (j + 1) * n, c * n : (c + 1) * n
-                ]
+            extra[pl.ds(j, owners, stride=8), :] = hub_acc[pl.ds(j, owners, stride=2), :]
 
 
 def middle(feat, feat_peer, agg, agg_peer, cot, cot_peer, inv, panel, own_w, nbr_w):
@@ -268,32 +259,26 @@
             jax.ShapeDtypeStruct((rows, half), BF16),
             jax.ShapeDtypeStruct((rows, 2 * half), BF16),
             jax.ShapeDtypeStruct((rows, half), BF16),
-            jax.ShapeDtypeStruct((8 * half, half), F32),
+            jax.ShapeDtypeStruct((4 * hubs, half), F32),
         ),
         grid=(rows // block,),
         in_specs=[by_row(half)] * 7
         + [by_row(hubs), whole(own_w.shape), whole(nbr_w.shape)],
-        out_specs=(by_row(half), by_row(2 * half), by_row(half), whole((8 * half, half))),
-        scratch_shapes=[
-            pltpu.VMEM((hubs, half), F32),
-            pltpu.VMEM((2 * half, 2 * half), F32),
-        ],
+        out_specs=(by_row(half), by_row(2 * half), by_row(half), whole((4 * hubs, half))),
+        scratch_shapes=[pltpu.VMEM((hubs, half), F32)],
         compiler_params=params(32, 1),
     )(feat, feat_peer, agg, agg_peer, cot, cot_peer, inv, panel, own_w, nbr_w)
 
 
-def back_kernel(order_row, order_owner, same, live, count, flipped, slopes, *rest):
-    extra = rest[0] if len(rest) == 3 else None
-    out, carry = rest[-2:]
+def back_kernel(order_row, order_owner, same, live, count, flipped, slopes, extra, out, carry):
     step = pl.program_id(0)
-    slots, part, edge = flipped.shape
+    slots, edge, _ = flipped.shape
 
     @pl.when(step == 0)
     def _():
-        out[:, :part, :] = jnp.zeros((out.shape[0], part, out.shape[2]), out.dtype)
+        out[:, :edge, :] = jnp.zeros((out.shape[0], edge, out.shape[2]), out.dtype)
+        out[:, edge:, :] = extra[...].astype(BF16)
         carry[...] = jnp.zeros_like(carry)
-        if extra is not None:
-            out[:, part:, :] = extra[...].astype(BF16)
 
     @pl.when(step * slots < count[0])
     def _():
@@ -305,107 +290,141 @@
         for i in range(slots):
             k = step * slots + i
             total = products[i] * live[k].astype(F32) + total * same[k].astype(F32)
-            out[order_owner[k], :part, :] = total.astype(BF16)
+            out[order_owner[k], :edge, :] = total.astype(BF16)
         carry[...] = total
 
 
-def back(order_row, order_owner, same, live, count, flipped, slopes, extra, side):
+def back(order_row, order_owner, same, live, count, flipped, slopes, extra):
     slots, edge, _ = flipped.shape
     rows, half = slopes.shape
-    part = edge // 2
-    parts = 128 if extra is None else extra.shape[0]
+    parts = extra.shape[0]
     per_step = 16
 
     def block(g, order_row, order_owner, same, live, count):
-        return (jnp.minimum(g, (count[0] - 1) // per_step), side, 0)
-
-    height = part + (8 if extra is not None else 0)
-    in_specs = [
-        pl.BlockSpec((per_step, part, edge), block),
-        pl.BlockSpec((rows, half), lambda g, *_: (0, 0)),
-    ]
-    args = [flipped, slopes]
-    if extra is not None:
-        in_specs.append(pl.BlockSpec(extra.shape, lambda g, *_: (0, 0, 0)))
-        args.append(extra)
+        return (jnp.minimum(g, (count[0] - 1) // per_step), 0, 0)
+
     return pl.pallas_call(
         back_kernel,
-        name=f"back_{side}",
-        out_shape=jax.ShapeDtypeStruct((parts, height, half), BF16),
+        name="back",
+        out_shape=jax.ShapeDtypeStruct((parts, edge + 8, half), BF16),
         grid_spec=pltpu.PrefetchScalarGridSpec(
             num_scalar_prefetch=5,
             grid=(slots // per_step,),
-            in_specs=in_specs,
-            out_specs=pl.BlockSpec((parts, height, half), lambda g, *_: (0, 0, 0)),
-            scratch_shapes=[pltpu.VMEM((part, half), F32)],
-        ),
-        compiler_params=params(32, 1),
-    )(order_row, order_owner, same, live, count, *args)
-
-
-def finish_first_kernel(send, hubs, slopes, own_w, returned, out, share):
-    parts, height, half = returned.shape
-    tiles, edge = out.shape[0], out.shape[1]
-    part = height - 8
-
-    @pl.loop(0, tiles)
-    def _(t):
-        at = pl.ds(pl.multiple_of(t * edge, edge), edge)
-        out[t] = dot(slopes[at, :], own_w[...], NT)
-
-    total = jnp.zeros((8, half), F32)
-    for p in range(parts):
-        out[send[p], :part, :] += returned[p, :part, :].astype(F32)
-        total = total + returned[p, part:, :].astype(F32)
-    share[...] = total
-    for j in range(2):
-        row = hubs[j]
-        tile, inside = row // edge, row % edge
-        base = pl.multiple_of((inside // 8) * 8, 8)
-        here = lax.broadcasted_iota(jnp.int32, (8, half), 0) == inside - base
-        out[tile, pl.ds(base, 8), :] += jnp.where(here, total[j : j + 1, :], 0.0)
-
-
-def finish_first(send_tile, hub_rows, slopes, own_w, returned, edge):
-    rows = slopes.shape[0]
-    half = returned.shape[2]
-    smem = pl.BlockSpec(memory_space=pltpu.SMEM)
-    vmem = pl.BlockSpec(memory_space=pltpu.VMEM)
+            in_specs=[
+                pl.BlockSpec((per_step, edge, edge), block),
+                pl.BlockSpec((rows, half), lambda g, *_: (0, 0)),
+                pl.BlockSpec(extra.shape, lambda g, *_: (0, 0, 0)),
+            ],
+            out_specs=pl.BlockSpec((parts, edge + 8, half), lambda g, *_: (0, 0, 0)),
+            scratch_shapes=[pltpu.VMEM((edge, half), F32)],
+        ),
+        compiler_params=params(58, 1),
+    )(order_row, order_owner, same, live, count, flipped, slopes, extra)
+
+
+def side_kernel(place, feat, agg, slopes, own_w, grads, direct, acc):
+    step, steps = pl.program_id(0), pl.num_programs(0)
+    half = feat.shape[1]
+    s = slopes[...]
+    direct[...] = dot(s, own_w[...], NT)
+    part = dot(jnp.concatenate([feat[...], agg[...]], axis=1), s, TN)
+
+    @pl.when(step == 0)
+    def _():
+        acc[...] = part
+
+    @pl.when(step > 0)
+    def _():
+        acc[...] += part
+
+    @pl.when(step == steps - 1)
+    def _():
+        n = half // 4
+        for c in range(4):
+            for r in range(4):
+                grads[(c + 4 - place[0]) % 4, (r + 4 - place[1]) % 4] = acc[
+                    (c // 2) * half + r * n : (c // 2) * half + (r + 1) * n,
+                    (c % 2) * half : (c % 2 + 1) * half,
+                ]
+
+
+def side(place, feat, agg, slopes, own_w):
+    rows, half = feat.shape
+    block = 512
+    by_row = lambda width: pl.BlockSpec((block, width), lambda g, *_: (g, 0))
     return pl.pallas_call(
-        finish_first_kernel,
-        name="finish_first",
+        side_kernel,
+        name="side",
         out_shape=(
-            jax.ShapeDtypeStruct((rows // edge, edge, half), F32),
-            jax.ShapeDtypeStruct((8, half), F32),
-        ),
-        in_specs=[smem, smem, vmem, vmem, vmem],
-        out_specs=(vmem, vmem),
-        compiler_params=pltpu.CompilerParams(vmem_limit_bytes=24 * MIB),
-    )(send_tile, hub_rows, slopes, own_w, returned)
-
-
-def finish_second_kernel(send, returned, before, out):
-    out[...] = before[...]
-    for p in range(returned.shape[0]):
-        out[send[p]] += returned[p].astype(F32)
-
-
-def finish_second(send_tile, returned, before):
-    tiles, edge, half = before.shape
-    spec = pl.BlockSpec((tiles, edge // 2, half), lambda g, *_: (0, 1, 0))
-    return pl.pallas_call(
-        finish_second_kernel,
-        name="finish_second",
-        out_shape=jax.ShapeDtypeStruct(before.shape, F32),
+            jax.ShapeDtypeStruct((4, 4, half // 4, half), F32),
+            jax.ShapeDtypeStruct((rows, half), F32),
+        ),
         grid_spec=pltpu.PrefetchScalarGridSpec(
             num_scalar_prefetch=1,
-            grid=(1,),
-            in_specs=[pl.BlockSpec(returned.shape, lambda g, *_: (0, 0, 0)), spec],
-            out_specs=spec,
-        ),
-        input_output_aliases={2: 0},
+            grid=(rows // block,),
+            in_specs=[
+                by_row(half),
+                by_row(half),
+                by_row(2 * half),
+                pl.BlockSpec(own_w.shape, lambda g, *_: (0, 0)),
+            ],
+            out_specs=(
+                pl.BlockSpec((4, 4, half // 4, half), lambda g, *_: (0, 0, 0, 0)),
+                by_row(half),
+            ),
+            scratch_shapes=[pltpu.VMEM((2 * half, 2 * half), F32)],
+        ),
         compiler_params=params(24, 1),
-    )(send_tile, returned, before)
+    )(place, feat, agg, slopes, own_w)
+
+
+def finish_kernel(send, hubs, returned, direct, out, total):
+    step, steps = pl.program_id(0), pl.num_programs(0)
+    parts, height, half = returned.shape
+    edge = out.shape[1]
+
+    @pl.when(step == 0)
+    def _():
+        out[...] = direct[...]
+        total[...] = jnp.zeros_like(total)
+
+    share = total[...]
+    for i in range(parts):
+        out[send[step * parts + i]] += returned[i, :edge, :].astype(F32)
+        share = share + returned[i, edge:, :].astype(F32)
+    total[...] = share
+
+    @pl.when(step == steps - 1)
+    def _():
+        for j in range(2):
+            row = hubs[j]
+            tile, inside = row // edge, row % edge
+            base = pl.multiple_of((inside // 8) * 8, 8)
+            here = lax.broadcasted_iota(jnp.int32, (8, half), 0) == inside - base
+            out[tile, pl.ds(base, 8), :] += jnp.where(here, total[j : j + 1, :], 0.0)
+
+
+def finish(send_tile, hub_rows, returned, direct):
+    tiles, edge, half = direct.shape
+    parts, height, _ = returned.shape
+    per_step = 16
+    whole = pl.BlockSpec((tiles, edge, half), lambda g, *_: (0, 0, 0))
+    return pl.pallas_call(
+        finish_kernel,
+        name="finish",
+        out_shape=jax.ShapeDtypeStruct(direct.shape, F32),
+        grid_spec=pltpu.PrefetchScalarGridSpec(
+            num_scalar_prefetch=2,
+            grid=(parts // per_step,),
+            in_specs=[
+                pl.BlockSpec((per_step, height, half), lambda g, *_: (g, 0, 0)),
+                whole,
+            ],
+            out_specs=whole,
+            scratch_shapes=[pltpu.VMEM((8, half), F32)],
+        ),
+        compiler_params=params(24, 1),
+    )(send_tile, hub_rows, returned, direct)
 
 
 def plan(tile_row, tile_owner, tile_count, tiles, parts):
@@ -459,6 +478,31 @@
 
 def swap(block):
     return lax.ppermute(block, "feat", [(0, 1), (1, 0)])
+
+
+def move(block, axis, amount):
+    def target(d):
+        z, x, y = d // 16, (d // 4) % 4, d % 4
+        if axis == "y":
+            y = (y + amount) % 4
+        elif axis == "x":
+            x = (x + amount) % 4
+        else:
+            z = z ^ amount
+        return (z * 4 + x) * 4 + y
+
+    return lax.ppermute(block, "dom", [(d, target(d)) for d in range(lax.axis_size("dom"))])
+
+
+def sum_over_dom(blocks):
+    for axis in ("y", "x"):
+        moved = [move(blocks[i], axis, i) for i in (1, 2, 3)]
+        blocks = (blocks[0] + moved[0]) + (moved[1] + moved[2])
+    for bit in (1, 2, 4):
+        blocks = blocks + move(blocks, "z", bit)
+    for axis in ("x", "y"):
+        blocks = jnp.stack([blocks] + [move(blocks, axis, i) for i in (1, 2, 3)])
+    return blocks
 
 
 def shards(
@@ -497,6 +541,9 @@
     by_owner, by_row, duos = plan(tile_row, tile_owner, tile_count, tiles_dev, dom_size)
     order, order_row, order_owner, same, live = by_owner
     first, second, kinds, pair_row, owner_a, owner_b, n_duos = by_row
+    tile_count, own_w, nbr_w, feat_peer, cot_peer = lax.optimization_barrier(
+        (tile_count, own_w, nbr_w, feat_peer, cot_peer)
+    )
     inv, flipped, pairs = prepare(
         tile_row, tile_count, order, first, second, kinds, tile_values, hub_panel, duos
     )
@@ -506,20 +553,29 @@
     layer_out, slopes, agg_slopes, extra = middle(
         features, feat_peer, aggregate, agg_peer, cotangent, cot_peer, inv, hub_panel, own_w, nbr_w
     )
-    extra = extra.reshape(dom_size, 8, half)
-    back_args = (order_row, order_owner, same, live, tile_count, flipped, agg_slopes)
-    returned_a = exchange(back(*back_args, extra, 0))
-    returned_b = exchange(back(*back_args, None, 1))
-
-    partial_grad, share = finish_first(
-        send_tile, hub_rows, slopes, own_w[:half], returned_a, tile_edge
-    )
-    grads = exchange(jnp.broadcast_to(share[None, 2:6], (dom_size, 4, half)))
-    input_grad = finish_second(send_tile, returned_b, partial_grad).reshape(rows_dev, half)
-
+    terms = back(
+        order_row, order_owner, same, live, tile_count, flipped, agg_slopes,
+        extra.reshape(dom_size, 8, half),
+    )
+    returned = exchange(terms)
+
+    _, slopes = lax.optimization_barrier((terms, slopes))
+    dom = lax.axis_index("dom")
+    place_y, place_x = dom % 4, (dom // 4) % 4
+    grads, direct = side(
+        jnp.stack([place_y, place_x]).astype(jnp.int32), features, aggregate, slopes, own_w[:half]
+    )
+    grads = sum_over_dom(grads)
+    c = jnp.arange(4) ^ core
+    r = jnp.arange(4)
+    index = (((place_y - c) % 4)[:, None] * 4 + ((place_x - r) % 4)[None, :]).reshape(16)
+    grads = grads.reshape(16, half // 4, half)[index].reshape(4, half, half)
     grads = grads * (1.0 / math.sqrt(rows_dev * dom_size))
-    sides = [jnp.concatenate([grads[:, 2 * j], grads[:, 2 * j + 1]], axis=1) for j in range(2)]
-    self_grad, neighbor_grad = (own_first(side) for side in sides)
+    self_grad = jnp.concatenate([grads[0], grads[1]], axis=1)
+    neighbor_grad = jnp.concatenate([grads[2], grads[3]], axis=1)
+    direct = direct.reshape(tiles_dev, tile_edge, half)
+    direct, self_grad, neighbor_grad = lax.optimization_barrier((direct, self_grad, neighbor_grad))
+    input_grad = finish(send_tile, hub_rows, returned, direct).reshape(rows_dev, half)
     return (layer_out, self_grad, neighbor_grad, input_grad)
 
 

time: 306 us -> 307 us (level)
  waiting for transfers between devices: 178 us -> 163 us
  starting transfers between devices: 45.4 us -> 56 us
  Pallas kernels: 57.2 us -> 63.4 us
  local copies, waits for them, and re-layouts: 19.7 us -> 15.3 us
    all_to_all x4 -> x2, waiting for transfers between devices: 176 us -> 70.3 us  [exchange(): return lax.all_to_all(block, 'dom', split_axis=0, concat_axis=0, tiled=True)]
    ppermute x0 -> x15, waiting for transfers between devices: none -> 90.8 us  [move(): lax.ppermute(block, 'dom', [(d, target(d)) for d in range(lax.axis_size('...]
    ppermute x0 -> x15, starting transfers between devices: none -> 26.8 us  [move(): lax.ppermute(block, 'dom', [(d, target(d)) for d in range(lax.axis_size('...]
    all_to_all x4 -> x2, starting transfers between devices: 44.6 us -> 28 us  [exchange(): return lax.all_to_all(block, 'dom', split_axis=0, concat_axis=0, tiled=True)]
    pallas_call x1, Pallas kernels: 1.03 us -> 5.55 us  [pack(): pl.pallas_call(pack_kernel, name='pack', out_shape=jax.ShapeDtypeStruct((...]
    unnamed x51 -> x45, local copies, waits for them, and re-layouts: 18 us -> 14.6 us
    pallas_call x4 -> x3, Pallas kernels: 17 us -> 18.6 us  [the longest x1 8.15 us: back(): pl.pallas_call(back_kernel, name='back', out_shape=jax.ShapeDtypeStruct((...]
  transfers between devices with their start and end apart: 8 -> 21, of which waited for: 5 -> 12; matrix products, arithmetic and copies ran while one was open for 1% -> 2% of each run, Pallas kernels for 15% -> 11%
where the time goes in v2:
time: 307 us; the launch traced here: 304 us
  waiting for transfers between devices  163 us (53%)
  Pallas kernels  63.4 us (21%)
  starting transfers between devices  56 us (18%)
  local copies, waits for them, and re-layouts  15.3 us (5%)
  other arithmetic  4.51 us (1%)
    ppermute x15, waiting for transfers between devices, move(): lax.ppermute(block, 'dom', [(d, target(d)) for d in range(lax.axis_size('...  90.8 us
    all_to_all x2, waiting for transfers between devices, exchange(): return lax.all_to_all(block, 'dom', split_axis=0, concat_axis=0, tiled=True)  70.3 us
    all_to_all x2, starting transfers between devices, exchange(): return lax.all_to_all(block, 'dom', split_axis=0, concat_axis=0, tiled=True)  28 us
    ppermute x15, starting transfers between devices, move(): lax.ppermute(block, 'dom', [(d, target(d)) for d in range(lax.axis_size('...  26.8 us
    pallas_call x1, Pallas kernels, prepare(): pl.pallas_call(prepare_kernel, name='prepare', out_shape=(jax.ShapeDtypeS...  22 us
    unnamed x45, local copies, waits for them, and re-layouts  14.6 us
    pallas_call x1, Pallas kernels, gather(): pl.pallas_call(gather_kernel, name='gather', out_shape=jax.ShapeDtypeStru...  8.66 us
    pallas_call x1, Pallas kernels, middle(): pl.pallas_call(middle_kernel, name='middle', out_shape=(jax.ShapeDtypeStr...  8.65 us
  transfers between devices with their start and end apart: 21, of which 12 were waited for; matrix products, arithmetic and copies ran while one was open for 2% of the time, Pallas kernels for 11%

profile of v2, /device:TPU:2, one launch (start us, length us, event | category | flops | bytes accessed | tf_op | source)
XLA Modules:
  0.0 303.5 jit_solution(7103776157400151756)
XLA Ops:
  0.6 5.5 %pack.1 = bf16[128,136,128]{2,1,0:T(8,128)(2,1)} custom-call(s32[128]{0:T(128)} %send.3, s32[2]{0:T(128)} %hubs.3, bf16[4096,128]{1,0:T(8,128)(2,1)} %feat.5), custom_call_target="tpu_custom_call" | custom-call | tf_op jit(solution)/shard_map/pack/pallas_call | solution.py:57
  6.2 16.0 %all-to-all-start = ((bf16[128,136,128]{2,1,0:T(8,128)(2,1)}), bf16[128,136,128]{2,1,0:T(8,128)(2,1)}, u32[]{:S(2)}, u32[]{:S(2)}) async-start(bf16[128,136,128]{2,1,0:T(8,128)(2,1)} %pack.1), calls=%async_computation | async-start | bytes 8912896 | tf_op jit(solution)/shard_map/all_to_all | solution.py:476
  25.7 1.6 copy-done.1
  27.3 22.0 %prepare.1 = (f32[4096,128]{1,0:T(8,128)S(1)}, bf16[160,128,128]{2,1,0:T(8,128)(2,1)S(1)}, bf16[96,128,256]{2,1,0:T(8,128)(2,1)}) custom-call(s32[160]{0:T(256)S(1)} %copy-done.15, s32[1]{0:T(128)} %copy.16.count, s32[160]{0:T(256)S(1)} %get-tuple-element.42.order, s32[96]{0:T(128)S(1)} %get-tuple-element.46.first, s32[96]{0:T(128)S(1)} %get-tuple-element.49.second, ...), custom_call_target="tpu_custom_call" | custom-call | flops 60000002048 | bytes 40000000 | tf_op jit(solution)/shard_map/prepare/pallas_call | solution.py:119
  49.3 1.3 copy-done.4
  50.6 2.4 copy-done.7
  53.0 70.3 %all-to-all-done.incoming = bf16[128,136,128]{2,1,0:T(8,128)(2,1)} async-done(((bf16[128,136,128]{2,1,0:T(8,128)(2,1)}), bf16[128,136,128]{2,1,0:T(8,128)(2,1)}, u32[]{:S(2)}, u32[]{:S(2)}) %all-to-all-start) | async-done | bytes 4456480 | tf_op jit(solution)/shard_map/all_to_all | solution.py:476
  123.3 1.6 copy-done.2
  124.8 1.6 copy-done.5
  126.4 8.7 %gather.7.agg = bf16[4096,128]{1,0:T(8,128)(2,1)S(1)} custom-call(s32[96]{0:T(128)S(1)} %get-tuple-element.47.row, s32[96]{0:T(128)S(1)} %get-tuple-element.44.owner_a, s32[96]{0:T(128)S(1)} %get-tuple-element.43.owner_b, s32[1]{0:T(128)} %bitcast.1.n_duos, bf16[96,128,256]{2,1,0:T(8,128)(2,1)} %get-tuple-element.24.pairs, ...), custom_call_target="tpu_custom_call" | custom-call | tf_op jit(solution)/shard_map/gather/pallas_call | solution.py:196
  136.6 1.5 collective-permute-done
  138.2 8.6 %middle.1 = (bf16[4096,128]{1,0:T(8,128)(2,1)}, bf16[4096,256]{1,0:T(8,128)(2,1)S(1)}, bf16[4096,128]{1,0:T(8,128)(2,1)S(1)}, f32[1024,128]{1,0:T(8,128)S(1)}) custom-call(bf16[4096,128]{1,0:T(8,128)(2,1)S(1)} %copy-done, bf16[4096,128]{1,0:T(8,128)(2,1)} %collective-permute-done.1.feat_peer, bf16[4096,128]{1,0:T(8,128)(2,1)S(1)} %gather.7.agg, ...), custom_call_target="tpu_custom_call" | custom-call | tf_op jit(solution)/shard_map/middle/pallas_call | solution.py:255
  149.9 8.2 %back.1 = bf16[128,136,128]{2,1,0:T(8,128)(2,1)} custom-call(s32[160]{0:T(256)} %get-tuple-element.41.order_row, s32[160]{0:T(256)} %copy-done.20, s32[160]{0:T(256)} %get-tuple-element.75.same, s32[160]{0:T(256)} %get-tuple-element.76.live, s32[1]{0:T(128)} %copy.16.count, bf16[160,128,128]{2,1,0:T(8,128)(2,1)} %copy-done.7, bf16[4096,128]{1,0:T(8,128)(2,1)} %copy-done.13, ...), custom_call_target="tpu_custom_call" | custom-call | tf_op jit(solution)/shard_map/back/pallas_call | solution.py:306
  158.1 12.0 %all-to-all-start.1 = ((bf16[128,136,128]{2,1,0:T(8,128)(2,1)}), bf16[128,136,128]{2,1,0:T(8,128)(2,1)}, u32[]{:S(2)}, u32[]{:S(2)}) async-start(bf16[128,136,128]{2,1,0:T(8,128)(2,1)} %back.1), calls=%async_computation.1 | async-start | bytes 8912896 | tf_op jit(solution)/shard_map/all_to_all | solution.py:476
  170.3 1.6 copy-done.11
  171.9 3.4 %side.1 = (f32[4,4,32,128]{3,2,1,0:T(8,128)S(1)}, f32[4096,128]{1,0:T(8,128)S(1)}) custom-call(s32[2]{0:T(128)S(1)} %pad_add_fusion.place, bf16[4096,128]{1,0:T(8,128)(2,1)S(1)} %copy-done, bf16[4096,128]{1,0:T(8,128)(2,1)S(1)} %gather.7.agg, bf16[4096,256]{1,0:T(8,128)(2,1)S(1)} %copy-done.11, bf16[128,256]{1,0:T(8,128)(2,1)S(1)} %slice.83.own_w), custom_call_target="tpu_custom_call" | custom-call | tf_op jit(solution)/shard_map/side/pallas_call | solution.py:355
  176.6 2.8 collective-permute-start.6
  181.1 4.9 %collective-permute-done.6 = f32[4,32,128]{2,1,0:T(8,128)S(1)} collective-permute-done((f32[4,32,128]{2,1,0:T(8,128)S(1)}, f32[4,32,128]{2,1,0:T(8,128)S(1)}, u32[]{:S(2)}, u32[]{:S(2)}) %collective-permute-start.6) | collective-permute-done | bytes 65568 | tf_op jit(solution)/shard_map/ppermute | solution.py:494
  186.1 2.6 collective-permute-done.4
  188.7 4.0 %collective-permute-start.9 = (f32[32,128]{1,0:T(8,128)S(1)}, f32[32,128]{1,0:T(8,128)S(1)}, u32[]{:S(2)}, u32[]{:S(2)}) collective-permute-start(f32[32,128]{1,0:T(8,128)S(1)} %get-tuple-element.70), channel_id=1, source_target_pairs={{0,24},{2,26},{4,28},{6,30},{8,0},{10,2},{12,4},{14,6},{16,8},{18,... | collective-permute-start | bytes 49160 | tf_op jit(solution)/shard_map/ppermute | solution.py:494
  192.7 1.6 collective-permute-start.7
  194.2 3.9 %collective-permute-done.8 = f32[32,128]{1,0:T(8,128)S(1)} collective-permute-done((f32[32,128]{1,0:T(8,128)S(1)}, f32[32,128]{1,0:T(8,128)S(1)}, u32[]{:S(2)}, u32[]{:S(2)}) %collective-permute-start.8) | collective-permute-done | bytes 16416 | tf_op jit(solution)/shard_map/ppermute | solution.py:494
  198.2 68.7 %collective-permute-done.10 = f32[32,128]{1,0:T(8,128)S(1)} collective-permute-done((f32[32,128]{1,0:T(8,128)S(1)}, f32[32,128]{1,0:T(8,128)S(1)}, u32[]{:S(2)}, u32[]{:S(2)}) %collective-permute-start.10) | collective-permute-done | bytes 16416 | tf_op jit(solution)/shard_map/ppermute | solution.py:494
  267.8 3.7 %collective-permute-done.11 = f32[32,128]{1,0:T(8,128)S(1)} collective-permute-done((f32[32,128]{1,0:T(8,128)S(1)}, f32[32,128]{1,0:T(8,128)S(1)}, u32[]{:S(2)}, u32[]{:S(2)}) %collective-permute-start.11) | collective-permute-done | bytes 16416 | tf_op jit(solution)/shard_map/ppermute | solution.py:494
  271.6 4.8 %collective-permute-start.12 = (f32[32,128]{1,0:T(8,128)S(1)}, f32[32,128]{1,0:T(8,128)S(1)}, u32[]{:S(2)}, u32[]{:S(2)}) collective-permute-start(f32[32,128]{1,0:T(8,128)S(1)} %add.148), channel_id=1, source_target_pairs={{0,128},{2,130},{4,132},{6,134},{8,136},{10,138},{12,140},{14,142}... | collective-permute-start | bytes 49160 | tf_op jit(solution)/shard_map/ppermute | solution.py:494
  276.6 2.7 collective-permute-done.12
  279.7 2.4 collective-permute-start.14
  282.1 1.8 collective-permute-start.13
  285.8 3.1 %collective-permute-start.17 = (f32[4,32,128]{2,1,0:T(8,128)S(1)}, f32[4,32,128]{2,1,0:T(8,128)S(1)}, u32[]{:S(2)}, u32[]{:S(2)}) collective-permute-start(f32[4,32,128]{2,1,0:T(8,128)S(1)} %get-tuple-element.69), channel_id=1, source_target_pairs={{0,4},{2,6},{4,0},{6,2},{8,12},{10,14},{12,8},{14,10},{16,20},{18,... | collective-permute-start | bytes 196616 | tf_op jit(solution)/shard_map/ppermute | solution.py:494
  289.5 2.7 collective-permute-start.18
  292.2 2.2 collective-permute-done.16
  296.4 7.1 %finish.1 = f32[32,128,128]{2,1,0:T(8,128)} custom-call(s32[128]{0:T(128)S(1)} %copy-done.16, s32[2]{0:T(128)S(1)} %copy-done.17, bf16[128,136,128]{2,1,0:T(8,128)(2,1)} %all-to-all-done.1.returned, f32[32,128,128]{2,1,0:T(8,128)S(1)} %bitcast.50), custom_call_target="tpu_custom_call" | custom-call | tf_op jit(solution)/shard_map/finish/pallas_call | solution.py:412
  (106 shorter events, 16.9 us)
Async XLA Ops:
  6.2 16.0 %copy-start = (bf16[4096,128]{1,0:T(8,128)(2,1)S(1)}, bf16[4096,128]{1,0:T(8,128)(2,1)}, u32[]{:S(2)}) copy-start(bf16[4096,128]{1,0:T(8,128)(2,1)} %feat.5) | copy-start | bytes 3145732
  6.2 16.1 %copy-start.12 = (bf16[4096,128]{1,0:T(8,128)(2,1)S(1)}, bf16[4096,128]{1,0:T(8,128)(2,1)}, u32[]{:S(2)}) copy-start(bf16[4096,128]{1,0:T(8,128)(2,1)} %cot.1) | copy-start | bytes 3145732
  6.2 17.3 %copy-start.15 = (s32[160]{0:T(256)S(1)}, s32[160]{0:T(256)}, u32[]{:S(2)}) copy-start(s32[160]{0:T(256)} %row.1) | copy-start | bytes 1924
  6.2 18.2 %copy-start.21 = (s32[160]{0:T(256)S(1)}, s32[160]{0:T(256)}, u32[]{:S(2)}) copy-start(s32[160]{0:T(256)} %param.16) | copy-start | bytes 1924
  6.2 19.5 %copy-start.18 = (bf16[128,256]{1,0:T(8,128)(2,1)S(1)}, bf16[128,256]{1,0:T(8,128)(2,1)}, u32[]{:S(2)}) copy-start(bf16[128,256]{1,0:T(8,128)(2,1)} %param.12) | copy-start | bytes 196612
  6.2 19.5 %copy-start.19 = (bf16[128,256]{1,0:T(8,128)(2,1)S(1)}, bf16[128,256]{1,0:T(8,128)(2,1)}, u32[]{:S(2)}) copy-start(bf16[128,256]{1,0:T(8,128)(2,1)} %param.13) | copy-start | bytes 196612
  6.2 117.0 %all-to-all-start = ((bf16[128,136,128]{2,1,0:T(8,128)(2,1)}), bf16[128,136,128]{2,1,0:T(8,128)(2,1)}, u32[]{:S(2)}, u32[]{:S(2)}) async-start(bf16[128,136,128]{2,1,0:T(8,128)(2,1)} %pack.1), calls=%async_computation | async-start | bytes 8912896 | tf_op jit(solution)/shard_map/all_to_all | solution.py:476
  22.2 115.9 %collective-permute-start.1 = (bf16[4096,128]{1,0:T(8,128)(2,1)S(1)}, bf16[4096,128]{1,0:T(8,128)(2,1)}, u32[]{:S(2)}, u32[]{:S(2)}) collective-permute-start(bf16[4096,128]{1,0:T(8,128)(2,1)S(1)} %copy-done), channel_id=1, source_target_pairs={{0,1},{1,0},{2,3},{3,2},{4,5},{5,4},{6,7},{7,6},{8,9},{9,8},{10,11... | collective-permute-start | bytes 3145736 | tf_op jit(solution)/shard_map/ppermute | solution.py:480
  22.3 115.8 %collective-permute-start.2 = (bf16[4096,128]{1,0:T(8,128)(2,1)S(1)}, bf16[4096,128]{1,0:T(8,128)(2,1)}, u32[]{:S(2)}, u32[]{:S(2)}) collective-permute-start(bf16[4096,128]{1,0:T(8,128)(2,1)S(1)} %copy-done.12), channel_id=1, source_target_pairs={{0,1},{1,0},{2,3},{3,2},{4,5},{5,4},{6,7},{7,6},{8,9},{9,8},{10,11... | collective-permute-start | bytes 3145736 | tf_op jit(solution)/shard_map/ppermute | solution.py:480
  25.4 110.4 %copy-start.20 = (s32[160]{0:T(256)}, s32[160]{0:T(256)S(1)}, u32[]{:S(2)}) copy-start(s32[160]{0:T(256)S(1)} %get-tuple-element.40.order_owner) | copy-start | bytes 1924
  126.4 11.7 %copy-start.6 = (f32[4096,128]{1,0:T(8,128)S(1)}, f32[4096,128]{1,0:T(8,128)}, u32[]{:S(2)}) copy-start(f32[4096,128]{1,0:T(8,128)} %copy-done.4) | copy-start | bytes 6291460
  135.1 3.0 collective-permute-start.3
  135.3 2.8 collective-permute-start
  158.1 138.3 %all-to-all-start.1 = ((bf16[128,136,128]{2,1,0:T(8,128)(2,1)}), bf16[128,136,128]{2,1,0:T(8,128)(2,1)}, u32[]{:S(2)}, u32[]{:S(2)}) async-start(bf16[128,136,128]{2,1,0:T(8,128)(2,1)} %back.1), calls=%async_computation.1 | async-start | bytes 8912896 | tf_op jit(solution)/shard_map/all_to_all | solution.py:476
  170.2 126.2 %copy-start.16 = (s32[128]{0:T(128)S(1)}, s32[128]{0:T(128)}, u32[]{:S(2)}) copy-start(s32[128]{0:T(128)} %send.3) | copy-start | bytes 1540
  170.2 126.2 %copy-start.17 = (s32[2]{0:T(128)S(1)}, s32[2]{0:T(128)}, u32[]{:S(2)}) copy-start(s32[2]{0:T(128)} %hubs.3) | copy-start | bytes 28
  176.6 119.8 %copy-start.9 = (f32[4096,128]{1,0:T(8,128)S(1)}, f32[4096,128]{1,0:T(8,128)}, u32[]{:S(2)}) copy-start(f32[4096,128]{1,0:T(8,128)} %copy-done.8) | copy-start | bytes 6291460
  176.6 9.3 %collective-permute-start.6 = (f32[4,32,128]{2,1,0:T(8,128)S(1)}, f32[4,32,128]{2,1,0:T(8,128)S(1)}, u32[]{:S(2)}, u32[]{:S(2)}) collective-permute-start(f32[4,32,128]{2,1,0:T(8,128)S(1)} %get-tuple-element.59), channel_id=1, source_target_pairs={{0,6},{2,0},{4,2},{6,4},{8,14},{10,8},{12,10},{14,12},{16,22},{18,... | collective-permute-start | bytes 196616 | tf_op jit(solution)/shard_map/ppermute | solution.py:494
  179.3 6.7 %collective-permute-start.5 = (f32[4,32,128]{2,1,0:T(8,128)S(1)}, f32[4,32,128]{2,1,0:T(8,128)S(1)}, u32[]{:S(2)}, u32[]{:S(2)}) collective-permute-start(f32[4,32,128]{2,1,0:T(8,128)S(1)} %get-tuple-element.60), channel_id=1, source_target_pairs={{0,4},{2,6},{4,0},{6,2},{8,12},{10,14},{12,8},{14,10},{16,20},{18,... | collective-permute-start | bytes 196616 | tf_op jit(solution)/shard_map/ppermute | solution.py:494
  180.2 8.4 %collective-permute-start.4 = (f32[4,32,128]{2,1,0:T(8,128)S(1)}, f32[4,32,128]{2,1,0:T(8,128)S(1)}, u32[]{:S(2)}, u32[]{:S(2)}) collective-permute-start(f32[4,32,128]{2,1,0:T(8,128)S(1)} %get-tuple-element.61), channel_id=1, source_target_pairs={{0,2},{2,4},{4,6},{6,0},{8,10},{10,12},{12,14},{14,8},{16,18},{18,... | collective-permute-start | bytes 196616 | tf_op jit(solution)/shard_map/ppermute | solution.py:494
  188.7 5.5 %collective-permute-start.9 = (f32[32,128]{1,0:T(8,128)S(1)}, f32[32,128]{1,0:T(8,128)S(1)}, u32[]{:S(2)}, u32[]{:S(2)}) collective-permute-start(f32[32,128]{1,0:T(8,128)S(1)} %get-tuple-element.70), channel_id=1, source_target_pairs={{0,24},{2,26},{4,28},{6,30},{8,0},{10,2},{12,4},{14,6},{16,8},{18,... | collective-permute-start | bytes 49160 | tf_op jit(solution)/shard_map/ppermute | solution.py:494
  192.7 5.4 %collective-permute-start.8 = (f32[32,128]{1,0:T(8,128)S(1)}, f32[32,128]{1,0:T(8,128)S(1)}, u32[]{:S(2)}, u32[]{:S(2)}) collective-permute-start(f32[32,128]{1,0:T(8,128)S(1)} %get-tuple-element.71), channel_id=1, source_target_pairs={{0,16},{2,18},{4,20},{6,22},{8,24},{10,26},{12,28},{14,30},{16,0},... | collective-permute-start | bytes 49160 | tf_op jit(solution)/shard_map/ppermute | solution.py:494
  192.7 5.4 %collective-permute-start.7 = (f32[32,128]{1,0:T(8,128)S(1)}, f32[32,128]{1,0:T(8,128)S(1)}, u32[]{:S(2)}, u32[]{:S(2)}) collective-permute-start(f32[32,128]{1,0:T(8,128)S(1)} %get-tuple-element.72), channel_id=1, source_target_pairs={{0,8},{2,10},{4,12},{6,14},{8,16},{10,18},{12,20},{14,22},{16,24},... | collective-permute-start | bytes 49160 | tf_op jit(solution)/shard_map/ppermute | solution.py:494
  198.1 68.8 %collective-permute-start.10 = (f32[32,128]{1,0:T(8,128)S(1)}, f32[32,128]{1,0:T(8,128)S(1)}, u32[]{:S(2)}, u32[]{:S(2)}) collective-permute-start(f32[32,128]{1,0:T(8,128)S(1)} %fusion.16), channel_id=1, source_target_pairs={{0,32},{2,34},{4,36},{6,38},{8,40},{10,42},{12,44},{14,46},{16,48}... | collective-permute-start | bytes 49160 | tf_op jit(solution)/shard_map/ppermute | solution.py:494
  266.9 4.6 %collective-permute-start.11 = (f32[32,128]{1,0:T(8,128)S(1)}, f32[32,128]{1,0:T(8,128)S(1)}, u32[]{:S(2)}, u32[]{:S(2)}) collective-permute-start(f32[32,128]{1,0:T(8,128)S(1)} %add.147), channel_id=1, source_target_pairs={{0,64},{2,66},{4,68},{6,70},{8,72},{10,74},{12,76},{14,78},{16,80}... | collective-permute-start | bytes 49160 | tf_op jit(solution)/shard_map/ppermute | solution.py:494
  271.6 7.6 %collective-permute-start.12 = (f32[32,128]{1,0:T(8,128)S(1)}, f32[32,128]{1,0:T(8,128)S(1)}, u32[]{:S(2)}, u32[]{:S(2)}) collective-permute-start(f32[32,128]{1,0:T(8,128)S(1)} %add.148), channel_id=1, source_target_pairs={{0,128},{2,130},{4,132},{6,134},{8,136},{10,138},{12,140},{14,142}... | collective-permute-start | bytes 49160 | tf_op jit(solution)/shard_map/ppermute | solution.py:494
  279.2 4.7 %collective-permute-start.15 = (f32[32,128]{1,0:T(8,128)S(1)}, f32[32,128]{1,0:T(8,128)S(1)}, u32[]{:S(2)}, u32[]{:S(2)}) collective-permute-start(f32[32,128]{1,0:T(8,128)S(1)} %add.149), channel_id=1, source_target_pairs={{0,24},{2,26},{4,28},{6,30},{8,0},{10,2},{12,4},{14,6},{16,8},{18,... | collective-permute-start | bytes 49160 | tf_op jit(solution)/shard_map/ppermute | solution.py:494
  279.7 5.2 %collective-permute-start.14 = (f32[32,128]{1,0:T(8,128)S(1)}, f32[32,128]{1,0:T(8,128)S(1)}, u32[]{:S(2)}, u32[]{:S(2)}) collective-permute-start(f32[32,128]{1,0:T(8,128)S(1)} %add.149), channel_id=1, source_target_pairs={{0,16},{2,18},{4,20},{6,22},{8,24},{10,26},{12,28},{14,30},{16,0},... | collective-permute-start | bytes 49160 | tf_op jit(solution)/shard_map/ppermute | solution.py:494
  282.1 3.7 %collective-permute-start.13 = (f32[32,128]{1,0:T(8,128)S(1)}, f32[32,128]{1,0:T(8,128)S(1)}, u32[]{:S(2)}, u32[]{:S(2)}) collective-permute-start(f32[32,128]{1,0:T(8,128)S(1)} %add.149), channel_id=1, source_target_pairs={{0,8},{2,10},{4,12},{6,14},{8,16},{10,18},{12,20},{14,22},{16,24},... | collective-permute-start | bytes 49160 | tf_op jit(solution)/shard_map/ppermute | solution.py:494
  285.8 6.3 %collective-permute-start.17 = (f32[4,32,128]{2,1,0:T(8,128)S(1)}, f32[4,32,128]{2,1,0:T(8,128)S(1)}, u32[]{:S(2)}, u32[]{:S(2)}) collective-permute-start(f32[4,32,128]{2,1,0:T(8,128)S(1)} %get-tuple-element.69), channel_id=1, source_target_pairs={{0,4},{2,6},{4,0},{6,2},{8,12},{10,14},{12,8},{14,10},{16,20},{18,... | collective-permute-start | bytes 196616 | tf_op jit(solution)/shard_map/ppermute | solution.py:494
  288.9 5.5 %collective-permute-start.16 = (f32[4,32,128]{2,1,0:T(8,128)S(1)}, f32[4,32,128]{2,1,0:T(8,128)S(1)}, u32[]{:S(2)}, u32[]{:S(2)}) collective-permute-start(f32[4,32,128]{2,1,0:T(8,128)S(1)} %get-tuple-element.69), channel_id=1, source_target_pairs={{0,2},{2,4},{4,6},{6,0},{8,10},{10,12},{12,14},{14,8},{16,18},{18,... | collective-permute-start | bytes 196616 | tf_op jit(solution)/shard_map/ppermute | solution.py:494
  289.5 4.9 %collective-permute-start.18 = (f32[4,32,128]{2,1,0:T(8,128)S(1)}, f32[4,32,128]{2,1,0:T(8,128)S(1)}, u32[]{:S(2)}, u32[]{:S(2)}) collective-permute-start(f32[4,32,128]{2,1,0:T(8,128)S(1)} %get-tuple-element.69), channel_id=1, source_target_pairs={{0,6},{2,0},{4,2},{6,4},{8,14},{10,8},{12,10},{14,12},{16,22},{18,... | collective-permute-start | bytes 196616 | tf_op jit(solution)/shard_map/ppermute | solution.py:494
  (11 other events, 26.2 us)

commit v3 on v2

v3 whole, which is shorter than its diff:
```python
import math

import jax
import jax.numpy as jnp
from jax import lax
from jax.experimental import pallas as pl
from jax.experimental.pallas import tpu as pltpu
from jax.sharding import PartitionSpec as P

F32 = jnp.float32
BF16 = jnp.bfloat16
MIB = 1 << 20


def dot(a, b, dims):
    return lax.dot_general(a, b, (dims, ((), ())), preferred_element_type=F32)


NN = ((1,), (0,))
NT = ((1,), (1,))
TN = ((0,), (0,))


def params(mib, steps):
    return pltpu.CompilerParams(
        dimension_semantics=("arbitrary",) * steps, vmem_limit_bytes=mib * MIB
    )


ANY = pl.BlockSpec(memory_space=pl.ANY)
HBM = pl.BlockSpec(memory_space=pltpu.HBM)


def own_copies(mib):
    return pltpu.CompilerParams(vmem_limit_bytes=mib * MIB)


def pack_kernel(send, hubs, feat, out, hub_rows, tails, sems):
    parts, height, width = out.shape
    edge = height - 8

    @pl.loop(0, parts // 8)
    def _(g):
        for i in range(8):
            q = g * 8 + i
            start = pl.multiple_of(send[q] * edge, edge)
            pltpu.make_async_copy(
                feat.at[pl.ds(start, edge), :], out.at[q, pl.ds(0, edge), :], sems.at[0]
            ).start()

    hub_rows[...] = jnp.zeros_like(hub_rows)
    for j in range(2):
        row = hubs[j]
        base = pl.multiple_of((row // 16) * 16, 16)
        block = feat[pl.ds(base, 16), :].astype(F32)
        here = lax.broadcasted_iota(jnp.int32, block.shape, 0) == row - base
        hub_rows[j : j + 1, :] = jnp.sum(jnp.where(here, block, 0.0), axis=0, keepdims=True)
    tails[...] = jnp.broadcast_to(hub_rows[...].astype(BF16)[None], tails.shape)
    tail = out.at[:, pl.ds(edge, 8), :]
    pltpu.make_async_copy(tails, tail, sems.at[1]).start()
    pltpu.make_async_copy(tails, tail, sems.at[1]).wait()
    body = out.at[:, pl.ds(0, edge), :]
    pltpu.make_async_copy(body, body, sems.at[0]).wait()


def pack(features, send_tile, hub_rows, edge):
    rows, width = features.shape
    parts = send_tile.shape[0]
    return pl.pallas_call(
        pack_kernel,
        name="pack",
        out_shape=jax.ShapeDtypeStruct((parts, edge + 8, width), BF16),
        grid_spec=pltpu.PrefetchScalarGridSpec(
            num_scalar_prefetch=2,
            grid=(1,),
            in_specs=[pl.BlockSpec((rows, width), lambda g, *_: (0, 0))],
            out_specs=HBM,
            scratch_shapes=[
                pltpu.VMEM((8, width), F32),
                pltpu.VMEM((parts, 8, width), BF16),
                pltpu.SemaphoreType.DMA((2,)),
            ],
        ),
        compiler_params=own_copies(58),
    )(send_tile, hub_rows, features)


def prepare_kernel(
    row, count, order, first, second, kinds, values, panel, *rest
):
    inv, flipped, pairs, squares = rest[-4:]
    step, steps = pl.program_id(0), pl.num_programs(0)
    edge = values.shape[1]
    slots, duos = flipped.shape[0], pairs.shape[0]

    @pl.when(step == 0)
    def _():
        squares[...] = jnp.zeros_like(squares)

    @pl.loop(0, slots)
    def _(i):
        k = step * slots + i
        flipped[i] = values[order[k]].T
        tile = values[k].astype(F32)
        live = (k < count[0]).astype(F32)
        start = pl.multiple_of(row[k] * edge, edge)
        squares[pl.ds(start, edge), :] += tile * tile * live

    @pl.loop(0, duos)
    def _(i):
        p = step * duos + i
        has_first = (kinds[p] > 0).astype(BF16)
        has_second = (kinds[p] > 1).astype(BF16)
        pairs[i, :, :edge] = values[first[p]] * has_first
        pairs[i, :, edge:] = values[second[p]] * has_second

    @pl.when(step == steps - 1)
    def _():
        @pl.loop(0, squares.shape[0] // edge)
        def _(t):
            at = pl.ds(pl.multiple_of(t * edge, edge), edge)
            wide = panel[at, :].astype(F32)
            wide = wide * wide
            half = wide.shape[1] // 2
            total = jnp.sum(
                squares[at, :] + wide[:, :half] + wide[:, half:], axis=1, keepdims=True
            )
            inv[at, :] = jnp.broadcast_to(lax.rsqrt(1.0 + total), (edge, inv.shape[1]))


def prepare(row, count, order, first, second, kinds, values, panel, duos, ready):
    slots, edge, _ = values.shape
    rows, hubs = panel.shape
    steps = 4
    whole = lambda g, *_: (0, 0)
    return pl.pallas_call(
        prepare_kernel,
        name="prepare",
        out_shape=(
            jax.ShapeDtypeStruct((rows, edge), F32),
            jax.ShapeDtypeStruct((slots, edge, edge), BF16),
            jax.ShapeDtypeStruct((duos, edge, 2 * edge), BF16),
        ),
        grid_spec=pltpu.PrefetchScalarGridSpec(
            num_scalar_prefetch=6,
            grid=(steps,),
            in_specs=[
                pl.BlockSpec((slots, edge, edge), lambda g, *_: (0, 0, 0)),
                pl.BlockSpec((rows, hubs), whole),
            ]
            + [ANY] * len(ready),
            out_specs=(
                pl.BlockSpec((rows, edge), whole),
                pl.BlockSpec((slots // steps, edge, edge), lambda g, *_: (g, 0, 0)),
                pl.BlockSpec((duos // steps, edge, 2 * edge), lambda g, *_: (g, 0, 0)),
            ),
            scratch_shapes=[pltpu.VMEM((rows, edge), F32)],
        ),
        compiler_params=params(40, 1),
        cost_estimate=pl.CostEstimate(
            flops=60_000_000_000, bytes_accessed=40_000_000, transcendentals=0
        ),
    )(row, count, order, first, second, kinds, values, panel, *ready)


DUO_STEP = 16


def gather_kernel(
    row, owner_a, owner_b, n_duos, pairs, incoming, panel, inv, out,
    tail, pan, tiles, norm, duos, tail_wide, hub_wide, sums, result, sems, duo_sems, out_sems,
):
    parts, edge, _ = tiles.shape
    rows = sums.shape[0]
    copy = pltpu.make_async_copy
    tail_in = copy(incoming.at[:, pl.ds(edge, 8), :], tail, sems.at[0])
    panel_in = copy(panel, pan, sems.at[1])
    tiles_in = copy(incoming.at[:, pl.ds(0, edge), :], tiles, sems.at[2])
    norm_in = copy(inv, norm, sems.at[3])
    steps = duos.shape[0] // DUO_STEP
    duo_in = [
        copy(pairs.at[pl.ds(c * DUO_STEP, DUO_STEP)], duos.at[pl.ds(c * DUO_STEP, DUO_STEP)], duo_sems.at[c])
        for c in range(steps)
    ]
    tail_in.start()
    panel_in.start()
    tiles_in.start()
    for c in range(steps):

        @pl.when(c * DUO_STEP < n_duos[0])
        def _():
            duo_in[c].start()

    norm_in.start()

    tail_in.wait()
    tail_wide[...] = tail[...].reshape(tail_wide.shape).astype(F32)
    for j in range(2):
        hub_wide[pl.ds(j, parts, stride=2), :] = tail_wide[pl.ds(j, parts, stride=8), :]
    hub_feats = hub_wide[...].astype(BF16)
    panel_in.wait()
    block = 512
    for t in range(rows // block):
        at = pl.ds(t * block, block)
        sums[at, :] = dot(pan[at, :], hub_feats, NN)
    tiles_in.wait()
    for c in range(steps):

        @pl.when(c * DUO_STEP < n_duos[0])
        def _():
            duo_in[c].wait()
            products = []
            for i in range(DUO_STEP):
                p = c * DUO_STEP + i
                columns = jnp.concatenate([tiles[owner_a[p]], tiles[owner_b[p]]], axis=0)
                products.append(dot(duos[p], columns, NN))
            for i in range(DUO_STEP):
                start = pl.multiple_of(row[c * DUO_STEP + i] * edge, edge)
                sums[pl.ds(start, edge), :] += products[i]

    norm_in.wait()
    block = rows // 4
    sent = []
    for t in range(4):
        at = pl.ds(t * block, block)
        result[at, :] = (sums[at, :] * norm[at, :]).astype(BF16)
        sent.append(copy(result.at[at, :], out.at[at, :], out_sems.at[t]))
        sent[-1].start()
    for s in sent:
        s.wait()


def gather(row, owner_a, owner_b, n_duos, pairs, incoming, panel, inv):
    duos, edge, _ = pairs.shape
    rows, hubs = panel.shape
    parts = incoming.shape[0]
    return pl.pallas_call(
        gather_kernel,
        name="gather",
        out_shape=jax.ShapeDtypeStruct((rows, edge), BF16),
        grid_spec=pltpu.PrefetchScalarGridSpec(
            num_scalar_prefetch=4,
            grid=(1,),
            in_specs=[ANY] * 4,
            out_specs=HBM,
            scratch_shapes=[
                pltpu.VMEM((parts, 8, edge), BF16),
                pltpu.VMEM((rows, hubs), BF16),
                pltpu.VMEM((parts, edge, edge), BF16),
                pltpu.VMEM((rows, edge), F32),
                pltpu.VMEM(pairs.shape, BF16),
                pltpu.VMEM((parts * 8, edge), F32),
                pltpu.VMEM((hubs, edge), F32),
                pltpu.VMEM((rows, edge), F32),
                pltpu.VMEM((rows, edge), BF16),
                pltpu.SemaphoreType.DMA((4,)),
                pltpu.SemaphoreType.DMA((duos // DUO_STEP,)),
                pltpu.SemaphoreType.DMA((4,)),
            ],
        ),
        compiler_params=own_copies(58),
    )(row, owner_a, owner_b, n_duos, pairs, incoming, panel, inv)


ROW_STEPS = 4
MID_MIB = 56
SLOT_STEP = 16


def middle_kernel(
    order_row, order_owner, count,
    feat, feat_peer, agg, agg_peer, cot, cot_peer, inv, panel, flipped, own_w, nbr_w,
    layer, slopes, terms,
    feat_v, feat_peer_v, agg_v, agg_peer_v, cot_v, cot_peer_v, inv_v, panel_v, flipped_v,
    layer_v, slopes_v, agg_slopes, terms_v, hub_acc, hub_wide, carry,
    in_sems, flip_sems, out_sems, term_sems,
):
    rows, half = feat_v.shape
    slots, edge, _ = flipped_v.shape
    parts = terms_v.shape[0]
    copy = pltpu.make_async_copy
    block = rows // ROW_STEPS
    sources = (feat, feat_peer, agg, agg_peer, cot, cot_peer, inv, panel)
    places = (feat_v, feat_peer_v, agg_v, agg_peer_v, cot_v, cot_peer_v, inv_v, panel_v)
    at = [pl.ds(t * block, block) for t in range(ROW_STEPS)]
    inputs = [
        [copy(s.at[at[t], :], d.at[at[t], :], in_sems.at[t, i]) for i, (s, d) in enumerate(zip(sources, places))]
        for t in range(ROW_STEPS)
    ]
    steps = slots // SLOT_STEP
    flips = [
        copy(flipped.at[pl.ds(b * SLOT_STEP, SLOT_STEP)], flipped_v.at[pl.ds(b * SLOT_STEP, SLOT_STEP)], flip_sems.at[b])
        for b in range(steps)
    ]
    for t in range(ROW_STEPS):
        for c in inputs[t]:
            c.start()
    for b in range(steps):

        @pl.when(b * SLOT_STEP < count[0])
        def _():
            flips[b].start()

    terms_v[:, :edge, :] = jnp.zeros((parts, edge, half), BF16)
    hub_wide[...] = jnp.zeros_like(hub_wide)
    carry[...] = jnp.zeros_like(carry)

    sent = []
    for t in range(ROW_STEPS):
        for c in inputs[t]:
            c.wait()
        here = at[t]
        preact = dot(
            jnp.concatenate([feat_v[here, :], feat_peer_v[here, :]], axis=1), own_w[...], NN
        ) + dot(jnp.concatenate([agg_v[here, :], agg_peer_v[here, :]], axis=1), nbr_w[...], NN)
        layer_v[here, :] = jnp.maximum(preact[:, :half], 0.0).astype(BF16)
        cotangent = jnp.concatenate([cot_v[here, :], cot_peer_v[here, :]], axis=1).astype(F32)
        slope = jnp.where(preact > 0, cotangent, 0.0).astype(BF16)
        slopes_v[here, :] = slope
        sent.append(copy(layer_v.at[here, :], layer.at[here, :], out_sems.at[t, 0]))
        sent.append(copy(slopes_v.at[here, :], slopes.at[here, :], out_sems.at[t, 1]))
        sent[-2].start()
        sent[-1].start()
        back = (dot(slope, nbr_w[:half, :], NT) * inv_v[here, :]).astype(BF16)
        agg_slopes[here, :] = back
        hub = dot(panel_v[here, :], back, TN)
        if t == 0:
            hub_acc[...] = hub
        else:
            hub_acc[...] += hub

    for j in range(2):
        hub_wide[pl.ds(j, parts, stride=8), :] = hub_acc[pl.ds(j, parts, stride=2), :]
    terms_v[:, edge:, :] = hub_wide[...].reshape(parts, 8, half).astype(BF16)

    group = parts // 8
    for b in range(steps):

        @pl.when(b * SLOT_STEP < count[0])
        def _():
            flips[b].wait()
            products = []
            for i in range(SLOT_STEP):
                k = b * SLOT_STEP + i
                start = pl.multiple_of(order_row[k] * edge, edge)
                products.append(dot(flipped_v[k], agg_slopes[pl.ds(start, edge), :], NN))
            total = carry[...]
            for i in range(SLOT_STEP):
                k = b * SLOT_STEP + i
                live = (k < count[0]).astype(F32)
                fresh = products[i] * live
                if k:
                    same = (order_owner[k] == order_owner[k - 1]).astype(F32)
                    total = fresh + total * same
                else:
                    total = fresh
                terms_v[order_owner[k], :edge, :] = total.astype(BF16)
            carry[...] = total
            first = order_owner[b * SLOT_STEP] // group if b else 0
            after = (b + 1) * SLOT_STEP
            last = jnp.where(
                after >= count[0], parts // group, order_owner[min(after, slots - 1)] // group
            )

            @pl.loop(first, last)
            def _(g):
                owners = pl.ds(g * group, group)
                copy(terms_v.at[owners], terms.at[owners], term_sems.at[0]).start()

    for c in sent:
        c.wait()
    copy(terms_v, terms, term_sems.at[0]).wait()


def middle(
    order_row, order_owner, count,
    feat, feat_peer, agg, agg_peer, cot, cot_peer, inv, panel, flipped, own_w, nbr_w, parts,
):
    rows, half = feat.shape
    hubs = panel.shape[1]
    edge = flipped.shape[1]
    narrow = pltpu.VMEM((rows, half), BF16)
    wide = pltpu.VMEM((rows, 2 * half), BF16)
    whole = lambda g, *_: (0, 0)
    height = edge + 8
    return pl.pallas_call(
        middle_kernel,
        name="middle",
        out_shape=(
            jax.ShapeDtypeStruct((rows, half), BF16),
            jax.ShapeDtypeStruct((rows, 2 * half), BF16),
            jax.ShapeDtypeStruct((parts, height, half), BF16),
        ),
        grid_spec=pltpu.PrefetchScalarGridSpec(
            num_scalar_prefetch=3,
            grid=(1,),
            in_specs=[ANY] * 9
            + [pl.BlockSpec(own_w.shape, whole), pl.BlockSpec(nbr_w.shape, whole)],
            out_specs=(HBM, HBM, HBM),
            scratch_shapes=[narrow] * 6
            + [
                pltpu.VMEM((rows, half), F32),
                pltpu.VMEM((rows, hubs), BF16),
                pltpu.VMEM(flipped.shape, BF16),
                narrow,
                wide,
                narrow,
                pltpu.VMEM((parts, height, half), BF16),
                pltpu.VMEM((hubs, half), F32),
                pltpu.VMEM((4 * hubs, half), F32),
                pltpu.VMEM((edge, half), F32),
                pltpu.SemaphoreType.DMA((ROW_STEPS, 8)),
                pltpu.SemaphoreType.DMA((flipped.shape[0] // SLOT_STEP,)),
                pltpu.SemaphoreType.DMA((ROW_STEPS, 2)),
                pltpu.SemaphoreType.DMA((1,)),
            ],
        ),
        compiler_params=own_copies(MID_MIB),
    )(
        order_row, order_owner, count,
        feat, feat_peer, agg, agg_peer, cot, cot_peer, inv, panel, flipped, own_w, nbr_w,
    )


def side_kernel(place, feat, agg, slopes, own_w, grads, direct, acc):
    step, steps = pl.program_id(0), pl.num_programs(0)
    half = feat.shape[1]
    s = slopes[...]
    direct[...] = dot(s, own_w[...], NT)
    part = dot(jnp.concatenate([feat[...], agg[...]], axis=1), s, TN)

    @pl.when(step == 0)
    def _():
        acc[...] = part

    @pl.when(step > 0)
    def _():
        acc[...] += part

    @pl.when(step == steps - 1)
    def _():
        n = half // 4
        for c in range(4):
            for r in range(4):
                grads[(c + 4 - place[0]) % 4, (r + 4 - place[1]) % 4] = acc[
                    (c // 2) * half + r * n : (c // 2) * half + (r + 1) * n,
                    (c % 2) * half : (c % 2 + 1) * half,
                ]


def side(place, feat, agg, slopes, own_w):
    rows, half = feat.shape
    block = 512
    by_row = lambda width: pl.BlockSpec((block, width), lambda g, *_: (g, 0))
    return pl.pallas_call(
        side_kernel,
        name="side",
        out_shape=(
            jax.ShapeDtypeStruct((4, 4, half // 4, half), F32),
            jax.ShapeDtypeStruct((rows, half), F32),
        ),
        grid_spec=pltpu.PrefetchScalarGridSpec(
            num_scalar_prefetch=1,
            grid=(rows // block,),
            in_specs=[
                by_row(half),
                by_row(half),
                by_row(2 * half),
                pl.BlockSpec(own_w.shape, lambda g, *_: (0, 0)),
            ],
            out_specs=(
                pl.BlockSpec((4, 4, half // 4, half), lambda g, *_: (0, 0, 0, 0)),
                by_row(half),
            ),
            scratch_shapes=[pltpu.VMEM((2 * half, 2 * half), F32)],
        ),
        compiler_params=params(24, 1),
    )(place, feat, agg, slopes, own_w)


def finish_kernel(send, hubs, returned, direct, grads, out, grads_out, acc, landed, sems, part_sems):
    parts, height, half = landed.shape
    edge = acc.shape[1]
    copy = pltpu.make_async_copy
    steps = 8
    group = parts // steps
    arrivals = [
        copy(returned.at[pl.ds(g * group, group)], landed.at[pl.ds(g * group, group)], part_sems.at[g])
        for g in range(steps)
    ]
    start = copy(direct, acc, sems.at[0])
    start.start()
    grads_out[...] = grads[...]
    for c in arrivals:
        c.start()
    start.wait()
    total = jnp.zeros((8, half), F32)
    for g in range(steps):
        arrivals[g].wait()
        for i in range(group):
            p = g * group + i
            acc[send[p]] += landed[p, :edge, :].astype(F32)
            total = total + landed[p, edge:, :].astype(F32)
    for j in range(2):
        row = hubs[j]
        tile, inside = row // edge, row % edge
        base = pl.multiple_of((inside // 8) * 8, 8)
        here = lax.broadcasted_iota(jnp.int32, (8, half), 0) == inside - base
        acc[tile, pl.ds(base, 8), :] += jnp.where(here, total[j : j + 1, :], 0.0)
    end = copy(acc, out, sems.at[1])
    end.start()
    end.wait()


def finish(send_tile, hub_rows, returned, direct, grads):
    small = pl.BlockSpec(grads.shape, lambda g, *_: (0, 0))
    return pl.pallas_call(
        finish_kernel,
        name="finish",
        out_shape=(
            jax.ShapeDtypeStruct(direct.shape, F32),
            jax.ShapeDtypeStruct(grads.shape, F32),
        ),
        grid_spec=pltpu.PrefetchScalarGridSpec(
            num_scalar_prefetch=2,
            grid=(1,),
            in_specs=[ANY, ANY, small],
            out_specs=(HBM, small),
            scratch_shapes=[
                pltpu.VMEM(direct.shape, F32),
                pltpu.VMEM(returned.shape, BF16),
                pltpu.SemaphoreType.DMA((2,)),
                pltpu.SemaphoreType.DMA((8,)),
            ],
        ),
        compiler_params=own_copies(58),
    )(send_tile, hub_rows, returned, direct, grads)


def plan(tile_row, tile_owner, tile_count, tiles, parts):
    slots = tile_row.shape[0]
    index = jnp.arange(slots, dtype=jnp.int32)
    live = index < tile_count[0]
    earlier = index[None, :] < index[:, None]
    pick = lambda where, what: jnp.sum(jnp.where(where, what, 0), axis=1, dtype=jnp.int32)

    key = jnp.where(live, tile_owner, parts)
    before = (key[None, :] < key[:, None]) | ((key[None, :] == key[:, None]) & earlier)
    rank = jnp.sum(before, axis=1, dtype=jnp.int32)
    last = jnp.minimum(index, tile_count[0] - 1)
    at = rank[None, :] == last[:, None]
    order = pick(at, index[None, :])
    order_row = pick(at, tile_row[None, :])
    order_owner = pick(at, tile_owner[None, :])

    mates = live[None, :] & (tile_row[None, :] == tile_row[:, None])
    inside = jnp.sum(mates & earlier, axis=1, dtype=jnp.int32)
    rows = jnp.arange(tiles, dtype=jnp.int32)
    per_row = jnp.sum(live[None, :] & (tile_row[None, :] == rows[:, None]), axis=1, dtype=jnp.int32)
    row_pairs = (per_row + 1) // 2
    lower = jnp.sum(
        jnp.where(rows[None, :] < tile_row[:, None], row_pairs[None, :], 0), axis=1, dtype=jnp.int32
    )
    pair = jnp.where(live, lower + inside // 2, -1)
    duos = (slots + tiles) // 2
    p = jnp.arange(duos, dtype=jnp.int32)
    is_first = (pair[None, :] == p[:, None]) & (inside[None, :] % 2 == 0)
    is_second = (pair[None, :] == p[:, None]) & (inside[None, :] % 2 == 1)
    first = pick(is_first, index[None, :])
    second = pick(is_second, index[None, :])
    owner_a = pick(is_first, tile_owner[None, :])
    owner_b = pick(is_second, tile_owner[None, :])
    pair_row = pick(is_first, tile_row[None, :])
    kinds = pick(is_first, 1) + pick(is_second, 1)
    n_duos = jnp.sum(row_pairs, dtype=jnp.int32).reshape(1)
    return (
        (order, order_row, order_owner),
        (first, second, kinds, pair_row, owner_a, owner_b, n_duos),
        duos,
    )


def exchange(block):
    return lax.all_to_all(block, "dom", split_axis=0, concat_axis=0, tiled=True)


def swap(block):
    return lax.ppermute(block, "feat", [(0, 1), (1, 0)])


def move(block, axis, amount):
    def target(d):
        z, x, y = d // 16, (d // 4) % 4, d % 4
        if axis == "y":
            y = (y + amount) % 4
        elif axis == "x":
            x = (x + amount) % 4
        else:
            z = z ^ amount
        return (z * 4 + x) * 4 + y

    return lax.ppermute(block, "dom", [(d, target(d)) for d in range(lax.axis_size("dom"))])


def add_up(blocks):
    for axis in ("y", "x"):
        moved = [move(blocks[i], axis, i) for i in (1, 2, 3)]
        blocks = (blocks[0] + moved[0]) + (moved[1] + moved[2])
    lines = [blocks] + [move(blocks, "z", bits) for bits in range(1, 8)]
    while len(lines) > 1:
        lines = [a + b for a, b in zip(lines[::2], lines[1::2])]
    return lines[0]


def shards(
    features,
    self_weight,
    neighbor_weight,
    tile_values,
    tile_row,
    tile_owner,
    send_tile,
    tile_count,
    hub_panel,
    hub_rows,
    cotangent,
):
    rows_dev, half = features.shape
    tile_edge = tile_values.shape[1]
    tiles_dev = rows_dev // tile_edge
    dom_size = lax.axis_size("dom")
    core = lax.axis_index("feat")

    outgoing = pack(features, send_tile, hub_rows, tile_edge)
    incoming = exchange(outgoing)

    def own_first(w):
        return jnp.where(core == 0, w, jnp.concatenate([w[:, half:], w[:, :half]], axis=1))

    weights = own_first(jnp.concatenate([self_weight, neighbor_weight], axis=0))
    peer_weights = swap(weights)
    peer_weights = jnp.concatenate([peer_weights[:, half:], peer_weights[:, :half]], axis=1)
    own_w = jnp.concatenate([weights[:half], peer_weights[:half]], axis=0)
    nbr_w = jnp.concatenate([weights[half:], peer_weights[half:]], axis=0)
    feat_peer = swap(features)
    cot_peer = swap(cotangent)

    by_owner, by_row, duos = plan(tile_row, tile_owner, tile_count, tiles_dev, dom_size)
    order, order_row, order_owner = by_owner
    first, second, kinds, pair_row, owner_a, owner_b, n_duos = by_row
    inv, flipped, pairs = prepare(
        tile_row, tile_count, order, first, second, kinds, tile_values, hub_panel, duos,
        (own_w, nbr_w, feat_peer, cot_peer),
    )

    aggregate = gather(pair_row, owner_a, owner_b, n_duos, pairs, incoming, hub_panel, inv)
    agg_peer = swap(aggregate)
    layer_out, slopes, terms = middle(
        order_row, order_owner, tile_count,
        features, feat_peer, aggregate, agg_peer, cotangent, cot_peer, inv, hub_panel, flipped,
        own_w, nbr_w, dom_size,
    )
    returned = exchange(terms)

    dom = lax.axis_index("dom")
    place_y, place_x = dom % 4, (dom // 4) % 4
    grads, direct = side(
        jnp.stack([place_y, place_x]).astype(jnp.int32), features, aggregate, slopes, own_w[:half]
    )
    grads = add_up(grads)
    from_x = [move(grads, "x", i) for i in (1, 2, 3)]
    input_grad, grads = finish(
        send_tile, hub_rows, returned, direct.reshape(tiles_dev, tile_edge, half), grads
    )
    input_grad = input_grad.reshape(rows_dev, half)
    grads = jnp.stack([grads] + from_x)
    grads = jnp.stack([grads] + [move(grads, "y", i) for i in (1, 2, 3)])
    c = jnp.arange(4) ^ core
    r = jnp.arange(4)
    index = (((place_y - c) % 4)[:, None] * 4 + ((place_x - r) % 4)[None, :]).reshape(16)
    grads = grads.reshape(16, half // 4, half)[index].reshape(4, half, half)
    grads = grads * (1.0 / math.sqrt(rows_dev * dom_size))
    self_grad = jnp.concatenate([grads[0], grads[1]], axis=1)
    neighbor_grad = jnp.concatenate([grads[2], grads[3]], axis=1)
    return (layer_out, self_grad, neighbor_grad, input_grad)


def solution(mesh):
    placed = (
        P("dom", "feat"),
        P("feat", None),
        P("feat", None),
        P("dom", None, None),
        P("dom"),
        P("dom"),
        P("dom"),
        P("dom"),
        P("dom", None),
        P("dom"),
        P("dom", "feat"),
    )
    return jax.shard_map(
        shards,
        mesh=mesh,
        in_specs=placed,
        out_specs=(P("dom", "feat"), P("feat", None), P("feat", None), P("dom", "feat")),
        check_vma=False,
    )
```

time: 307 us -> 288 us (0.938)
  waiting for transfers between devices: 163 us -> 150 us
  starting transfers between devices: 56 us -> 67.9 us
  Pallas kernels: 63.4 us -> 54 us
  local copies, waits for them, and re-layouts: 15.3 us -> 8.41 us
    ppermute x15 -> x19, waiting for transfers between devices: 90.8 us -> 75.1 us  [move(): lax.ppermute(block, 'dom', [(d, target(d)) for d in range(lax.axis_size('...]
    ppermute x15 -> x19, starting transfers between devices: 26.8 us -> 38.2 us  [move(): lax.ppermute(block, 'dom', [(d, target(d)) for d in range(lax.axis_size('...]
    pallas_call x2 -> x1, Pallas kernels: 15.3 us -> 7.1 us  [finish(): pl.pallas_call(finish_kernel, name='finish', out_shape=(jax.ShapeDtypeStr...]
    unnamed x45 -> x33, local copies, waits for them, and re-layouts: 14.6 us -> 7.68 us
  transfers between devices with their start and end apart: 21 -> 25, of which waited for: 12 -> 10; matrix products, arithmetic and copies ran while one was open for 2% -> 1% of each run, Pallas kernels for 11% -> 13%
where the time goes in v3:
time: 288 us
  waiting for transfers between devices  150 us (52%)
  starting transfers between devices  67.9 us (24%)
  Pallas kernels  54 us (19%)
  local copies, waits for them, and re-layouts  8.41 us (3%)
  other arithmetic  5.15 us (2%)
    ppermute x19, waiting for transfers between devices, move(): lax.ppermute(block, 'dom', [(d, target(d)) for d in range(lax.axis_size('...  75.1 us
    all_to_all x2, waiting for transfers between devices, exchange(): return lax.all_to_all(block, 'dom', split_axis=0, concat_axis=0, tiled=True)  72.3 us
    ppermute x19, starting transfers between devices, move(): lax.ppermute(block, 'dom', [(d, target(d)) for d in range(lax.axis_size('...  38.2 us
    all_to_all x2, starting transfers between devices, exchange(): return lax.all_to_all(block, 'dom', split_axis=0, concat_axis=0, tiled=True)  28.8 us
    pallas_call x1, Pallas kernels, prepare(): pl.pallas_call(prepare_kernel, name='prepare', out_shape=(jax.ShapeDtypeS...  21.9 us
    pallas_call x1, Pallas kernels, middle(): pl.pallas_call(middle_kernel, name='middle', out_shape=(jax.ShapeDtypeStr...  10.6 us
    unnamed x33, local copies, waits for them, and re-layouts  7.68 us
    pallas_call x1, Pallas kernels, finish(): pl.pallas_call(finish_kernel, name='finish', out_shape=(jax.ShapeDtypeStr...  7.1 us
  transfers between devices with their start and end apart: 25, of which 10 were waited for; matrix products, arithmetic and copies ran while one was open for 1% of the time, Pallas kernels for 13%

profile of v3, /device:TPU:2, one launch (start us, length us, event | category | flops | bytes accessed | tf_op | source)
XLA Modules:
  0.0 287.5 jit_solution(8687660794394623877)
XLA Ops:
  0.7 4.0 %pack.1 = bf16[128,136,128]{2,1,0:T(8,128)(2,1)} custom-call(s32[128]{0:T(128)} %send.3, s32[2]{0:T(128)} %hubs.3, bf16[4096,128]{1,0:T(8,128)(2,1)} %feat.5), custom_call_target="tpu_custom_call" | custom-call | tf_op jit(solution)/shard_map/pack/pallas_call | solution.py:69
  4.8 16.0 %all-to-all-start = ((bf16[128,136,128]{2,1,0:T(8,128)(2,1)}), bf16[128,136,128]{2,1,0:T(8,128)(2,1)}, u32[]{:S(2)}, u32[]{:S(2)}) async-start(bf16[128,136,128]{2,1,0:T(8,128)(2,1)} %pack.1), calls=%async_computation | async-start | bytes 8912896 | tf_op jit(solution)/shard_map/all_to_all | solution.py:584
  25.1 21.9 %prepare.1 = (f32[4096,128]{1,0:T(8,128)S(1)}, bf16[160,128,128]{2,1,0:T(8,128)(2,1)S(1)}, bf16[96,128,256]{2,1,0:T(8,128)(2,1)}) custom-call(s32[160]{0:T(256)S(1)} %copy-done.10, s32[1]{0:T(128)} %copy.16.count, s32[160]{0:T(256)S(1)} %get-tuple-element.24.order, s32[96]{0:T(128)S(1)} %get-tuple-element.30.first, s32[96]{0:T(128)S(1)} %get-tuple-element.33.second, ...), custom_call_target="tpu_custom_call" | custom-call | flops 60000002048 | bytes 40000000 | tf_op jit(solution)/shard_map/prepare/pallas_call | solution.py:136
  48.4 2.4 copy-done.4
  50.8 72.3 %all-to-all-done.incoming = bf16[128,136,128]{2,1,0:T(8,128)(2,1)} async-done(((bf16[128,136,128]{2,1,0:T(8,128)(2,1)}), bf16[128,136,128]{2,1,0:T(8,128)(2,1)}, u32[]{:S(2)}, u32[]{:S(2)}) %all-to-all-start) | async-done | bytes 4456480 | tf_op jit(solution)/shard_map/all_to_all | solution.py:584
  123.1 7.0 %gather.7.agg = bf16[4096,128]{1,0:T(8,128)(2,1)} custom-call(s32[96]{0:T(128)} %get-tuple-element.31.row, s32[96]{0:T(128)} %get-tuple-element.28.owner_a, s32[96]{0:T(128)} %get-tuple-element.27.owner_b, s32[1]{0:T(128)} %bitcast.1.n_duos, bf16[96,128,256]{2,1,0:T(8,128)(2,1)} %get-tuple-element.14.pairs, bf16[128,136,128]{2,1,0:T(8,128)(2,1)} %all-to-all-done.incoming, ...), custom_call_target="tpu_custom_call" | custom-call | tf_op jit(solution)/shard_map/gather/pallas_call | solution.py:237
  130.3 2.9 collective-permute-done.3.agg_peer
  134.2 10.6 %middle.1 = (bf16[4096,128]{1,0:T(8,128)(2,1)}, bf16[4096,256]{1,0:T(8,128)(2,1)}, bf16[128,136,128]{2,1,0:T(8,128)(2,1)}) custom-call(s32[160]{0:T(256)} %get-tuple-element.26.order_row, s32[160]{0:T(256)} %get-tuple-element.25.order_owner, s32[1]{0:T(128)} %copy.16.count, bf16[4096,128]{1,0:T(8,128)(2,1)} %feat.5, bf16[4096,128]{1,0:T(8,128)(2,1)} %copy-done.7, ...), custom_call_target="tpu_custom_call" | custom-call | tf_op jit(solution)/shard_map/middle/pallas_call | solution.py:386
  144.8 12.8 %all-to-all-start.1 = ((bf16[128,136,128]{2,1,0:T(8,128)(2,1)}), bf16[128,136,128]{2,1,0:T(8,128)(2,1)}, u32[]{:S(2)}, u32[]{:S(2)}) async-start(bf16[128,136,128]{2,1,0:T(8,128)(2,1)} %get-tuple-element.18), calls=%async_computation.1 | async-start | bytes 8912896 | tf_op jit(solution)/shard_map/all_to_all | solution.py:584
  157.7 1.6 copy-done.6
  159.3 3.4 %side.1 = (f32[4,4,32,128]{3,2,1,0:T(8,128)S(1)}, f32[4096,128]{1,0:T(8,128)S(1)}) custom-call(s32[2]{0:T(128)S(1)} %pad_add_fusion.place, bf16[4096,128]{1,0:T(8,128)(2,1)S(1)} %copy-done.1, bf16[4096,128]{1,0:T(8,128)(2,1)S(1)} %copy-done, bf16[4096,256]{1,0:T(8,128)(2,1)S(1)} %copy-done.6, bf16[128,256]{1,0:T(8,128)(2,1)S(1)} %get-tuple-element.47.own_w), custom_call_target="tpu_custom_call" | custom-call | tf_op jit(solution)/shard_map/side/pallas_call | solution.py:455
  162.7 1.3 copy-done.5
  164.0 2.8 collective-permute-start.6
  168.5 4.9 %collective-permute-done.6 = f32[4,32,128]{2,1,0:T(8,128)S(1)} collective-permute-done((f32[4,32,128]{2,1,0:T(8,128)S(1)}, f32[4,32,128]{2,1,0:T(8,128)S(1)}, u32[]{:S(2)}, u32[]{:S(2)}) %collective-permute-start.6) | collective-permute-done | bytes 65568 | tf_op jit(solution)/shard_map/ppermute | solution.py:602
  173.5 2.6 collective-permute-done.4
  176.2 4.2 %collective-permute-start.9 = (f32[32,128]{1,0:T(8,128)S(1)}, f32[32,128]{1,0:T(8,128)S(1)}, u32[]{:S(2)}, u32[]{:S(2)}) collective-permute-start(f32[32,128]{1,0:T(8,128)S(1)} %get-tuple-element.54), channel_id=1, source_target_pairs={{0,24},{2,26},{4,28},{6,30},{8,0},{10,2},{12,4},{14,6},{16,8},{18,... | collective-permute-start | bytes 49160 | tf_op jit(solution)/shard_map/ppermute | solution.py:602
  180.4 1.6 collective-permute-start.7
  181.9 3.9 %collective-permute-done.8 = f32[32,128]{1,0:T(8,128)S(1)} collective-permute-done((f32[32,128]{1,0:T(8,128)S(1)}, f32[32,128]{1,0:T(8,128)S(1)}, u32[]{:S(2)}, u32[]{:S(2)}) %collective-permute-start.8) | collective-permute-done | bytes 16416 | tf_op jit(solution)/shard_map/ppermute | solution.py:602
  185.8 2.9 %collective-permute-start.16 = (f32[32,128]{1,0:T(8,128)S(1)}, f32[32,128]{1,0:T(8,128)S(1)}, u32[]{:S(2)}, u32[]{:S(2)}) collective-permute-start(f32[32,128]{1,0:T(8,128)S(1)} %fusion.16), channel_id=1, source_target_pairs={{0,224},{2,226},{4,228},{6,230},{8,232},{10,234},{12,236},{14,238}... | collective-permute-start | bytes 49160 | tf_op jit(solution)/shard_map/ppermute | solution.py:602
  189.7 4.7 %collective-permute-start.14 = (f32[32,128]{1,0:T(8,128)S(1)}, f32[32,128]{1,0:T(8,128)S(1)}, u32[]{:S(2)}, u32[]{:S(2)}) collective-permute-start(f32[32,128]{1,0:T(8,128)S(1)} %fusion.16), channel_id=1, source_target_pairs={{0,160},{2,162},{4,164},{6,166},{8,168},{10,170},{12,172},{14,174}... | collective-permute-start | bytes 49160 | tf_op jit(solution)/shard_map/ppermute | solution.py:602
  194.4 1.5 collective-permute-start.13
  195.9 2.4 collective-permute-start.12
  198.3 59.2 %collective-permute-done.16 = f32[32,128]{1,0:T(8,128)S(1)} collective-permute-done((f32[32,128]{1,0:T(8,128)S(1)}, f32[32,128]{1,0:T(8,128)S(1)}, u32[]{:S(2)}, u32[]{:S(2)}) %collective-permute-start.16) | collective-permute-done | bytes 16416 | tf_op jit(solution)/shard_map/ppermute | solution.py:602
  257.5 3.0 %collective-permute-start.11 = (f32[32,128]{1,0:T(8,128)S(1)}, f32[32,128]{1,0:T(8,128)S(1)}, u32[]{:S(2)}, u32[]{:S(2)}) collective-permute-start(f32[32,128]{1,0:T(8,128)S(1)} %fusion.16), channel_id=1, source_target_pairs={{0,64},{2,66},{4,68},{6,70},{8,72},{10,74},{12,76},{14,78},{16,80}... | collective-permute-start | bytes 49160 | tf_op jit(solution)/shard_map/ppermute | solution.py:602
  260.4 1.4 collective-permute-start.10
  262.1 2.0 collective-permute-done.10
  265.0 1.8 collective-permute-start.18
  266.8 2.3 collective-permute-start.17
  269.1 7.1 %finish.1 = (f32[32,128,128]{2,1,0:T(8,128)}, f32[32,128]{1,0:T(8,128)}) custom-call(s32[128]{0:T(128)} %send.3, s32[2]{0:T(128)} %hubs.3, bf16[128,136,128]{2,1,0:T(8,128)(2,1)} %all-to-all-done.1.returned, f32[32,128,128]{2,1,0:T(8,128)} %bitcast.48, f32[32,128]{1,0:T(8,128)} %copy-done.12), custom_call_target="tpu_custom_call" | custom-call | tf_op jit(solution)/shard_map/finish/pallas_call | solution.py:517
  277.0 3.1 %collective-permute-start.21 = (f32[4,32,128]{2,1,0:T(8,128)S(1)}, f32[4,32,128]{2,1,0:T(8,128)S(1)}, u32[]{:S(2)}, u32[]{:S(2)}) collective-permute-start(f32[4,32,128]{2,1,0:T(8,128)S(1)} %get-tuple-element.53), channel_id=1, source_target_pairs={{0,4},{2,6},{4,0},{6,2},{8,12},{10,14},{12,8},{14,10},{16,20},{18,... | collective-permute-start | bytes 196616 | tf_op jit(solution)/shard_map/ppermute | solution.py:602
  280.6 2.7 collective-permute-start.22
  283.3 2.2 collective-permute-done.20
  (96 shorter events, 13.6 us)
Async XLA Ops:
  0.6 24.4 %collective-permute-start = (bf16[4096,128]{1,0:T(8,128)(2,1)}, bf16[4096,128]{1,0:T(8,128)(2,1)S(1)}, u32[]{:S(2)}, u32[]{:S(2)}) collective-permute-start(bf16[4096,128]{1,0:T(8,128)(2,1)} %feat.5), channel_id=1, source_target_pairs={{0,1},{1,0},{2,3},{3,2},{4,5},{5,4},{6,7},{7,6},{8,9},{9,8},{10,11... | collective-permute-start | bytes 3145736 | tf_op jit(solution)/shard_map/ppermute | solution.py:588
  4.7 16.1 %copy-start.14 = (bf16[128,256]{1,0:T(8,128)(2,1)S(1)}, bf16[128,256]{1,0:T(8,128)(2,1)}, u32[]{:S(2)}) copy-start(bf16[128,256]{1,0:T(8,128)(2,1)} %param.13) | copy-start | bytes 196612
  4.7 17.4 %copy-start.10 = (s32[160]{0:T(256)S(1)}, s32[160]{0:T(256)}, u32[]{:S(2)}) copy-start(s32[160]{0:T(256)} %row.1) | copy-start | bytes 1924
  4.8 17.5 %copy-start.15 = (s32[160]{0:T(256)S(1)}, s32[160]{0:T(256)}, u32[]{:S(2)}) copy-start(s32[160]{0:T(256)} %param.16) | copy-start | bytes 1924
  4.8 20.3 %copy-start.2 = (bf16[4096,256]{1,0:T(8,128)(2,1)S(1)}, bf16[4096,256]{1,0:T(8,128)(2,1)}, u32[]{:S(2)}) copy-start(bf16[4096,256]{1,0:T(8,128)(2,1)} %panel.5) | copy-start | bytes 6291460
  4.8 118.3 %all-to-all-start = ((bf16[128,136,128]{2,1,0:T(8,128)(2,1)}), bf16[128,136,128]{2,1,0:T(8,128)(2,1)}, u32[]{:S(2)}, u32[]{:S(2)}) async-start(bf16[128,136,128]{2,1,0:T(8,128)(2,1)} %pack.1), calls=%async_computation | async-start | bytes 8912896 | tf_op jit(solution)/shard_map/all_to_all | solution.py:584
  20.9 4.1 %collective-permute-start.1 = (bf16[256,256]{1,0:T(8,128)(2,1)S(1)}, bf16[256,256]{1,0:T(8,128)(2,1)S(1)}, u32[]{:S(2)}, u32[]{:S(2)}) collective-permute-start(bf16[256,256]{1,0:T(8,128)(2,1)S(1)} %maximum_select_fusion), channel_id=1, source_target_pairs={{0,1},{1,0},{2,3},{3,2},{4,5},{5,4},{6,7},{7,6},{8,9},{9,8},{10,11... | collective-permute-start | bytes 393224 | tf_op jit(solution)/shard_map/ppermute | solution.py:588
  21.0 4.1 %collective-permute-start.2 = (bf16[4096,128]{1,0:T(8,128)(2,1)}, bf16[4096,128]{1,0:T(8,128)(2,1)}, u32[]{:S(2)}, u32[]{:S(2)}) collective-permute-start(bf16[4096,128]{1,0:T(8,128)(2,1)} %cot.1), channel_id=1, source_target_pairs={{0,1},{1,0},{2,3},{3,2},{4,5},{5,4},{6,7},{7,6},{8,9},{9,8},{10,11... | collective-permute-start | bytes 3145736 | tf_op jit(solution)/shard_map/ppermute | solution.py:588
  25.0 22.0 %copy-start.8 = (bf16[256,256]{1,0:T(8,128)(2,1)}, bf16[256,256]{1,0:T(8,128)(2,1)S(1)}, u32[]{:S(2)}) copy-start(bf16[256,256]{1,0:T(8,128)(2,1)S(1)} %get-tuple-element.57.rest_1_.nbr_w) | copy-start | bytes 393220
  25.0 22.0 %copy-start.9 = (bf16[256,256]{1,0:T(8,128)(2,1)}, bf16[256,256]{1,0:T(8,128)(2,1)S(1)}, u32[]{:S(2)}) copy-start(bf16[256,256]{1,0:T(8,128)(2,1)S(1)} %get-tuple-element.58.rest_0_.own_w) | copy-start | bytes 393220
  25.1 22.0 %copy-start.7 = (bf16[4096,128]{1,0:T(8,128)(2,1)}, bf16[4096,128]{1,0:T(8,128)(2,1)S(1)}, u32[]{:S(2)}) copy-start(bf16[4096,128]{1,0:T(8,128)(2,1)S(1)} %collective-permute-done.rest_2_.feat_peer) | copy-start | bytes 3145732
  130.0 3.1 %collective-permute-start.3 = (bf16[4096,128]{1,0:T(8,128)(2,1)}, bf16[4096,128]{1,0:T(8,128)(2,1)S(1)}, u32[]{:S(2)}, u32[]{:S(2)}) collective-permute-start(bf16[4096,128]{1,0:T(8,128)(2,1)} %gather.7.agg), channel_id=1, source_target_pairs={{0,1},{1,0},{2,3},{3,2},{4,5},{5,4},{6,7},{7,6},{8,9},{9,8},{10,11... | collective-permute-start | bytes 3145736 | tf_op jit(solution)/shard_map/ppermute | solution.py:588
  144.8 124.3 %all-to-all-start.1 = ((bf16[128,136,128]{2,1,0:T(8,128)(2,1)}), bf16[128,136,128]{2,1,0:T(8,128)(2,1)}, u32[]{:S(2)}, u32[]{:S(2)}) async-start(bf16[128,136,128]{2,1,0:T(8,128)(2,1)} %get-tuple-element.18), calls=%async_computation.1 | async-start | bytes 8912896 | tf_op jit(solution)/shard_map/all_to_all | solution.py:584
  164.0 9.4 %collective-permute-start.6 = (f32[4,32,128]{2,1,0:T(8,128)S(1)}, f32[4,32,128]{2,1,0:T(8,128)S(1)}, u32[]{:S(2)}, u32[]{:S(2)}) collective-permute-start(f32[4,32,128]{2,1,0:T(8,128)S(1)} %get-tuple-element.43), channel_id=1, source_target_pairs={{0,6},{2,0},{4,2},{6,4},{8,14},{10,8},{12,10},{14,12},{16,22},{18,... | collective-permute-start | bytes 196616 | tf_op jit(solution)/shard_map/ppermute | solution.py:602
  166.8 6.7 %collective-permute-start.5 = (f32[4,32,128]{2,1,0:T(8,128)S(1)}, f32[4,32,128]{2,1,0:T(8,128)S(1)}, u32[]{:S(2)}, u32[]{:S(2)}) collective-permute-start(f32[4,32,128]{2,1,0:T(8,128)S(1)} %get-tuple-element.44), channel_id=1, source_target_pairs={{0,4},{2,6},{4,0},{6,2},{8,12},{10,14},{12,8},{14,10},{16,20},{18,... | collective-permute-start | bytes 196616 | tf_op jit(solution)/shard_map/ppermute | solution.py:602
  167.7 8.5 %collective-permute-start.4 = (f32[4,32,128]{2,1,0:T(8,128)S(1)}, f32[4,32,128]{2,1,0:T(8,128)S(1)}, u32[]{:S(2)}, u32[]{:S(2)}) collective-permute-start(f32[4,32,128]{2,1,0:T(8,128)S(1)} %get-tuple-element.45), channel_id=1, source_target_pairs={{0,2},{2,4},{4,6},{6,0},{8,10},{10,12},{12,14},{14,8},{16,18},{18,... | collective-permute-start | bytes 196616 | tf_op jit(solution)/shard_map/ppermute | solution.py:602
  176.2 5.8 %collective-permute-start.9 = (f32[32,128]{1,0:T(8,128)S(1)}, f32[32,128]{1,0:T(8,128)S(1)}, u32[]{:S(2)}, u32[]{:S(2)}) collective-permute-start(f32[32,128]{1,0:T(8,128)S(1)} %get-tuple-element.54), channel_id=1, source_target_pairs={{0,24},{2,26},{4,28},{6,30},{8,0},{10,2},{12,4},{14,6},{16,8},{18,... | collective-permute-start | bytes 49160 | tf_op jit(solution)/shard_map/ppermute | solution.py:602
  180.4 5.5 %collective-permute-start.8 = (f32[32,128]{1,0:T(8,128)S(1)}, f32[32,128]{1,0:T(8,128)S(1)}, u32[]{:S(2)}, u32[]{:S(2)}) collective-permute-start(f32[32,128]{1,0:T(8,128)S(1)} %get-tuple-element.55), channel_id=1, source_target_pairs={{0,16},{2,18},{4,20},{6,22},{8,24},{10,26},{12,28},{14,30},{16,0},... | collective-permute-start | bytes 49160 | tf_op jit(solution)/shard_map/ppermute | solution.py:602
  180.4 5.5 %collective-permute-start.7 = (f32[32,128]{1,0:T(8,128)S(1)}, f32[32,128]{1,0:T(8,128)S(1)}, u32[]{:S(2)}, u32[]{:S(2)}) collective-permute-start(f32[32,128]{1,0:T(8,128)S(1)} %get-tuple-element.56), channel_id=1, source_target_pairs={{0,8},{2,10},{4,12},{6,14},{8,16},{10,18},{12,20},{14,22},{16,24},... | collective-permute-start | bytes 49160 | tf_op jit(solution)/shard_map/ppermute | solution.py:602
  185.8 71.6 %collective-permute-start.16 = (f32[32,128]{1,0:T(8,128)S(1)}, f32[32,128]{1,0:T(8,128)S(1)}, u32[]{:S(2)}, u32[]{:S(2)}) collective-permute-start(f32[32,128]{1,0:T(8,128)S(1)} %fusion.16), channel_id=1, source_target_pairs={{0,224},{2,226},{4,228},{6,230},{8,232},{10,234},{12,236},{14,238}... | collective-permute-start | bytes 49160 | tf_op jit(solution)/shard_map/ppermute | solution.py:602
  188.8 71.6 %collective-permute-start.15 = (f32[32,128]{1,0:T(8,128)S(1)}, f32[32,128]{1,0:T(8,128)S(1)}, u32[]{:S(2)}, u32[]{:S(2)}) collective-permute-start(f32[32,128]{1,0:T(8,128)S(1)} %fusion.16), channel_id=1, source_target_pairs={{0,192},{2,194},{4,196},{6,198},{8,200},{10,202},{12,204},{14,206}... | collective-permute-start | bytes 49160 | tf_op jit(solution)/shard_map/ppermute | solution.py:602
  189.7 72.2 %collective-permute-start.14 = (f32[32,128]{1,0:T(8,128)S(1)}, f32[32,128]{1,0:T(8,128)S(1)}, u32[]{:S(2)}, u32[]{:S(2)}) collective-permute-start(f32[32,128]{1,0:T(8,128)S(1)} %fusion.16), channel_id=1, source_target_pairs={{0,160},{2,162},{4,164},{6,166},{8,168},{10,170},{12,172},{14,174}... | collective-permute-start | bytes 49160 | tf_op jit(solution)/shard_map/ppermute | solution.py:602
  194.4 67.5 %collective-permute-start.13 = (f32[32,128]{1,0:T(8,128)S(1)}, f32[32,128]{1,0:T(8,128)S(1)}, u32[]{:S(2)}, u32[]{:S(2)}) collective-permute-start(f32[32,128]{1,0:T(8,128)S(1)} %fusion.16), channel_id=1, source_target_pairs={{0,128},{2,130},{4,132},{6,134},{8,136},{10,138},{12,140},{14,142}... | collective-permute-start | bytes 49160 | tf_op jit(solution)/shard_map/ppermute | solution.py:602
  195.9 66.0 %collective-permute-start.12 = (f32[32,128]{1,0:T(8,128)S(1)}, f32[32,128]{1,0:T(8,128)S(1)}, u32[]{:S(2)}, u32[]{:S(2)}) collective-permute-start(f32[32,128]{1,0:T(8,128)S(1)} %fusion.16), channel_id=1, source_target_pairs={{0,96},{2,98},{4,100},{6,102},{8,104},{10,106},{12,108},{14,110},{... | collective-permute-start | bytes 49160 | tf_op jit(solution)/shard_map/ppermute | solution.py:602
  257.5 4.7 %collective-permute-start.11 = (f32[32,128]{1,0:T(8,128)S(1)}, f32[32,128]{1,0:T(8,128)S(1)}, u32[]{:S(2)}, u32[]{:S(2)}) collective-permute-start(f32[32,128]{1,0:T(8,128)S(1)} %fusion.16), channel_id=1, source_target_pairs={{0,64},{2,66},{4,68},{6,70},{8,72},{10,74},{12,76},{14,78},{16,80}... | collective-permute-start | bytes 49160 | tf_op jit(solution)/shard_map/ppermute | solution.py:602
  260.4 3.7 %collective-permute-start.10 = (f32[32,128]{1,0:T(8,128)S(1)}, f32[32,128]{1,0:T(8,128)S(1)}, u32[]{:S(2)}, u32[]{:S(2)}) collective-permute-start(f32[32,128]{1,0:T(8,128)S(1)} %fusion.16), channel_id=1, source_target_pairs={{0,32},{2,34},{4,36},{6,38},{8,40},{10,42},{12,44},{14,46},{16,48}... | collective-permute-start | bytes 49160 | tf_op jit(solution)/shard_map/ppermute | solution.py:602
  264.2 12.0 %collective-permute-start.19 = (f32[32,128]{1,0:T(8,128)S(1)}, f32[32,128]{1,0:T(8,128)S(1)}, u32[]{:S(2)}, u32[]{:S(2)}) collective-permute-start(f32[32,128]{1,0:T(8,128)S(1)} %add_add_fusion.grads), channel_id=1, source_target_pairs={{0,24},{2,26},{4,28},{6,30},{8,0},{10,2},{12,4},{14,6},{16,8},{18,... | collective-permute-start | bytes 49160 | tf_op jit(solution)/shard_map/ppermute | solution.py:602
  265.0 11.2 %collective-permute-start.18 = (f32[32,128]{1,0:T(8,128)S(1)}, f32[32,128]{1,0:T(8,128)S(1)}, u32[]{:S(2)}, u32[]{:S(2)}) collective-permute-start(f32[32,128]{1,0:T(8,128)S(1)} %add_add_fusion.grads), channel_id=1, source_target_pairs={{0,16},{2,18},{4,20},{6,22},{8,24},{10,26},{12,28},{14,30},{16,0},... | collective-permute-start | bytes 49160 | tf_op jit(solution)/shard_map/ppermute | solution.py:602
  266.8 9.4 %collective-permute-start.17 = (f32[32,128]{1,0:T(8,128)S(1)}, f32[32,128]{1,0:T(8,128)S(1)}, u32[]{:S(2)}, u32[]{:S(2)}) collective-permute-start(f32[32,128]{1,0:T(8,128)S(1)} %add_add_fusion.grads), channel_id=1, source_target_pairs={{0,8},{2,10},{4,12},{6,14},{8,16},{10,18},{12,20},{14,22},{16,24},... | collective-permute-start | bytes 49160 | tf_op jit(solution)/shard_map/ppermute | solution.py:602
  277.0 6.3 %collective-permute-start.21 = (f32[4,32,128]{2,1,0:T(8,128)S(1)}, f32[4,32,128]{2,1,0:T(8,128)S(1)}, u32[]{:S(2)}, u32[]{:S(2)}) collective-permute-start(f32[4,32,128]{2,1,0:T(8,128)S(1)} %get-tuple-element.53), channel_id=1, source_target_pairs={{0,4},{2,6},{4,0},{6,2},{8,12},{10,14},{12,8},{14,10},{16,20},{18,... | collective-permute-start | bytes 196616 | tf_op jit(solution)/shard_map/ppermute | solution.py:602
  280.0 5.5 %collective-permute-start.20 = (f32[4,32,128]{2,1,0:T(8,128)S(1)}, f32[4,32,128]{2,1,0:T(8,128)S(1)}, u32[]{:S(2)}, u32[]{:S(2)}) collective-permute-start(f32[4,32,128]{2,1,0:T(8,128)S(1)} %get-tuple-element.53), channel_id=1, source_target_pairs={{0,2},{2,4},{4,6},{6,0},{8,10},{10,12},{12,14},{14,8},{16,18},{18,... | collective-permute-start | bytes 196616 | tf_op jit(solution)/shard_map/ppermute | solution.py:602
  280.6 4.9 %collective-permute-start.22 = (f32[4,32,128]{2,1,0:T(8,128)S(1)}, f32[4,32,128]{2,1,0:T(8,128)S(1)}, u32[]{:S(2)}, u32[]{:S(2)}) collective-permute-start(f32[4,32,128]{2,1,0:T(8,128)S(1)} %get-tuple-element.53), channel_id=1, source_target_pairs={{0,6},{2,0},{4,2},{6,4},{8,14},{10,8},{12,10},{14,12},{16,22},{18,... | collective-permute-start | bytes 196616 | tf_op jit(solution)/shard_map/ppermute | solution.py:602
  (9 other events, 54.4 us)

commit v4 on v3

--- a/solution.py
+++ b/solution.py
@@ -29,6 +29,8 @@
 
 ANY = pl.BlockSpec(memory_space=pl.ANY)
 HBM = pl.BlockSpec(memory_space=pltpu.HBM)
+VMEM = pl.BlockSpec(memory_space=pltpu.VMEM)
+SMEM = pl.BlockSpec(memory_space=pltpu.SMEM)
 
 
 def own_copies(mib):
@@ -422,12 +424,10 @@
     )
 
 
-def side_kernel(place, feat, agg, slopes, own_w, grads, direct, acc):
+def side_kernel(where, feat, agg, slopes, grads, acc):
     step, steps = pl.program_id(0), pl.num_programs(0)
     half = feat.shape[1]
-    s = slopes[...]
-    direct[...] = dot(s, own_w[...], NT)
-    part = dot(jnp.concatenate([feat[...], agg[...]], axis=1), s, TN)
+    part = dot(jnp.concatenate([feat[...], agg[...]], axis=1), slopes[...], TN)
 
     @pl.when(step == 0)
     def _():
@@ -439,81 +439,92 @@
 
     @pl.when(step == steps - 1)
     def _():
+        y, x = where[0] % 4, (where[0] // 4) % 4
         n = half // 4
         for c in range(4):
             for r in range(4):
-                grads[(c + 4 - place[0]) % 4, (r + 4 - place[1]) % 4] = acc[
+                grads[jnp.bitwise_xor(c, y), jnp.bitwise_xor(r, x)] = acc[
                     (c // 2) * half + r * n : (c // 2) * half + (r + 1) * n,
                     (c % 2) * half : (c % 2 + 1) * half,
                 ]
 
 
-def side(place, feat, agg, slopes, own_w):
+def side(where, feat, agg, slopes):
     rows, half = feat.shape
-    block = 512
+    block = 1024
     by_row = lambda width: pl.BlockSpec((block, width), lambda g, *_: (g, 0))
     return pl.pallas_call(
         side_kernel,
         name="side",
-        out_shape=(
-            jax.ShapeDtypeStruct((4, 4, half // 4, half), F32),
-            jax.ShapeDtypeStruct((rows, half), F32),
-        ),
+        out_shape=jax.ShapeDtypeStruct((4, 4, half // 4, half), F32),
         grid_spec=pltpu.PrefetchScalarGridSpec(
             num_scalar_prefetch=1,
             grid=(rows // block,),
-            in_specs=[
-                by_row(half),
-                by_row(half),
-                by_row(2 * half),
-                pl.BlockSpec(own_w.shape, lambda g, *_: (0, 0)),
-            ],
-            out_specs=(
-                pl.BlockSpec((4, 4, half // 4, half), lambda g, *_: (0, 0, 0, 0)),
-                by_row(half),
-            ),
+            in_specs=[by_row(half), by_row(half), by_row(2 * half)],
+            out_specs=pl.BlockSpec((4, 4, half // 4, half), lambda g, *_: (0, 0, 0, 0)),
             scratch_shapes=[pltpu.VMEM((2 * half, 2 * half), F32)],
         ),
-        compiler_params=params(24, 1),
-    )(place, feat, agg, slopes, own_w)
-
-
-def finish_kernel(send, hubs, returned, direct, grads, out, grads_out, acc, landed, sems, part_sems):
+        compiler_params=params(32, 1),
+    )(where, feat, agg, slopes)
+
+
+def direct_kernel(slopes, own_w, passed, direct, passed_out):
+    passed_out[...] = passed[...]
+    block = 512
+    for t in range(slopes.shape[0] // block):
+        at = pl.ds(t * block, block)
+        direct[at, :] = dot(slopes[at, :], own_w[...], NT)
+
+
+def direct_part(slopes, own_w, passed):
+    return pl.pallas_call(
+        direct_kernel,
+        name="direct",
+        out_shape=(
+            jax.ShapeDtypeStruct((slopes.shape[0], own_w.shape[0]), F32),
+            jax.ShapeDtypeStruct(passed.shape, passed.dtype),
+        ),
+        in_specs=[VMEM] * 3,
+        out_specs=(VMEM, VMEM),
+        compiler_params=own_copies(8),
+    )(slopes, own_w, passed)
+
+
+def finish_kernel(
+    send, hubs, returned, direct, grads, out, grads_out, acc, landed, sems, part_sems
+):
     parts, height, half = landed.shape
     edge = acc.shape[1]
     copy = pltpu.make_async_copy
-    steps = 8
+    steps = 4
     group = parts // steps
     arrivals = [
         copy(returned.at[pl.ds(g * group, group)], landed.at[pl.ds(g * group, group)], part_sems.at[g])
         for g in range(steps)
     ]
-    start = copy(direct, acc, sems.at[0])
-    start.start()
-    grads_out[...] = grads[...]
     for c in arrivals:
         c.start()
-    start.wait()
-    total = jnp.zeros((8, half), F32)
+    grads_out[...] = grads[...]
+    acc[...] = direct[...]
+    share = jnp.zeros((8, half), F32)
     for g in range(steps):
         arrivals[g].wait()
         for i in range(group):
             p = g * group + i
             acc[send[p]] += landed[p, :edge, :].astype(F32)
-            total = total + landed[p, edge:, :].astype(F32)
+            share = share + landed[p, edge:, :].astype(F32)
     for j in range(2):
         row = hubs[j]
         tile, inside = row // edge, row % edge
         base = pl.multiple_of((inside // 8) * 8, 8)
         here = lax.broadcasted_iota(jnp.int32, (8, half), 0) == inside - base
-        acc[tile, pl.ds(base, 8), :] += jnp.where(here, total[j : j + 1, :], 0.0)
-    end = copy(acc, out, sems.at[1])
+        acc[tile, pl.ds(base, 8), :] += jnp.where(here, share[j : j + 1, :], 0.0)
+    end = copy(acc, out, sems.at[0])
     end.start()
     end.wait()
 
 
 def finish(send_tile, hub_rows, returned, direct, grads):
-    small = pl.BlockSpec(grads.shape, lambda g, *_: (0, 0))
     return pl.pallas_call(
         finish_kernel,
         name="finish",
@@ -521,20 +532,44 @@
             jax.ShapeDtypeStruct(direct.shape, F32),
             jax.ShapeDtypeStruct(grads.shape, F32),
         ),
-        grid_spec=pltpu.PrefetchScalarGridSpec(
-            num_scalar_prefetch=2,
-            grid=(1,),
-            in_specs=[ANY, ANY, small],
-            out_specs=(HBM, small),
-            scratch_shapes=[
-                pltpu.VMEM(direct.shape, F32),
-                pltpu.VMEM(returned.shape, BF16),
-                pltpu.SemaphoreType.DMA((2,)),
-                pltpu.SemaphoreType.DMA((8,)),
-            ],
-        ),
-        compiler_params=own_copies(58),
+        in_specs=[SMEM, SMEM, ANY, VMEM, VMEM],
+        out_specs=(HBM, VMEM),
+        scratch_shapes=[
+            pltpu.VMEM(direct.shape, F32),
+            pltpu.VMEM(returned.shape, BF16),
+            pltpu.SemaphoreType.DMA((1,)),
+            pltpu.SemaphoreType.DMA((4,)),
+        ],
+        compiler_params=own_copies(16),
     )(send_tile, hub_rows, returned, direct, grads)
+
+
+def place_kernel(factor, where, own, one, two, three, self_grad, neighbor_grad, blocks):
+    for m, group in enumerate((own, one, two, three)):
+        blocks[m] = group[...]
+    y, x, core = where[0] % 4, (where[0] // 4) % 4, where[1]
+    n, half = blocks.shape[2:]
+    for j, out in enumerate((self_grad, neighbor_grad)):
+        for c in range(2):
+            column = 2 * j + jnp.bitwise_xor(c, core)
+            for r in range(4):
+                out[r * n : (r + 1) * n, c * half : (c + 1) * half] = (
+                    blocks[jnp.bitwise_xor(column, y), jnp.bitwise_xor(r, x)] * factor
+                )
+
+
+def put_in_place(where, groups, factor):
+    four, n, half = groups[0].shape
+    out = jax.ShapeDtypeStruct((four * n, 2 * half), F32)
+    return pl.pallas_call(
+        lambda *refs: place_kernel(factor, *refs),
+        name="place",
+        out_shape=(out, out),
+        in_specs=[SMEM] + [VMEM] * 4,
+        out_specs=(VMEM, VMEM),
+        scratch_shapes=[pltpu.VMEM((4, four, n, half), F32)],
+        compiler_params=own_copies(8),
+    )(where, *groups)
 
 
 def plan(tile_row, tile_owner, tile_count, tiles, parts):
@@ -588,28 +623,18 @@
     return lax.ppermute(block, "feat", [(0, 1), (1, 0)])
 
 
-def move(block, axis, amount):
-    def target(d):
-        z, x, y = d // 16, (d // 4) % 4, d % 4
-        if axis == "y":
-            y = (y + amount) % 4
-        elif axis == "x":
-            x = (x + amount) % 4
-        else:
-            z = z ^ amount
-        return (z * 4 + x) * 4 + y
-
-    return lax.ppermute(block, "dom", [(d, target(d)) for d in range(lax.axis_size("dom"))])
-
-
-def add_up(blocks):
-    for axis in ("y", "x"):
-        moved = [move(blocks[i], axis, i) for i in (1, 2, 3)]
-        blocks = (blocks[0] + moved[0]) + (moved[1] + moved[2])
-    lines = [blocks] + [move(blocks, "z", bits) for bits in range(1, 8)]
-    while len(lines) > 1:
-        lines = [a + b for a, b in zip(lines[::2], lines[1::2])]
-    return lines[0]
+def move(block, axis, bits):
+    shift = {"z": 4, "x": 2, "y": 0}[axis]
+    pairs = [(d, d ^ (bits << shift)) for d in range(lax.axis_size("dom"))]
+    return lax.ppermute(block, "dom", pairs)
+
+
+def moved_three(blocks, axis):
+    return [move(blocks[i], axis, i) for i in (1, 2, 3)]
+
+
+def total(own, near):
+    return (own + near[0]) + (near[1] + near[2])
 
 
 def shards(
@@ -662,26 +687,22 @@
     )
     returned = exchange(terms)
 
-    dom = lax.axis_index("dom")
-    place_y, place_x = dom % 4, (dom // 4) % 4
-    grads, direct = side(
-        jnp.stack([place_y, place_x]).astype(jnp.int32), features, aggregate, slopes, own_w[:half]
-    )
-    grads = add_up(grads)
-    from_x = [move(grads, "x", i) for i in (1, 2, 3)]
+    where = jnp.stack([lax.axis_index("dom").astype(jnp.int32), core.astype(jnp.int32)])
+    grads = side(where, features, aggregate, slopes)
+    grads = total(grads[0], moved_three(grads, "y"))
+    direct, grads = direct_part(slopes, own_w[:half], grads)
+    grads = total(grads[0], moved_three(grads, "x"))
+    grads = total(grads, [move(grads, "z", i) for i in (1, 2, 3)])
+    grads = grads + move(grads, "z", 4)
+    grads = jnp.stack([grads] + [move(grads, "x", i) for i in (1, 2, 3)])
+    near = [move(grads, "y", i) for i in (1, 2, 3)]
     input_grad, grads = finish(
         send_tile, hub_rows, returned, direct.reshape(tiles_dev, tile_edge, half), grads
     )
     input_grad = input_grad.reshape(rows_dev, half)
-    grads = jnp.stack([grads] + from_x)
-    grads = jnp.stack([grads] + [move(grads, "y", i) for i in (1, 2, 3)])
-    c = jnp.arange(4) ^ core
-    r = jnp.arange(4)
-    index = (((place_y - c) % 4)[:, None] * 4 + ((place_x - r) % 4)[None, :]).reshape(16)
-    grads = grads.reshape(16, half // 4, half)[index].reshape(4, half, half)
-    grads = grads * (1.0 / math.sqrt(rows_dev * dom_size))
-    self_grad = jnp.concatenate([grads[0], grads[1]], axis=1)
-    neighbor_grad = jnp.concatenate([grads[2], grads[3]], axis=1)
+    self_grad, neighbor_grad = put_in_place(
+        where, [grads] + near, 1.0 / math.sqrt(rows_dev * dom_size)
+    )
     return (layer_out, self_grad, neighbor_grad, input_grad)
 
 

time: 288 us -> 281 us (0.976)
  starting transfers between devices: 67.9 us -> 54 us
  waiting for transfers between devices: 150 us -> 160 us
    ppermute x19 -> x16, starting transfers between devices: 38.2 us -> 27.7 us  [move(): return lax.ppermute(block, 'dom', pairs)]
    ppermute x19 -> x16, waiting for transfers between devices: 75.1 us -> 84.6 us  [move(): return lax.ppermute(block, 'dom', pairs)]
    all_to_all x2, starting transfers between devices: 28.8 us -> 25.4 us  [exchange(): return lax.all_to_all(block, 'dom', split_axis=0, concat_axis=0, tiled=True)]
  transfers between devices with their start and end apart: 25 -> 22, of which waited for: 10 -> 8; matrix products, arithmetic and copies ran while one was open for 1% -> 1% of each run, Pallas kernels for 13% -> 12%
where the time goes in v4:
time: 281 us; the launch traced here: 278 us
  waiting for transfers between devices  160 us (57%)
  starting transfers between devices  54 us (19%)
  Pallas kernels  53.2 us (19%)
  local copies, waits for them, and re-layouts  6.43 us (2%)
  other arithmetic  2.92 us (1%)
    ppermute x16, waiting for transfers between devices, move(): return lax.ppermute(block, 'dom', pairs)  84.6 us
    all_to_all x2, waiting for transfers between devices, exchange(): return lax.all_to_all(block, 'dom', split_axis=0, concat_axis=0, tiled=True)  72.3 us
    ppermute x16, starting transfers between devices, move(): return lax.ppermute(block, 'dom', pairs)  27.7 us
    all_to_all x2, starting transfers between devices, exchange(): return lax.all_to_all(block, 'dom', split_axis=0, concat_axis=0, tiled=True)  25.4 us
    pallas_call x1, Pallas kernels, prepare(): pl.pallas_call(prepare_kernel, name='prepare', out_shape=(jax.ShapeDtypeS...  21.9 us
    pallas_call x1, Pallas kernels, middle(): pl.pallas_call(middle_kernel, name='middle', out_shape=(jax.ShapeDtypeStr...  11 us
    pallas_call x1, Pallas kernels, gather(): pl.pallas_call(gather_kernel, name='gather', out_shape=jax.ShapeDtypeStru...  7.66 us
    unnamed x33, local copies, waits for them, and re-layouts  6.37 us
  transfers between devices with their start and end apart: 22, of which 8 were waited for; matrix products, arithmetic and copies ran while one was open for 1% of the time, Pallas kernels for 12%

profile of v4, /device:TPU:2, one launch (start us, length us, event | category | flops | bytes accessed | tf_op | source)
XLA Modules:
  0.0 278.1 jit_solution(2431060138005980368)
XLA Ops:
  0.7 4.0 %pack.1 = bf16[128,136,128]{2,1,0:T(8,128)(2,1)} custom-call(s32[128]{0:T(128)} %send.3, s32[2]{0:T(128)} %hubs.3, bf16[4096,128]{1,0:T(8,128)(2,1)} %feat.5), custom_call_target="tpu_custom_call" | custom-call | tf_op jit(solution)/shard_map/pack/pallas_call | solution.py:71
  4.8 16.0 %all-to-all-start = ((bf16[128,136,128]{2,1,0:T(8,128)(2,1)}), bf16[128,136,128]{2,1,0:T(8,128)(2,1)}, u32[]{:S(2)}, u32[]{:S(2)}) async-start(bf16[128,136,128]{2,1,0:T(8,128)(2,1)} %pack.1), calls=%async_computation | async-start | bytes 8912896 | tf_op jit(solution)/shard_map/all_to_all | solution.py:619
  22.5 0.9 fusion.4
  25.1 21.9 %prepare.1 = (f32[4096,128]{1,0:T(8,128)S(1)}, bf16[160,128,128]{2,1,0:T(8,128)(2,1)S(1)}, bf16[96,128,256]{2,1,0:T(8,128)(2,1)}) custom-call(s32[160]{0:T(256)S(1)} %copy-done.9, s32[1]{0:T(128)} %copy.16.count, s32[160]{0:T(256)S(1)} %get-tuple-element.28.order, s32[96]{0:T(128)S(1)} %get-tuple-element.34.first, s32[96]{0:T(128)S(1)} %get-tuple-element.37.second, ...), custom_call_target="tpu_custom_call" | custom-call | flops 60000002048 | bytes 40000000 | tf_op jit(solution)/shard_map/prepare/pallas_call | solution.py:138
  47.1 1.3 copy-done.3
  48.4 2.4 copy-done.5
  50.8 72.3 %all-to-all-done.incoming = bf16[128,136,128]{2,1,0:T(8,128)(2,1)} async-done(((bf16[128,136,128]{2,1,0:T(8,128)(2,1)}), bf16[128,136,128]{2,1,0:T(8,128)(2,1)}, u32[]{:S(2)}, u32[]{:S(2)}) %all-to-all-start) | async-done | bytes 4456480 | tf_op jit(solution)/shard_map/all_to_all | solution.py:619
  123.1 7.7 %gather.1.agg = bf16[4096,128]{1,0:T(8,128)(2,1)} custom-call(s32[96]{0:T(128)} %get-tuple-element.35.row, s32[96]{0:T(128)} %get-tuple-element.32.owner_a, s32[96]{0:T(128)} %get-tuple-element.31.owner_b, s32[1]{0:T(128)} %bitcast.1.n_duos, bf16[96,128,256]{2,1,0:T(8,128)(2,1)} %get-tuple-element.16.pairs, bf16[128,136,128]{2,1,0:T(8,128)(2,1)} %all-to-all-done.incoming, ...), custom_call_target="tpu_custom_call" | custom-call | tf_op jit(solution)/shard_map/gather/pallas_call | solution.py:239
  131.0 2.9 %collective-permute-done.3.agg_peer = bf16[4096,128]{1,0:T(8,128)(2,1)S(1)} collective-permute-done((bf16[4096,128]{1,0:T(8,128)(2,1)}, bf16[4096,128]{1,0:T(8,128)(2,1)S(1)}, u32[]{:S(2)}, u32[]{:S(2)}) %collective-permute-start.3) | collective-permute-done | bytes 1048608 | tf_op jit(solution)/shard_map/ppermute | solution.py:623
  133.9 1.0 copy-done.12
  134.9 11.0 %middle.1 = (bf16[4096,128]{1,0:T(8,128)(2,1)}, bf16[4096,256]{1,0:T(8,128)(2,1)}, bf16[128,136,128]{2,1,0:T(8,128)(2,1)}) custom-call(s32[160]{0:T(256)} %get-tuple-element.30.order_row, s32[160]{0:T(256)} %get-tuple-element.29.order_owner, s32[1]{0:T(128)} %copy.16.count, bf16[4096,128]{1,0:T(8,128)(2,1)} %feat.5, bf16[4096,128]{1,0:T(8,128)(2,1)} %copy-done.6, ...), custom_call_target="tpu_custom_call" | custom-call | tf_op jit(solution)/shard_map/middle/pallas_call | solution.py:388
  146.0 9.4 %all-to-all-start.1 = ((bf16[128,136,128]{2,1,0:T(8,128)(2,1)}), bf16[128,136,128]{2,1,0:T(8,128)(2,1)}, u32[]{:S(2)}, u32[]{:S(2)}) async-start(bf16[128,136,128]{2,1,0:T(8,128)(2,1)} %get-tuple-element.20), calls=%async_computation.1 | async-start | bytes 8912896 | tf_op jit(solution)/shard_map/all_to_all | solution.py:619
  155.5 1.6 copy-done.4
  157.1 2.1 side.1
  159.3 2.8 collective-permute-start.6
  163.4 10.5 %collective-permute-done.6 = f32[4,32,128]{2,1,0:T(8,128)S(1)} collective-permute-done((f32[4,32,128]{2,1,0:T(8,128)S(1)}, f32[4,32,128]{2,1,0:T(8,128)S(1)}, u32[]{:S(2)}, u32[]{:S(2)}) %collective-permute-start.6) | collective-permute-done | bytes 65568 | tf_op jit(solution)/shard_map/ppermute | solution.py:629
  174.7 1.0 collective-permute-start.9
  175.7 4.8 %collective-permute-start.8 = (f32[32,128]{1,0:T(8,128)S(1)}, f32[32,128]{1,0:T(8,128)S(1)}, u32[]{:S(2)}, u32[]{:S(2)}) collective-permute-start(f32[32,128]{1,0:T(8,128)S(1)} %get-tuple-element.53), channel_id=1, source_target_pairs={{0,16},{2,18},{4,20},{6,22},{8,24},{10,26},{12,28},{14,30},{16,0},... | collective-permute-start | bytes 49160 | tf_op jit(solution)/shard_map/ppermute | solution.py:629
  180.5 1.8 collective-permute-done.8
  182.3 2.5 collective-permute-done.7
  184.8 3.7 %collective-permute-start.12 = (f32[32,128]{1,0:T(8,128)S(1)}, f32[32,128]{1,0:T(8,128)S(1)}, u32[]{:S(2)}, u32[]{:S(2)}) collective-permute-start(f32[32,128]{1,0:T(8,128)S(1)} %fusion.16), channel_id=1, source_target_pairs={{0,96},{2,98},{4,100},{6,102},{8,104},{10,106},{12,108},{14,110},{... | collective-permute-start | bytes 49160 | tf_op jit(solution)/shard_map/ppermute | solution.py:629
  189.3 64.0 %collective-permute-done.12 = f32[32,128]{1,0:T(8,128)S(1)} collective-permute-done((f32[32,128]{1,0:T(8,128)S(1)}, f32[32,128]{1,0:T(8,128)S(1)}, u32[]{:S(2)}, u32[]{:S(2)}) %collective-permute-start.12) | collective-permute-done | bytes 16416 | tf_op jit(solution)/shard_map/ppermute | solution.py:629
  253.3 4.9 %collective-permute-start.13 = (f32[32,128]{1,0:T(8,128)S(1)}, f32[32,128]{1,0:T(8,128)S(1)}, u32[]{:S(2)}, u32[]{:S(2)}) collective-permute-start(f32[32,128]{1,0:T(8,128)S(1)} %add_add_fusion), channel_id=1, source_target_pairs={{0,128},{2,130},{4,132},{6,134},{8,136},{10,138},{12,140},{14,142}... | collective-permute-start | bytes 49160 | tf_op jit(solution)/shard_map/ppermute | solution.py:629
  258.3 2.8 %collective-permute-done.13 = f32[32,128]{1,0:T(8,128)S(1)} collective-permute-done((f32[32,128]{1,0:T(8,128)S(1)}, f32[32,128]{1,0:T(8,128)S(1)}, u32[]{:S(2)}, u32[]{:S(2)}) %collective-permute-start.13) | collective-permute-done | bytes 16416 | tf_op jit(solution)/shard_map/ppermute | solution.py:629
  261.1 1.8 collective-permute-start.16
  263.7 1.5 collective-permute-start.14
  265.2 3.0 %collective-permute-done.15 = f32[32,128]{1,0:T(8,128)S(1)} collective-permute-done((f32[32,128]{1,0:T(8,128)S(1)}, f32[32,128]{1,0:T(8,128)S(1)}, u32[]{:S(2)}, u32[]{:S(2)}) %collective-permute-start.15) | collective-permute-done | bytes 16416 | tf_op jit(solution)/shard_map/ppermute | solution.py:629
  268.2 2.1 collective-permute-start.19
  270.3 0.9 collective-permute-start.18
  271.3 1.1 collective-permute-start.17
  272.4 4.4 %finish.1 = (f32[32,128,128]{2,1,0:T(8,128)}, f32[4,32,128]{2,1,0:T(8,128)S(1)}) custom-call(s32[128]{0:T(128)S(1)} %copy-done.10, s32[2]{0:T(128)S(1)} %copy-done.11, bf16[128,136,128]{2,1,0:T(8,128)(2,1)} %all-to-all-done.1.returned, f32[32,128,128]{2,1,0:T(8,128)S(1)} %bitcast.36, f32[4,32,128]{2,1,0:T(8,128)S(1)} %pad_maximum_fusion.1.grads), custom_call_target="tpu_custom_call" | custom-call | tf_op jit(solution)/shard_map/finish/pallas_call | solution.py:528
  276.8 1.3 place.1
  (81 shorter events, 6.8 us)
Async XLA Ops:
  0.6 24.4 %collective-permute-start = (bf16[4096,128]{1,0:T(8,128)(2,1)}, bf16[4096,128]{1,0:T(8,128)(2,1)S(1)}, u32[]{:S(2)}, u32[]{:S(2)}) collective-permute-start(bf16[4096,128]{1,0:T(8,128)(2,1)} %feat.5), channel_id=1, source_target_pairs={{0,1},{1,0},{2,3},{3,2},{4,5},{5,4},{6,7},{7,6},{8,9},{9,8},{10,11... | collective-permute-start | bytes 3145736 | tf_op jit(solution)/shard_map/ppermute | solution.py:623
  4.7 16.0 %copy-start.13 = (bf16[128,256]{1,0:T(8,128)(2,1)S(1)}, bf16[128,256]{1,0:T(8,128)(2,1)}, u32[]{:S(2)}) copy-start(bf16[128,256]{1,0:T(8,128)(2,1)} %param.12) | copy-start | bytes 196612
  4.8 16.1 %copy-start.14 = (bf16[128,256]{1,0:T(8,128)(2,1)S(1)}, bf16[128,256]{1,0:T(8,128)(2,1)}, u32[]{:S(2)}) copy-start(bf16[128,256]{1,0:T(8,128)(2,1)} %param.13) | copy-start | bytes 196612
  4.8 17.4 %copy-start.9 = (s32[160]{0:T(256)S(1)}, s32[160]{0:T(256)}, u32[]{:S(2)}) copy-start(s32[160]{0:T(256)} %row.1) | copy-start | bytes 1924
  4.8 17.5 %copy-start.15 = (s32[160]{0:T(256)S(1)}, s32[160]{0:T(256)}, u32[]{:S(2)}) copy-start(s32[160]{0:T(256)} %param.16) | copy-start | bytes 1924
  4.8 20.3 %copy-start.2 = (bf16[4096,256]{1,0:T(8,128)(2,1)S(1)}, bf16[4096,256]{1,0:T(8,128)(2,1)}, u32[]{:S(2)}) copy-start(bf16[4096,256]{1,0:T(8,128)(2,1)} %panel.5) | copy-start | bytes 6291460
  4.8 118.3 %all-to-all-start = ((bf16[128,136,128]{2,1,0:T(8,128)(2,1)}), bf16[128,136,128]{2,1,0:T(8,128)(2,1)}, u32[]{:S(2)}, u32[]{:S(2)}) async-start(bf16[128,136,128]{2,1,0:T(8,128)(2,1)} %pack.1), calls=%async_computation | async-start | bytes 8912896 | tf_op jit(solution)/shard_map/all_to_all | solution.py:619
  20.9 4.0 %collective-permute-start.1 = (bf16[256,256]{1,0:T(8,128)(2,1)S(1)}, bf16[256,256]{1,0:T(8,128)(2,1)S(1)}, u32[]{:S(2)}, u32[]{:S(2)}) collective-permute-start(bf16[256,256]{1,0:T(8,128)(2,1)S(1)} %maximum_select_fusion), channel_id=1, source_target_pairs={{0,1},{1,0},{2,3},{3,2},{4,5},{5,4},{6,7},{7,6},{8,9},{9,8},{10,11... | collective-permute-start | bytes 393224 | tf_op jit(solution)/shard_map/ppermute | solution.py:623
  21.0 4.0 %collective-permute-start.2 = (bf16[4096,128]{1,0:T(8,128)(2,1)}, bf16[4096,128]{1,0:T(8,128)(2,1)}, u32[]{:S(2)}, u32[]{:S(2)}) collective-permute-start(bf16[4096,128]{1,0:T(8,128)(2,1)} %cot.1), channel_id=1, source_target_pairs={{0,1},{1,0},{2,3},{3,2},{4,5},{5,4},{6,7},{7,6},{8,9},{9,8},{10,11... | collective-permute-start | bytes 3145736 | tf_op jit(solution)/shard_map/ppermute | solution.py:623
  25.0 22.0 %copy-start.7 = (bf16[256,256]{1,0:T(8,128)(2,1)}, bf16[256,256]{1,0:T(8,128)(2,1)S(1)}, u32[]{:S(2)}) copy-start(bf16[256,256]{1,0:T(8,128)(2,1)S(1)} %get-tuple-element.55.rest_1_.nbr_w) | copy-start | bytes 393220
  25.0 22.0 %copy-start.8 = (bf16[256,256]{1,0:T(8,128)(2,1)}, bf16[256,256]{1,0:T(8,128)(2,1)S(1)}, u32[]{:S(2)}) copy-start(bf16[256,256]{1,0:T(8,128)(2,1)S(1)} %get-tuple-element.56.rest_0_.own_w) | copy-start | bytes 393220
  25.1 22.0 %copy-start.6 = (bf16[4096,128]{1,0:T(8,128)(2,1)}, bf16[4096,128]{1,0:T(8,128)(2,1)S(1)}, u32[]{:S(2)}) copy-start(bf16[4096,128]{1,0:T(8,128)(2,1)S(1)} %collective-permute-done.rest_2_.feat_peer) | copy-start | bytes 3145732
  130.8 3.1 %collective-permute-start.3 = (bf16[4096,128]{1,0:T(8,128)(2,1)}, bf16[4096,128]{1,0:T(8,128)(2,1)S(1)}, u32[]{:S(2)}, u32[]{:S(2)}) collective-permute-start(bf16[4096,128]{1,0:T(8,128)(2,1)} %gather.1.agg), channel_id=1, source_target_pairs={{0,1},{1,0},{2,3},{3,2},{4,5},{5,4},{6,7},{7,6},{8,9},{9,8},{10,11... | collective-permute-start | bytes 3145736 | tf_op jit(solution)/shard_map/ppermute | solution.py:623
  146.0 126.4 %all-to-all-start.1 = ((bf16[128,136,128]{2,1,0:T(8,128)(2,1)}), bf16[128,136,128]{2,1,0:T(8,128)(2,1)}, u32[]{:S(2)}, u32[]{:S(2)}) async-start(bf16[128,136,128]{2,1,0:T(8,128)(2,1)} %get-tuple-element.20), calls=%async_computation.1 | async-start | bytes 8912896 | tf_op jit(solution)/shard_map/all_to_all | solution.py:619
  155.4 117.0 %copy-start.10 = (s32[128]{0:T(128)S(1)}, s32[128]{0:T(128)}, u32[]{:S(2)}) copy-start(s32[128]{0:T(128)} %send.3) | copy-start | bytes 1540
  155.4 117.0 %copy-start.11 = (s32[2]{0:T(128)S(1)}, s32[2]{0:T(128)}, u32[]{:S(2)}) copy-start(s32[2]{0:T(128)} %hubs.3) | copy-start | bytes 28
  159.3 14.7 %collective-permute-start.6 = (f32[4,32,128]{2,1,0:T(8,128)S(1)}, f32[4,32,128]{2,1,0:T(8,128)S(1)}, u32[]{:S(2)}, u32[]{:S(2)}) collective-permute-start(f32[4,32,128]{2,1,0:T(8,128)S(1)} %get-tuple-element.43), channel_id=1, source_target_pairs={{0,6},{2,4},{4,2},{6,0},{8,14},{10,12},{12,10},{14,8},{16,22},{18,... | collective-permute-start | bytes 196616 | tf_op jit(solution)/shard_map/ppermute | solution.py:629
  162.0 11.9 %collective-permute-start.5 = (f32[4,32,128]{2,1,0:T(8,128)S(1)}, f32[4,32,128]{2,1,0:T(8,128)S(1)}, u32[]{:S(2)}, u32[]{:S(2)}) collective-permute-start(f32[4,32,128]{2,1,0:T(8,128)S(1)} %get-tuple-element.44), channel_id=1, source_target_pairs={{0,4},{2,6},{4,0},{6,2},{8,12},{10,14},{12,8},{14,10},{16,20},{18,... | collective-permute-start | bytes 196616 | tf_op jit(solution)/shard_map/ppermute | solution.py:629
  162.9 11.1 %collective-permute-start.4 = (f32[4,32,128]{2,1,0:T(8,128)S(1)}, f32[4,32,128]{2,1,0:T(8,128)S(1)}, u32[]{:S(2)}, u32[]{:S(2)}) collective-permute-start(f32[4,32,128]{2,1,0:T(8,128)S(1)} %get-tuple-element.45), channel_id=1, source_target_pairs={{0,2},{2,0},{4,6},{6,4},{8,10},{10,8},{12,14},{14,12},{16,18},{18,... | collective-permute-start | bytes 196616 | tf_op jit(solution)/shard_map/ppermute | solution.py:629
  174.7 5.8 %collective-permute-start.9 = (f32[32,128]{1,0:T(8,128)S(1)}, f32[32,128]{1,0:T(8,128)S(1)}, u32[]{:S(2)}, u32[]{:S(2)}) collective-permute-start(f32[32,128]{1,0:T(8,128)S(1)} %get-tuple-element.52), channel_id=1, source_target_pairs={{0,24},{2,26},{4,28},{6,30},{8,16},{10,18},{12,20},{14,22},{16,8},... | collective-permute-start | bytes 49160 | tf_op jit(solution)/shard_map/ppermute | solution.py:629
  175.7 6.6 %collective-permute-start.8 = (f32[32,128]{1,0:T(8,128)S(1)}, f32[32,128]{1,0:T(8,128)S(1)}, u32[]{:S(2)}, u32[]{:S(2)}) collective-permute-start(f32[32,128]{1,0:T(8,128)S(1)} %get-tuple-element.53), channel_id=1, source_target_pairs={{0,16},{2,18},{4,20},{6,22},{8,24},{10,26},{12,28},{14,30},{16,0},... | collective-permute-start | bytes 49160 | tf_op jit(solution)/shard_map/ppermute | solution.py:629
  180.5 4.3 %collective-permute-start.7 = (f32[32,128]{1,0:T(8,128)S(1)}, f32[32,128]{1,0:T(8,128)S(1)}, u32[]{:S(2)}, u32[]{:S(2)}) collective-permute-start(f32[32,128]{1,0:T(8,128)S(1)} %get-tuple-element.54), channel_id=1, source_target_pairs={{0,8},{2,10},{4,12},{6,14},{8,0},{10,2},{12,4},{14,6},{16,24},{18,... | collective-permute-start | bytes 49160 | tf_op jit(solution)/shard_map/ppermute | solution.py:629
  184.8 68.5 %collective-permute-start.12 = (f32[32,128]{1,0:T(8,128)S(1)}, f32[32,128]{1,0:T(8,128)S(1)}, u32[]{:S(2)}, u32[]{:S(2)}) collective-permute-start(f32[32,128]{1,0:T(8,128)S(1)} %fusion.16), channel_id=1, source_target_pairs={{0,96},{2,98},{4,100},{6,102},{8,104},{10,106},{12,108},{14,110},{... | collective-permute-start | bytes 49160 | tf_op jit(solution)/shard_map/ppermute | solution.py:629
  188.5 64.8 %collective-permute-start.11 = (f32[32,128]{1,0:T(8,128)S(1)}, f32[32,128]{1,0:T(8,128)S(1)}, u32[]{:S(2)}, u32[]{:S(2)}) collective-permute-start(f32[32,128]{1,0:T(8,128)S(1)} %fusion.16), channel_id=1, source_target_pairs={{0,64},{2,66},{4,68},{6,70},{8,72},{10,74},{12,76},{14,78},{16,80}... | collective-permute-start | bytes 49160 | tf_op jit(solution)/shard_map/ppermute | solution.py:629
  188.5 64.8 %collective-permute-start.10 = (f32[32,128]{1,0:T(8,128)S(1)}, f32[32,128]{1,0:T(8,128)S(1)}, u32[]{:S(2)}, u32[]{:S(2)}) collective-permute-start(f32[32,128]{1,0:T(8,128)S(1)} %fusion.16), channel_id=1, source_target_pairs={{0,32},{2,34},{4,36},{6,38},{8,40},{10,42},{12,44},{14,46},{16,48}... | collective-permute-start | bytes 49160 | tf_op jit(solution)/shard_map/ppermute | solution.py:629
  253.3 7.7 %collective-permute-start.13 = (f32[32,128]{1,0:T(8,128)S(1)}, f32[32,128]{1,0:T(8,128)S(1)}, u32[]{:S(2)}, u32[]{:S(2)}) collective-permute-start(f32[32,128]{1,0:T(8,128)S(1)} %add_add_fusion), channel_id=1, source_target_pairs={{0,128},{2,130},{4,132},{6,134},{8,136},{10,138},{12,140},{14,142}... | collective-permute-start | bytes 49160 | tf_op jit(solution)/shard_map/ppermute | solution.py:629
  261.1 4.1 %collective-permute-start.16 = (f32[32,128]{1,0:T(8,128)S(1)}, f32[32,128]{1,0:T(8,128)S(1)}, u32[]{:S(2)}, u32[]{:S(2)}) collective-permute-start(f32[32,128]{1,0:T(8,128)S(1)} %add.91), channel_id=1, source_target_pairs={{0,24},{2,26},{4,28},{6,30},{8,16},{10,18},{12,20},{14,22},{16,8},... | collective-permute-start | bytes 49160 | tf_op jit(solution)/shard_map/ppermute | solution.py:629
  262.9 5.2 %collective-permute-start.15 = (f32[32,128]{1,0:T(8,128)S(1)}, f32[32,128]{1,0:T(8,128)S(1)}, u32[]{:S(2)}, u32[]{:S(2)}) collective-permute-start(f32[32,128]{1,0:T(8,128)S(1)} %add.91), channel_id=1, source_target_pairs={{0,16},{2,18},{4,20},{6,22},{8,24},{10,26},{12,28},{14,30},{16,0},... | collective-permute-start | bytes 49160 | tf_op jit(solution)/shard_map/ppermute | solution.py:629
  263.7 4.5 %collective-permute-start.14 = (f32[32,128]{1,0:T(8,128)S(1)}, f32[32,128]{1,0:T(8,128)S(1)}, u32[]{:S(2)}, u32[]{:S(2)}) collective-permute-start(f32[32,128]{1,0:T(8,128)S(1)} %add.91), channel_id=1, source_target_pairs={{0,8},{2,10},{4,12},{6,14},{8,0},{10,2},{12,4},{14,6},{16,24},{18,... | collective-permute-start | bytes 49160 | tf_op jit(solution)/shard_map/ppermute | solution.py:629
  268.2 8.6 %collective-permute-start.19 = (f32[4,32,128]{2,1,0:T(8,128)S(1)}, f32[4,32,128]{2,1,0:T(8,128)S(1)}, u32[]{:S(2)}, u32[]{:S(2)}) collective-permute-start(f32[4,32,128]{2,1,0:T(8,128)S(1)} %pad_maximum_fusion.1.grads), channel_id=1, source_target_pairs={{0,6},{2,4},{4,2},{6,0},{8,14},{10,12},{12,10},{14,8},{16,22},{18,... | collective-permute-start | bytes 196616 | tf_op jit(solution)/shard_map/ppermute | solution.py:629
  270.3 6.5 %collective-permute-start.18 = (f32[4,32,128]{2,1,0:T(8,128)S(1)}, f32[4,32,128]{2,1,0:T(8,128)S(1)}, u32[]{:S(2)}, u32[]{:S(2)}) collective-permute-start(f32[4,32,128]{2,1,0:T(8,128)S(1)} %pad_maximum_fusion.1.grads), channel_id=1, source_target_pairs={{0,4},{2,6},{4,0},{6,2},{8,12},{10,14},{12,8},{14,10},{16,20},{18,... | collective-permute-start | bytes 196616 | tf_op jit(solution)/shard_map/ppermute | solution.py:629
  271.3 5.6 %collective-permute-start.17 = (f32[4,32,128]{2,1,0:T(8,128)S(1)}, f32[4,32,128]{2,1,0:T(8,128)S(1)}, u32[]{:S(2)}, u32[]{:S(2)}) collective-permute-start(f32[4,32,128]{2,1,0:T(8,128)S(1)} %pad_maximum_fusion.1.grads), channel_id=1, source_target_pairs={{0,2},{2,0},{4,6},{6,4},{8,10},{10,8},{12,14},{14,12},{16,18},{18,... | collective-permute-start | bytes 196616 | tf_op jit(solution)/shard_map/ppermute | solution.py:629
  (6 other events, 25.4 us)

commit v5 on v4

--- a/solution.py
+++ b/solution.py
@@ -90,7 +90,7 @@
 def prepare_kernel(
     row, count, order, first, second, kinds, values, panel, *rest
 ):
-    inv, flipped, pairs, squares = rest[-4:]
+    inv, flipped, pairs, panel_t, squares = rest[-5:]
     step, steps = pl.program_id(0), pl.num_programs(0)
     edge = values.shape[1]
     slots, duos = flipped.shape[0], pairs.shape[0]
@@ -121,6 +121,7 @@
         @pl.loop(0, squares.shape[0] // edge)
         def _(t):
             at = pl.ds(pl.multiple_of(t * edge, edge), edge)
+            panel_t[:, at] = panel[at, :].T
             wide = panel[at, :].astype(F32)
             wide = wide * wide
             half = wide.shape[1] // 2
@@ -142,6 +143,7 @@
             jax.ShapeDtypeStruct((rows, edge), F32),
             jax.ShapeDtypeStruct((slots, edge, edge), BF16),
             jax.ShapeDtypeStruct((duos, edge, 2 * edge), BF16),
+            jax.ShapeDtypeStruct((hubs, rows), BF16),
         ),
         grid_spec=pltpu.PrefetchScalarGridSpec(
             num_scalar_prefetch=6,
@@ -155,6 +157,7 @@
                 pl.BlockSpec((rows, edge), whole),
                 pl.BlockSpec((slots // steps, edge, edge), lambda g, *_: (g, 0, 0)),
                 pl.BlockSpec((duos // steps, edge, 2 * edge), lambda g, *_: (g, 0, 0)),
+                pl.BlockSpec((hubs, rows), whole),
             ),
             scratch_shapes=[pltpu.VMEM((rows, edge), F32)],
         ),
@@ -271,22 +274,22 @@
 
 def middle_kernel(
     order_row, order_owner, count,
-    feat, feat_peer, agg, agg_peer, cot, cot_peer, inv, panel, flipped, own_w, nbr_w,
-    layer, slopes, terms,
+    feat, feat_peer, agg, agg_peer, cot, cot_peer, inv, panel_t, flipped, own_w, nbr_w,
+    terms,
     feat_v, feat_peer_v, agg_v, agg_peer_v, cot_v, cot_peer_v, inv_v, panel_v, flipped_v,
-    layer_v, slopes_v, agg_slopes, terms_v, hub_acc, hub_wide, carry,
-    in_sems, flip_sems, out_sems, term_sems,
+    agg_slopes, terms_v, hub_acc, hub_wide, carry, in_sems, flip_sems, term_sems,
 ):
     rows, half = feat_v.shape
     slots, edge, _ = flipped_v.shape
     parts = terms_v.shape[0]
     copy = pltpu.make_async_copy
     block = rows // ROW_STEPS
-    sources = (feat, feat_peer, agg, agg_peer, cot, cot_peer, inv, panel)
-    places = (feat_v, feat_peer_v, agg_v, agg_peer_v, cot_v, cot_peer_v, inv_v, panel_v)
+    sources = (feat, feat_peer, agg, agg_peer, cot, cot_peer, inv)
+    places = (feat_v, feat_peer_v, agg_v, agg_peer_v, cot_v, cot_peer_v, inv_v)
     at = [pl.ds(t * block, block) for t in range(ROW_STEPS)]
     inputs = [
         [copy(s.at[at[t], :], d.at[at[t], :], in_sems.at[t, i]) for i, (s, d) in enumerate(zip(sources, places))]
+        + [copy(panel_t.at[:, at[t]], panel_v.at[:, at[t]], in_sems.at[t, 7])]
         for t in range(ROW_STEPS)
     ]
     steps = slots // SLOT_STEP
@@ -307,7 +310,6 @@
     hub_wide[...] = jnp.zeros_like(hub_wide)
     carry[...] = jnp.zeros_like(carry)
 
-    sent = []
     for t in range(ROW_STEPS):
         for c in inputs[t]:
             c.wait()
@@ -315,17 +317,11 @@
         preact = dot(
             jnp.concatenate([feat_v[here, :], feat_peer_v[here, :]], axis=1), own_w[...], NN
         ) + dot(jnp.concatenate([agg_v[here, :], agg_peer_v[here, :]], axis=1), nbr_w[...], NN)
-        layer_v[here, :] = jnp.maximum(preact[:, :half], 0.0).astype(BF16)
         cotangent = jnp.concatenate([cot_v[here, :], cot_peer_v[here, :]], axis=1).astype(F32)
         slope = jnp.where(preact > 0, cotangent, 0.0).astype(BF16)
-        slopes_v[here, :] = slope
-        sent.append(copy(layer_v.at[here, :], layer.at[here, :], out_sems.at[t, 0]))
-        sent.append(copy(slopes_v.at[here, :], slopes.at[here, :], out_sems.at[t, 1]))
-        sent[-2].start()
-        sent[-1].start()
         back = (dot(slope, nbr_w[:half, :], NT) * inv_v[here, :]).astype(BF16)
         agg_slopes[here, :] = back
-        hub = dot(panel_v[here, :], back, TN)
+        hub = dot(panel_v[:, here], back, NN)
         if t == 0:
             hub_acc[...] = hub
         else:
@@ -369,43 +365,34 @@
                 owners = pl.ds(g * group, group)
                 copy(terms_v.at[owners], terms.at[owners], term_sems.at[0]).start()
 
-    for c in sent:
-        c.wait()
     copy(terms_v, terms, term_sems.at[0]).wait()
 
 
 def middle(
     order_row, order_owner, count,
-    feat, feat_peer, agg, agg_peer, cot, cot_peer, inv, panel, flipped, own_w, nbr_w, parts,
+    feat, feat_peer, agg, agg_peer, cot, cot_peer, inv, panel_t, flipped, own_w, nbr_w, parts,
 ):
     rows, half = feat.shape
-    hubs = panel.shape[1]
+    hubs = panel_t.shape[0]
     edge = flipped.shape[1]
     narrow = pltpu.VMEM((rows, half), BF16)
-    wide = pltpu.VMEM((rows, 2 * half), BF16)
     whole = lambda g, *_: (0, 0)
     height = edge + 8
     return pl.pallas_call(
         middle_kernel,
         name="middle",
-        out_shape=(
-            jax.ShapeDtypeStruct((rows, half), BF16),
-            jax.ShapeDtypeStruct((rows, 2 * half), BF16),
-            jax.ShapeDtypeStruct((parts, height, half), BF16),
-        ),
+        out_shape=jax.ShapeDtypeStruct((parts, height, half), BF16),
         grid_spec=pltpu.PrefetchScalarGridSpec(
             num_scalar_prefetch=3,
             grid=(1,),
             in_specs=[ANY] * 9
             + [pl.BlockSpec(own_w.shape, whole), pl.BlockSpec(nbr_w.shape, whole)],
-            out_specs=(HBM, HBM, HBM),
+            out_specs=HBM,
             scratch_shapes=[narrow] * 6
             + [
                 pltpu.VMEM((rows, half), F32),
-                pltpu.VMEM((rows, hubs), BF16),
+                pltpu.VMEM((hubs, rows), BF16),
                 pltpu.VMEM(flipped.shape, BF16),
-                narrow,
-                wide,
                 narrow,
                 pltpu.VMEM((parts, height, half), BF16),
                 pltpu.VMEM((hubs, half), F32),
@@ -413,21 +400,30 @@
                 pltpu.VMEM((edge, half), F32),
                 pltpu.SemaphoreType.DMA((ROW_STEPS, 8)),
                 pltpu.SemaphoreType.DMA((flipped.shape[0] // SLOT_STEP,)),
-                pltpu.SemaphoreType.DMA((ROW_STEPS, 2)),
                 pltpu.SemaphoreType.DMA((1,)),
             ],
         ),
         compiler_params=own_copies(MID_MIB),
     )(
         order_row, order_owner, count,
-        feat, feat_peer, agg, agg_peer, cot, cot_peer, inv, panel, flipped, own_w, nbr_w,
-    )
-
-
-def side_kernel(where, feat, agg, slopes, grads, acc):
+        feat, feat_peer, agg, agg_peer, cot, cot_peer, inv, panel_t, flipped, own_w, nbr_w,
+    )
+
+
+def side_kernel(
+    where, feat, feat_peer, agg, agg_peer, cot, cot_peer, own_w, nbr_w, layer, slopes, grads, acc
+):
     step, steps = pl.program_id(0), pl.num_programs(0)
     half = feat.shape[1]
-    part = dot(jnp.concatenate([feat[...], agg[...]], axis=1), slopes[...], TN)
+    x, a = feat[...], agg[...]
+    preact = dot(jnp.concatenate([x, feat_peer[...]], axis=1), own_w[...], NN) + dot(
+        jnp.concatenate([a, agg_peer[...]], axis=1), nbr_w[...], NN
+    )
+    layer[...] = jnp.maximum(preact[:, :half], 0.0).astype(BF16)
+    cotangent = jnp.concatenate([cot[...], cot_peer[...]], axis=1).astype(F32)
+    slope = jnp.where(preact > 0, cotangent, 0.0).astype(BF16)
+    slopes[...] = slope
+    part = dot(jnp.concatenate([x, a], axis=1), slope, TN)
 
     @pl.when(step == 0)
     def _():
@@ -439,33 +435,40 @@
 
     @pl.when(step == steps - 1)
     def _():
-        y, x = where[0] % 4, (where[0] // 4) % 4
-        n = half // 4
+        y = where[0] % 4
         for c in range(4):
-            for r in range(4):
-                grads[jnp.bitwise_xor(c, y), jnp.bitwise_xor(r, x)] = acc[
-                    (c // 2) * half + r * n : (c // 2) * half + (r + 1) * n,
-                    (c % 2) * half : (c % 2 + 1) * half,
-                ]
-
-
-def side(where, feat, agg, slopes):
+            grads[jnp.bitwise_xor(c, y)] = acc[
+                (c // 2) * half : (c // 2 + 1) * half, (c % 2) * half : (c % 2 + 1) * half
+            ]
+
+
+def side(where, feat, feat_peer, agg, agg_peer, cot, cot_peer, own_w, nbr_w, after):
     rows, half = feat.shape
-    block = 1024
+    block = rows // ROW_STEPS
     by_row = lambda width: pl.BlockSpec((block, width), lambda g, *_: (g, 0))
+    whole = lambda g, *_: (0, 0)
     return pl.pallas_call(
-        side_kernel,
+        lambda *refs: side_kernel(*refs[:9], *refs[10:]),
         name="side",
-        out_shape=jax.ShapeDtypeStruct((4, 4, half // 4, half), F32),
+        out_shape=(
+            jax.ShapeDtypeStruct((rows, half), BF16),
+            jax.ShapeDtypeStruct((rows, 2 * half), BF16),
+            jax.ShapeDtypeStruct((4, half, half), F32),
+        ),
         grid_spec=pltpu.PrefetchScalarGridSpec(
             num_scalar_prefetch=1,
             grid=(rows // block,),
-            in_specs=[by_row(half), by_row(half), by_row(2 * half)],
-            out_specs=pl.BlockSpec((4, 4, half // 4, half), lambda g, *_: (0, 0, 0, 0)),
+            in_specs=[by_row(half)] * 6
+            + [pl.BlockSpec(own_w.shape, whole), pl.BlockSpec(nbr_w.shape, whole), ANY],
+            out_specs=(
+                by_row(half),
+                by_row(2 * half),
+                pl.BlockSpec((4, half, half), lambda g, *_: (0, 0, 0)),
+            ),
             scratch_shapes=[pltpu.VMEM((2 * half, 2 * half), F32)],
         ),
         compiler_params=params(32, 1),
-    )(where, feat, agg, slopes)
+    )(where, feat, feat_peer, agg, agg_peer, cot, cot_peer, own_w, nbr_w, after)
 
 
 def direct_kernel(slopes, own_w, passed, direct, passed_out):
@@ -547,27 +550,24 @@
 def place_kernel(factor, where, own, one, two, three, self_grad, neighbor_grad, blocks):
     for m, group in enumerate((own, one, two, three)):
         blocks[m] = group[...]
-    y, x, core = where[0] % 4, (where[0] // 4) % 4, where[1]
-    n, half = blocks.shape[2:]
+    y, core = where[0] % 4, where[1]
+    half = blocks.shape[2]
     for j, out in enumerate((self_grad, neighbor_grad)):
         for c in range(2):
             column = 2 * j + jnp.bitwise_xor(c, core)
-            for r in range(4):
-                out[r * n : (r + 1) * n, c * half : (c + 1) * half] = (
-                    blocks[jnp.bitwise_xor(column, y), jnp.bitwise_xor(r, x)] * factor
-                )
+            out[:, c * half : (c + 1) * half] = blocks[jnp.bitwise_xor(column, y)] * factor
 
 
 def put_in_place(where, groups, factor):
-    four, n, half = groups[0].shape
-    out = jax.ShapeDtypeStruct((four * n, 2 * half), F32)
+    rows, half = groups[0].shape
+    out = jax.ShapeDtypeStruct((rows, 2 * half), F32)
     return pl.pallas_call(
         lambda *refs: place_kernel(factor, *refs),
         name="place",
         out_shape=(out, out),
         in_specs=[SMEM] + [VMEM] * 4,
         out_specs=(VMEM, VMEM),
-        scratch_shapes=[pltpu.VMEM((4, four, n, half), F32)],
+        scratch_shapes=[pltpu.VMEM((4, rows, half), F32)],
         compiler_params=own_copies(8),
     )(where, *groups)
 
@@ -673,28 +673,29 @@
     by_owner, by_row, duos = plan(tile_row, tile_owner, tile_count, tiles_dev, dom_size)
     order, order_row, order_owner = by_owner
     first, second, kinds, pair_row, owner_a, owner_b, n_duos = by_row
-    inv, flipped, pairs = prepare(
+    inv, flipped, pairs, panel_t = prepare(
         tile_row, tile_count, order, first, second, kinds, tile_values, hub_panel, duos,
         (own_w, nbr_w, feat_peer, cot_peer),
     )
 
     aggregate = gather(pair_row, owner_a, owner_b, n_duos, pairs, incoming, hub_panel, inv)
     agg_peer = swap(aggregate)
-    layer_out, slopes, terms = middle(
+    terms = middle(
         order_row, order_owner, tile_count,
-        features, feat_peer, aggregate, agg_peer, cotangent, cot_peer, inv, hub_panel, flipped,
+        features, feat_peer, aggregate, agg_peer, cotangent, cot_peer, inv, panel_t, flipped,
         own_w, nbr_w, dom_size,
     )
     returned = exchange(terms)
 
     where = jnp.stack([lax.axis_index("dom").astype(jnp.int32), core.astype(jnp.int32)])
-    grads = side(where, features, aggregate, slopes)
+    layer_out, slopes, grads = side(
+        where, features, feat_peer, aggregate, agg_peer, cotangent, cot_peer, own_w, nbr_w, terms
+    )
     grads = total(grads[0], moved_three(grads, "y"))
     direct, grads = direct_part(slopes, own_w[:half], grads)
-    grads = total(grads[0], moved_three(grads, "x"))
+    grads = total(grads, [move(grads, "x", i) for i in (1, 2, 3)])
     grads = total(grads, [move(grads, "z", i) for i in (1, 2, 3)])
     grads = grads + move(grads, "z", 4)
-    grads = jnp.stack([grads] + [move(grads, "x", i) for i in (1, 2, 3)])
     near = [move(grads, "y", i) for i in (1, 2, 3)]
     input_grad, grads = finish(
         send_tile, hub_rows, returned, direct.reshape(tiles_dev, tile_edge, half), grads

time: 281 us -> 278 us (0.989)
  local copies, waits for them, and re-layouts: 6.43 us -> 14.5 us
  waiting for transfers between devices: 160 us -> 153 us
  starting transfers between devices: 54 us -> 49.3 us
    unnamed x33 -> x51, local copies, waits for them, and re-layouts: 6.37 us -> 14.4 us
    ppermute x16 -> x13, starting transfers between devices: 27.7 us -> 22.7 us  [move(): return lax.ppermute(block, 'dom', pairs)]
    all_to_all x2, waiting for transfers between devices: 72.3 us -> 68.1 us  [exchange(): return lax.all_to_all(block, 'dom', split_axis=0, concat_axis=0, tiled=True)]
    ppermute x16 -> x13, waiting for transfers between devices: 84.6 us -> 81.7 us  [move(): return lax.ppermute(block, 'dom', pairs)]
  transfers between devices with their start and end apart: 22 -> 19, of which waited for: 8 -> 11; matrix products, arithmetic and copies ran while one was open for 1% -> 1% of each run, Pallas kernels for 12% -> 13%
where the time goes in v5:
time: 278 us; the launch traced here: 277 us
  waiting for transfers between devices  153 us (55%)
  Pallas kernels  55.5 us (20%)
  starting transfers between devices  49.3 us (18%)
  local copies, waits for them, and re-layouts  14.5 us (5%)
  other arithmetic  2.98 us (1%)
    ppermute x13, waiting for transfers between devices, move(): return lax.ppermute(block, 'dom', pairs)  81.7 us
    all_to_all x2, waiting for transfers between devices, exchange(): return lax.all_to_all(block, 'dom', split_axis=0, concat_axis=0, tiled=True)  68.1 us
    all_to_all x2, starting transfers between devices, exchange(): return lax.all_to_all(block, 'dom', split_axis=0, concat_axis=0, tiled=True)  25.7 us
    ppermute x13, starting transfers between devices, move(): return lax.ppermute(block, 'dom', pairs)  22.7 us
    pallas_call x1, Pallas kernels, prepare(): pl.pallas_call(prepare_kernel, name='prepare', out_shape=(jax.ShapeDtypeS...  22.4 us
    unnamed x51, local copies, waits for them, and re-layouts  14.4 us
    pallas_call x1, Pallas kernels, middle(): pl.pallas_call(middle_kernel, name='middle', out_shape=jax.ShapeDtypeStru...  10.6 us
    pallas_call x1, Pallas kernels, gather(): pl.pallas_call(gather_kernel, name='gather', out_shape=jax.ShapeDtypeStru...  7.71 us
  transfers between devices with their start and end apart: 19, of which 11 were waited for; matrix products, arithmetic and copies ran while one was open for 1% of the time, Pallas kernels for 13%

profile of v5, /device:TPU:2, one launch (start us, length us, event | category | flops | bytes accessed | tf_op | source)
XLA Modules:
  0.0 276.6 jit_solution(12099412413615563192)
XLA Ops:
  0.7 4.0 %pack.1 = bf16[128,136,128]{2,1,0:T(8,128)(2,1)} custom-call(s32[128]{0:T(128)} %send.3, s32[2]{0:T(128)} %hubs.3, bf16[4096,128]{1,0:T(8,128)(2,1)} %refs_1_.1), custom_call_target="tpu_custom_call" | custom-call | tf_op jit(solution)/shard_map/pack/pallas_call | solution.py:71
  4.8 16.0 %all-to-all-start = ((bf16[128,136,128]{2,1,0:T(8,128)(2,1)}), bf16[128,136,128]{2,1,0:T(8,128)(2,1)}, u32[]{:S(2)}, u32[]{:S(2)}) async-start(bf16[128,136,128]{2,1,0:T(8,128)(2,1)} %pack.1), calls=%async_computation | async-start | bytes 8912896 | tf_op jit(solution)/shard_map/all_to_all | solution.py:619
  25.1 2.4 copy-done.13
  27.5 22.4 %prepare.1 = (f32[4096,128]{1,0:T(8,128)S(1)}, bf16[160,128,128]{2,1,0:T(8,128)(2,1)S(1)}, bf16[96,128,256]{2,1,0:T(8,128)(2,1)}, bf16[256,4096]{1,0:T(8,128)(2,1)S(1)}) custom-call(s32[160]{0:T(256)S(1)} %copy-done.19, s32[1]{0:T(128)} %copy.16.count, s32[160]{0:T(256)S(1)} %get-tuple-element.32.order, s32[96]{0:T(128)S(1)} %get-tuple-element.36.first, ...), custom_call_target="tpu_custom_call" | custom-call | flops 60000002048 | bytes 40000000 | tf_op jit(solution)/shard_map/prepare/pallas_call | solution.py:139
  50.0 1.3 copy-done.3
  51.3 2.4 copy-done.4
  53.6 1.3 copy-done.14
  55.0 68.1 %all-to-all-done.incoming = bf16[128,136,128]{2,1,0:T(8,128)(2,1)} async-done(((bf16[128,136,128]{2,1,0:T(8,128)(2,1)}), bf16[128,136,128]{2,1,0:T(8,128)(2,1)}, u32[]{:S(2)}, u32[]{:S(2)}) %all-to-all-start) | async-done | bytes 4456480 | tf_op jit(solution)/shard_map/all_to_all | solution.py:619
  123.0 7.7 %gather.1.agg.refs_3_ = bf16[4096,128]{1,0:T(8,128)(2,1)} custom-call(s32[96]{0:T(128)} %get-tuple-element.37.row, s32[96]{0:T(128)} %get-tuple-element.34.owner_a, s32[96]{0:T(128)} %get-tuple-element.33.owner_b, s32[1]{0:T(128)} %bitcast.3.n_duos, bf16[96,128,256]{2,1,0:T(8,128)(2,1)} %get-tuple-element.17.pairs, ...), custom_call_target="tpu_custom_call" | custom-call | tf_op jit(solution)/shard_map/gather/pallas_call | solution.py:242
  131.0 2.9 %collective-permute-done.3.agg_peer.refs_4_ = bf16[4096,128]{1,0:T(8,128)(2,1)S(1)} collective-permute-done((bf16[4096,128]{1,0:T(8,128)(2,1)}, bf16[4096,128]{1,0:T(8,128)(2,1)S(1)}, u32[]{:S(2)}, u32[]{:S(2)}) %collective-permute-start.3) | collective-permute-done | bytes 1048608 | tf_op jit(solution)/shard_map/ppermute | solution.py:623
  134.9 10.6 %middle.1.refs_9_ = bf16[128,136,128]{2,1,0:T(8,128)(2,1)} custom-call(s32[160]{0:T(256)} %get-tuple-element.31.order_row, s32[160]{0:T(256)} %get-tuple-element.30.order_owner, s32[1]{0:T(128)} %copy.16.count, bf16[4096,128]{1,0:T(8,128)(2,1)} %refs_1_.1, bf16[4096,128]{1,0:T(8,128)(2,1)} %copy-done.7, bf16[4096,128]{1,0:T(8,128)(2,1)} %gather.1.agg.refs_3_, ...), custom_call_target="tpu_custom_call" | custom-call | tf_op jit(solution)/shard_map/middle/pallas_call | solution.py:381
  145.6 9.7 %all-to-all-start.1 = ((bf16[128,136,128]{2,1,0:T(8,128)(2,1)}), bf16[128,136,128]{2,1,0:T(8,128)(2,1)}, u32[]{:S(2)}, u32[]{:S(2)}) async-start(bf16[128,136,128]{2,1,0:T(8,128)(2,1)} %middle.1.refs_9_), calls=%async_computation.1 | async-start | bytes 8912896 | tf_op jit(solution)/shard_map/all_to_all | solution.py:619
  155.4 2.3 copy-done
  157.6 1.2 copy-done.8
  158.8 1.2 copy-done.10
  160.1 1.2 copy-done.12
  161.3 4.4 %side.1 = (bf16[4096,128]{1,0:T(8,128)(2,1)}, bf16[4096,256]{1,0:T(8,128)(2,1)S(1)}, f32[4,128,128]{2,1,0:T(8,128)S(1)}) custom-call(s32[2]{0:T(128)S(1)} %pad_add_fusion.refs_0_, bf16[4096,128]{1,0:T(8,128)(2,1)S(1)} %copy-done.2, bf16[4096,128]{1,0:T(8,128)(2,1)S(1)} %copy-done.8, bf16[4096,128]{1,0:T(8,128)(2,1)S(1)} %copy-done.1, ...), custom_call_target="tpu_custom_call" | custom-call | tf_op jit(solution)/shard_map/side/pallas_call | solution.py:450
  165.7 2.8 collective-permute-start.6
  169.9 4.2 %collective-permute-done.6 = f32[128,128]{1,0:T(8,128)S(1)} collective-permute-done((f32[128,128]{1,0:T(8,128)S(1)}, f32[128,128]{1,0:T(8,128)S(1)}, u32[]{:S(2)}, u32[]{:S(2)}) %collective-permute-start.6) | collective-permute-done | bytes 65568 | tf_op jit(solution)/shard_map/ppermute | solution.py:629
  176.1 1.8 collective-permute-start.9
  177.9 3.2 %collective-permute-start.8 = (f32[128,128]{1,0:T(8,128)S(1)}, f32[128,128]{1,0:T(8,128)S(1)}, u32[]{:S(2)}, u32[]{:S(2)}) collective-permute-start(f32[128,128]{1,0:T(8,128)S(1)} %get-tuple-element.25), channel_id=1, source_target_pairs={{0,16},{2,18},{4,20},{6,22},{8,24},{10,26},{12,28},{14,30},{16,0},... | collective-permute-start | bytes 196616 | tf_op jit(solution)/shard_map/ppermute | solution.py:629
  181.1 2.1 collective-permute-done.9
  183.2 2.0 collective-permute-done.8
  185.2 1.7 collective-permute-done.7
  187.0 4.6 %collective-permute-start.12 = (f32[128,128]{1,0:T(8,128)S(1)}, f32[128,128]{1,0:T(8,128)S(1)}, u32[]{:S(2)}, u32[]{:S(2)}) collective-permute-start(f32[128,128]{1,0:T(8,128)S(1)} %add_add_fusion.1), channel_id=1, source_target_pairs={{0,96},{2,98},{4,100},{6,102},{8,104},{10,106},{12,108},{14,110},{... | collective-permute-start | bytes 196616 | tf_op jit(solution)/shard_map/ppermute | solution.py:629
  192.2 63.8 %collective-permute-done.12 = f32[128,128]{1,0:T(8,128)S(1)} collective-permute-done((f32[128,128]{1,0:T(8,128)S(1)}, f32[128,128]{1,0:T(8,128)S(1)}, u32[]{:S(2)}, u32[]{:S(2)}) %collective-permute-start.12) | collective-permute-done | bytes 65568 | tf_op jit(solution)/shard_map/ppermute | solution.py:629
  256.0 2.2 collective-permute-done.11
  258.2 4.1 %collective-permute-start.13 = (f32[128,128]{1,0:T(8,128)S(1)}, f32[128,128]{1,0:T(8,128)S(1)}, u32[]{:S(2)}, u32[]{:S(2)}) collective-permute-start(f32[128,128]{1,0:T(8,128)S(1)} %add_add_fusion), channel_id=1, source_target_pairs={{0,128},{2,130},{4,132},{6,134},{8,136},{10,138},{12,140},{14,142}... | collective-permute-start | bytes 196616 | tf_op jit(solution)/shard_map/ppermute | solution.py:629
  262.3 4.4 %collective-permute-done.13 = f32[128,128]{1,0:T(8,128)S(1)} collective-permute-done((f32[128,128]{1,0:T(8,128)S(1)}, f32[128,128]{1,0:T(8,128)S(1)}, u32[]{:S(2)}, u32[]{:S(2)}) %collective-permute-start.13) | collective-permute-done | bytes 65568 | tf_op jit(solution)/shard_map/ppermute | solution.py:629
  266.7 2.6 collective-permute-start.16
  270.9 4.4 %finish.1 = (f32[32,128,128]{2,1,0:T(8,128)}, f32[128,128]{1,0:T(8,128)S(1)}) custom-call(s32[128]{0:T(128)S(1)} %copy-done.20, s32[2]{0:T(128)S(1)} %copy-done.21, bf16[128,136,128]{2,1,0:T(8,128)(2,1)} %all-to-all-done.1.returned, f32[32,128,128]{2,1,0:T(8,128)S(1)} %bitcast.20, f32[128,128]{1,0:T(8,128)S(1)} %add.91.grads), custom_call_target="tpu_custom_call" | custom-call | tf_op jit(solution)/shard_map/finish/pallas_call | solution.py:531
  275.4 1.3 place.1
  (91 shorter events, 10.7 us)
Async XLA Ops:
  0.6 24.5 %collective-permute-start = (bf16[4096,128]{1,0:T(8,128)(2,1)}, bf16[4096,128]{1,0:T(8,128)(2,1)S(1)}, u32[]{:S(2)}, u32[]{:S(2)}) collective-permute-start(bf16[4096,128]{1,0:T(8,128)(2,1)} %refs_1_.1), channel_id=1, source_target_pairs={{0,1},{1,0},{2,3},{3,2},{4,5},{5,4},{6,7},{7,6},{8,9},{9,8},{10,11... | collective-permute-start | bytes 3145736 | tf_op jit(solution)/shard_map/ppermute | solution.py:623
  4.7 16.0 %copy-start.22 = (bf16[128,256]{1,0:T(8,128)(2,1)S(1)}, bf16[128,256]{1,0:T(8,128)(2,1)}, u32[]{:S(2)}) copy-start(bf16[128,256]{1,0:T(8,128)(2,1)} %param.12) | copy-start | bytes 196612
  4.7 16.1 %copy-start.23 = (bf16[128,256]{1,0:T(8,128)(2,1)S(1)}, bf16[128,256]{1,0:T(8,128)(2,1)}, u32[]{:S(2)}) copy-start(bf16[128,256]{1,0:T(8,128)(2,1)} %param.13) | copy-start | bytes 196612
  4.7 16.2 %copy-start.5 = (bf16[4096,128]{1,0:T(8,128)(2,1)S(1)}, bf16[4096,128]{1,0:T(8,128)(2,1)}, u32[]{:S(2)}) copy-start(bf16[4096,128]{1,0:T(8,128)(2,1)} %refs_5_.1) | copy-start | bytes 3145732
  4.7 17.4 %copy-start.19 = (s32[160]{0:T(256)S(1)}, s32[160]{0:T(256)}, u32[]{:S(2)}) copy-start(s32[160]{0:T(256)} %row.1) | copy-start | bytes 1924
  4.8 17.5 %copy-start.24 = (s32[160]{0:T(256)S(1)}, s32[160]{0:T(256)}, u32[]{:S(2)}) copy-start(s32[160]{0:T(256)} %param.16) | copy-start | bytes 1924
  4.8 118.3 %all-to-all-start = ((bf16[128,136,128]{2,1,0:T(8,128)(2,1)}), bf16[128,136,128]{2,1,0:T(8,128)(2,1)}, u32[]{:S(2)}, u32[]{:S(2)}) async-start(bf16[128,136,128]{2,1,0:T(8,128)(2,1)} %pack.1), calls=%async_computation | async-start | bytes 8912896 | tf_op jit(solution)/shard_map/all_to_all | solution.py:619
  20.9 4.1 %collective-permute-start.1 = (bf16[256,256]{1,0:T(8,128)(2,1)S(1)}, bf16[256,256]{1,0:T(8,128)(2,1)S(1)}, u32[]{:S(2)}, u32[]{:S(2)}) collective-permute-start(bf16[256,256]{1,0:T(8,128)(2,1)S(1)} %maximum_select_fusion), channel_id=1, source_target_pairs={{0,1},{1,0},{2,3},{3,2},{4,5},{5,4},{6,7},{7,6},{8,9},{9,8},{10,11... | collective-permute-start | bytes 393224 | tf_op jit(solution)/shard_map/ppermute | solution.py:623
  21.0 4.1 %collective-permute-start.2 = (bf16[4096,128]{1,0:T(8,128)(2,1)S(1)}, bf16[4096,128]{1,0:T(8,128)(2,1)S(1)}, u32[]{:S(2)}, u32[]{:S(2)}) collective-permute-start(bf16[4096,128]{1,0:T(8,128)(2,1)S(1)} %copy-done.5), channel_id=1, source_target_pairs={{0,1},{1,0},{2,3},{3,2},{4,5},{5,4},{6,7},{7,6},{8,9},{9,8},{10,11... | collective-permute-start | bytes 3145736 | tf_op jit(solution)/shard_map/ppermute | solution.py:623
  25.0 24.9 %copy-start.15 = (bf16[256,256]{1,0:T(8,128)(2,1)}, bf16[256,256]{1,0:T(8,128)(2,1)S(1)}, u32[]{:S(2)}) copy-start(bf16[256,256]{1,0:T(8,128)(2,1)S(1)} %get-tuple-element.54.rest_1_.nbr_w.refs_8_) | copy-start | bytes 393220
  25.1 24.9 %copy-start.17 = (bf16[256,256]{1,0:T(8,128)(2,1)}, bf16[256,256]{1,0:T(8,128)(2,1)S(1)}, u32[]{:S(2)}) copy-start(bf16[256,256]{1,0:T(8,128)(2,1)S(1)} %get-tuple-element.55.rest_0_.own_w.refs_7_) | copy-start | bytes 393220
  25.1 24.9 %copy-start.9 = (bf16[4096,128]{1,0:T(8,128)(2,1)}, bf16[4096,128]{1,0:T(8,128)(2,1)S(1)}, u32[]{:S(2)}) copy-start(bf16[4096,128]{1,0:T(8,128)(2,1)S(1)} %collective-permute-done.2.rest_3_.cot_peer.refs_6_) | copy-start | bytes 3145732
  25.1 24.8 %copy-start.7 = (bf16[4096,128]{1,0:T(8,128)(2,1)}, bf16[4096,128]{1,0:T(8,128)(2,1)S(1)}, u32[]{:S(2)}) copy-start(bf16[4096,128]{1,0:T(8,128)(2,1)S(1)} %collective-permute-done.rest_2_.feat_peer.refs_2_) | copy-start | bytes 3145732
  130.8 3.1 %collective-permute-start.3 = (bf16[4096,128]{1,0:T(8,128)(2,1)}, bf16[4096,128]{1,0:T(8,128)(2,1)S(1)}, u32[]{:S(2)}, u32[]{:S(2)}) collective-permute-start(bf16[4096,128]{1,0:T(8,128)(2,1)} %gather.1.agg.refs_3_), channel_id=1, source_target_pairs={{0,1},{1,0},{2,3},{3,2},{4,5},{5,4},{6,7},{7,6},{8,9},{9,8},{10,11... | collective-permute-start | bytes 3145736 | tf_op jit(solution)/shard_map/ppermute | solution.py:623
  145.5 9.8 %copy-start.1 = (bf16[4096,128]{1,0:T(8,128)(2,1)S(1)}, bf16[4096,128]{1,0:T(8,128)(2,1)}, u32[]{:S(2)}) copy-start(bf16[4096,128]{1,0:T(8,128)(2,1)} %gather.1.agg.refs_3_) | copy-start | bytes 3145732
  145.5 9.8 %copy-start.2 = (bf16[4096,128]{1,0:T(8,128)(2,1)S(1)}, bf16[4096,128]{1,0:T(8,128)(2,1)}, u32[]{:S(2)}) copy-start(bf16[4096,128]{1,0:T(8,128)(2,1)} %refs_1_.1) | copy-start | bytes 3145732
  145.6 125.3 %all-to-all-start.1 = ((bf16[128,136,128]{2,1,0:T(8,128)(2,1)}), bf16[128,136,128]{2,1,0:T(8,128)(2,1)}, u32[]{:S(2)}, u32[]{:S(2)}) async-start(bf16[128,136,128]{2,1,0:T(8,128)(2,1)} %middle.1.refs_9_), calls=%async_computation.1 | async-start | bytes 8912896 | tf_op jit(solution)/shard_map/all_to_all | solution.py:619
  161.3 109.6 %copy-start.20 = (s32[128]{0:T(128)S(1)}, s32[128]{0:T(128)}, u32[]{:S(2)}) copy-start(s32[128]{0:T(128)} %send.3) | copy-start | bytes 1540
  161.3 109.6 %copy-start.21 = (s32[2]{0:T(128)S(1)}, s32[2]{0:T(128)}, u32[]{:S(2)}) copy-start(s32[2]{0:T(128)} %hubs.3) | copy-start | bytes 28
  165.7 8.4 %collective-permute-start.6 = (f32[128,128]{1,0:T(8,128)S(1)}, f32[128,128]{1,0:T(8,128)S(1)}, u32[]{:S(2)}, u32[]{:S(2)}) collective-permute-start(f32[128,128]{1,0:T(8,128)S(1)} %get-tuple-element.45), channel_id=1, source_target_pairs={{0,6},{2,4},{4,2},{6,0},{8,14},{10,12},{12,10},{14,8},{16,22},{18,... | collective-permute-start | bytes 196616 | tf_op jit(solution)/shard_map/ppermute | solution.py:629
  168.5 6.6 %collective-permute-start.5 = (f32[128,128]{1,0:T(8,128)S(1)}, f32[128,128]{1,0:T(8,128)S(1)}, u32[]{:S(2)}, u32[]{:S(2)}) collective-permute-start(f32[128,128]{1,0:T(8,128)S(1)} %get-tuple-element.46), channel_id=1, source_target_pairs={{0,4},{2,6},{4,0},{6,2},{8,12},{10,14},{12,8},{14,10},{16,20},{18,... | collective-permute-start | bytes 196616 | tf_op jit(solution)/shard_map/ppermute | solution.py:629
  169.3 6.1 %collective-permute-start.4 = (f32[128,128]{1,0:T(8,128)S(1)}, f32[128,128]{1,0:T(8,128)S(1)}, u32[]{:S(2)}, u32[]{:S(2)}) collective-permute-start(f32[128,128]{1,0:T(8,128)S(1)} %get-tuple-element.47), channel_id=1, source_target_pairs={{0,2},{2,0},{4,6},{6,4},{8,10},{10,8},{12,14},{14,12},{16,18},{18,... | collective-permute-start | bytes 196616 | tf_op jit(solution)/shard_map/ppermute | solution.py:629
  176.1 7.1 %collective-permute-start.9 = (f32[128,128]{1,0:T(8,128)S(1)}, f32[128,128]{1,0:T(8,128)S(1)}, u32[]{:S(2)}, u32[]{:S(2)}) collective-permute-start(f32[128,128]{1,0:T(8,128)S(1)} %get-tuple-element.25), channel_id=1, source_target_pairs={{0,24},{2,26},{4,28},{6,30},{8,16},{10,18},{12,20},{14,22},{16,8},... | collective-permute-start | bytes 196616 | tf_op jit(solution)/shard_map/ppermute | solution.py:629
  177.9 7.3 %collective-permute-start.8 = (f32[128,128]{1,0:T(8,128)S(1)}, f32[128,128]{1,0:T(8,128)S(1)}, u32[]{:S(2)}, u32[]{:S(2)}) collective-permute-start(f32[128,128]{1,0:T(8,128)S(1)} %get-tuple-element.25), channel_id=1, source_target_pairs={{0,16},{2,18},{4,20},{6,22},{8,24},{10,26},{12,28},{14,30},{16,0},... | collective-permute-start | bytes 196616 | tf_op jit(solution)/shard_map/ppermute | solution.py:629
  181.1 5.9 %collective-permute-start.7 = (f32[128,128]{1,0:T(8,128)S(1)}, f32[128,128]{1,0:T(8,128)S(1)}, u32[]{:S(2)}, u32[]{:S(2)}) collective-permute-start(f32[128,128]{1,0:T(8,128)S(1)} %get-tuple-element.25), channel_id=1, source_target_pairs={{0,8},{2,10},{4,12},{6,14},{8,0},{10,2},{12,4},{14,6},{16,24},{18,... | collective-permute-start | bytes 196616 | tf_op jit(solution)/shard_map/ppermute | solution.py:629
  187.0 69.1 %collective-permute-start.12 = (f32[128,128]{1,0:T(8,128)S(1)}, f32[128,128]{1,0:T(8,128)S(1)}, u32[]{:S(2)}, u32[]{:S(2)}) collective-permute-start(f32[128,128]{1,0:T(8,128)S(1)} %add_add_fusion.1), channel_id=1, source_target_pairs={{0,96},{2,98},{4,100},{6,102},{8,104},{10,106},{12,108},{14,110},{... | collective-permute-start | bytes 196616 | tf_op jit(solution)/shard_map/ppermute | solution.py:629
  191.6 66.6 %collective-permute-start.11 = (f32[128,128]{1,0:T(8,128)S(1)}, f32[128,128]{1,0:T(8,128)S(1)}, u32[]{:S(2)}, u32[]{:S(2)}) collective-permute-start(f32[128,128]{1,0:T(8,128)S(1)} %add_add_fusion.1), channel_id=1, source_target_pairs={{0,64},{2,66},{4,68},{6,70},{8,72},{10,74},{12,76},{14,78},{16,80}... | collective-permute-start | bytes 196616 | tf_op jit(solution)/shard_map/ppermute | solution.py:629
  191.6 66.6 %collective-permute-start.10 = (f32[128,128]{1,0:T(8,128)S(1)}, f32[128,128]{1,0:T(8,128)S(1)}, u32[]{:S(2)}, u32[]{:S(2)}) collective-permute-start(f32[128,128]{1,0:T(8,128)S(1)} %add_add_fusion.1), channel_id=1, source_target_pairs={{0,32},{2,34},{4,36},{6,38},{8,40},{10,42},{12,44},{14,46},{16,48}... | collective-permute-start | bytes 196616 | tf_op jit(solution)/shard_map/ppermute | solution.py:629
  258.2 8.5 %collective-permute-start.13 = (f32[128,128]{1,0:T(8,128)S(1)}, f32[128,128]{1,0:T(8,128)S(1)}, u32[]{:S(2)}, u32[]{:S(2)}) collective-permute-start(f32[128,128]{1,0:T(8,128)S(1)} %add_add_fusion), channel_id=1, source_target_pairs={{0,128},{2,130},{4,132},{6,134},{8,136},{10,138},{12,140},{14,142}... | collective-permute-start | bytes 196616 | tf_op jit(solution)/shard_map/ppermute | solution.py:629
  266.7 8.6 %collective-permute-start.16 = (f32[128,128]{1,0:T(8,128)S(1)}, f32[128,128]{1,0:T(8,128)S(1)}, u32[]{:S(2)}, u32[]{:S(2)}) collective-permute-start(f32[128,128]{1,0:T(8,128)S(1)} %add.91.grads), channel_id=1, source_target_pairs={{0,6},{2,4},{4,2},{6,0},{8,14},{10,12},{12,10},{14,8},{16,22},{18,... | collective-permute-start | bytes 196616 | tf_op jit(solution)/shard_map/ppermute | solution.py:629
  269.3 6.0 %collective-permute-start.15 = (f32[128,128]{1,0:T(8,128)S(1)}, f32[128,128]{1,0:T(8,128)S(1)}, u32[]{:S(2)}, u32[]{:S(2)}) collective-permute-start(f32[128,128]{1,0:T(8,128)S(1)} %add.91.grads), channel_id=1, source_target_pairs={{0,4},{2,6},{4,0},{6,2},{8,12},{10,14},{12,8},{14,10},{16,20},{18,... | collective-permute-start | bytes 196616 | tf_op jit(solution)/shard_map/ppermute | solution.py:629
  270.3 5.0 %collective-permute-start.14 = (f32[128,128]{1,0:T(8,128)S(1)}, f32[128,128]{1,0:T(8,128)S(1)}, u32[]{:S(2)}, u32[]{:S(2)}) collective-permute-start(f32[128,128]{1,0:T(8,128)S(1)} %add.91.grads), channel_id=1, source_target_pairs={{0,2},{2,0},{4,6},{6,4},{8,10},{10,8},{12,14},{14,12},{16,18},{18,... | collective-permute-start | bytes 196616 | tf_op jit(solution)/shard_map/ppermute | solution.py:629
  (12 other events, 43.8 us)

commit v6 on v5

--- a/solution.py
+++ b/solution.py
@@ -695,12 +695,13 @@
     direct, grads = direct_part(slopes, own_w[:half], grads)
     grads = total(grads, [move(grads, "x", i) for i in (1, 2, 3)])
     grads = total(grads, [move(grads, "z", i) for i in (1, 2, 3)])
-    grads = grads + move(grads, "z", 4)
-    near = [move(grads, "y", i) for i in (1, 2, 3)]
+    far = move(grads, "z", 4)
     input_grad, grads = finish(
         send_tile, hub_rows, returned, direct.reshape(tiles_dev, tile_edge, half), grads
     )
     input_grad = input_grad.reshape(rows_dev, half)
+    grads = grads + far
+    near = [move(grads, "y", i) for i in (1, 2, 3)]
     self_grad, neighbor_grad = put_in_place(
         where, [grads] + near, 1.0 / math.sqrt(rows_dev * dom_size)
     )

time: 278 us -> 277 us (level)
  transfers between devices with their start and end apart: 19 -> 19, of which waited for: 11 -> 12; matrix products, arithmetic and copies ran while one was open for 1% -> 1% of each run, Pallas kernels for 13% -> 13%
where the time goes in v6:
time: 277 us
  waiting for transfers between devices  153 us (55%)
  Pallas kernels  55.4 us (20%)
  starting transfers between devices  49.4 us (18%)
  local copies, waits for them, and re-layouts  14.5 us (5%)
  other arithmetic  2.98 us (1%)
    ppermute x13, waiting for transfers between devices, move(): return lax.ppermute(block, 'dom', pairs)  81.8 us
    all_to_all x2, waiting for transfers between devices, exchange(): return lax.all_to_all(block, 'dom', split_axis=0, concat_axis=0, tiled=True)  68.1 us
    all_to_all x2, starting transfers between devices, exchange(): return lax.all_to_all(block, 'dom', split_axis=0, concat_axis=0, tiled=True)  25.9 us
    ppermute x13, starting transfers between devices, move(): return lax.ppermute(block, 'dom', pairs)  22.5 us
    pallas_call x1, Pallas kernels, prepare(): pl.pallas_call(prepare_kernel, name='prepare', out_shape=(jax.ShapeDtypeS...  22.4 us
    unnamed x51, local copies, waits for them, and re-layouts  14.4 us
    pallas_call x1, Pallas kernels, middle(): pl.pallas_call(middle_kernel, name='middle', out_shape=jax.ShapeDtypeStru...  10.5 us
    pallas_call x1, Pallas kernels, gather(): pl.pallas_call(gather_kernel, name='gather', out_shape=jax.ShapeDtypeStru...  7.71 us
  transfers between devices with their start and end apart: 19, of which 12 were waited for; matrix products, arithmetic and copies ran while one was open for 1% of the time, Pallas kernels for 13%

profile of v6, /device:TPU:2, one launch (start us, length us, event | category | flops | bytes accessed | tf_op | source)
XLA Modules:
  0.0 276.8 jit_solution(4044511306053087644)
XLA Ops:
  0.7 4.0 %pack.1 = bf16[128,136,128]{2,1,0:T(8,128)(2,1)} custom-call(s32[128]{0:T(128)} %send.3, s32[2]{0:T(128)} %hubs.3, bf16[4096,128]{1,0:T(8,128)(2,1)} %refs_1_.1), custom_call_target="tpu_custom_call" | custom-call | tf_op jit(solution)/shard_map/pack/pallas_call | solution.py:71
  4.8 16.0 %all-to-all-start = ((bf16[128,136,128]{2,1,0:T(8,128)(2,1)}), bf16[128,136,128]{2,1,0:T(8,128)(2,1)}, u32[]{:S(2)}, u32[]{:S(2)}) async-start(bf16[128,136,128]{2,1,0:T(8,128)(2,1)} %pack.1), calls=%async_computation | async-start | bytes 8912896 | tf_op jit(solution)/shard_map/all_to_all | solution.py:619
  25.1 2.4 copy-done.13
  27.5 22.4 %prepare.1 = (f32[4096,128]{1,0:T(8,128)S(1)}, bf16[160,128,128]{2,1,0:T(8,128)(2,1)S(1)}, bf16[96,128,256]{2,1,0:T(8,128)(2,1)}, bf16[256,4096]{1,0:T(8,128)(2,1)S(1)}) custom-call(s32[160]{0:T(256)S(1)} %copy-done.19, s32[1]{0:T(128)} %copy.16.count, s32[160]{0:T(256)S(1)} %get-tuple-element.32.order, s32[96]{0:T(128)S(1)} %get-tuple-element.36.first, ...), custom_call_target="tpu_custom_call" | custom-call | flops 60000002048 | bytes 40000000 | tf_op jit(solution)/shard_map/prepare/pallas_call | solution.py:139
  50.0 1.3 copy-done.3
  51.3 2.4 copy-done.4
  53.6 1.3 copy-done.14
  55.0 68.1 %all-to-all-done.incoming = bf16[128,136,128]{2,1,0:T(8,128)(2,1)} async-done(((bf16[128,136,128]{2,1,0:T(8,128)(2,1)}), bf16[128,136,128]{2,1,0:T(8,128)(2,1)}, u32[]{:S(2)}, u32[]{:S(2)}) %all-to-all-start) | async-done | bytes 4456480 | tf_op jit(solution)/shard_map/all_to_all | solution.py:619
  123.0 7.7 %gather.1.agg.refs_3_ = bf16[4096,128]{1,0:T(8,128)(2,1)} custom-call(s32[96]{0:T(128)} %get-tuple-element.37.row, s32[96]{0:T(128)} %get-tuple-element.34.owner_a, s32[96]{0:T(128)} %get-tuple-element.33.owner_b, s32[1]{0:T(128)} %bitcast.3.n_duos, bf16[96,128,256]{2,1,0:T(8,128)(2,1)} %get-tuple-element.17.pairs, ...), custom_call_target="tpu_custom_call" | custom-call | tf_op jit(solution)/shard_map/gather/pallas_call | solution.py:242
  131.0 2.9 %collective-permute-done.3.agg_peer.refs_4_ = bf16[4096,128]{1,0:T(8,128)(2,1)S(1)} collective-permute-done((bf16[4096,128]{1,0:T(8,128)(2,1)}, bf16[4096,128]{1,0:T(8,128)(2,1)S(1)}, u32[]{:S(2)}, u32[]{:S(2)}) %collective-permute-start.3) | collective-permute-done | bytes 1048608 | tf_op jit(solution)/shard_map/ppermute | solution.py:623
  134.9 10.5 %middle.1.refs_9_ = bf16[128,136,128]{2,1,0:T(8,128)(2,1)} custom-call(s32[160]{0:T(256)} %get-tuple-element.31.order_row, s32[160]{0:T(256)} %get-tuple-element.30.order_owner, s32[1]{0:T(128)} %copy.16.count, bf16[4096,128]{1,0:T(8,128)(2,1)} %refs_1_.1, bf16[4096,128]{1,0:T(8,128)(2,1)} %copy-done.7, bf16[4096,128]{1,0:T(8,128)(2,1)} %gather.1.agg.refs_3_, ...), custom_call_target="tpu_custom_call" | custom-call | tf_op jit(solution)/shard_map/middle/pallas_call | solution.py:381
  145.5 9.9 %all-to-all-start.1 = ((bf16[128,136,128]{2,1,0:T(8,128)(2,1)}), bf16[128,136,128]{2,1,0:T(8,128)(2,1)}, u32[]{:S(2)}, u32[]{:S(2)}) async-start(bf16[128,136,128]{2,1,0:T(8,128)(2,1)} %middle.1.refs_9_), calls=%async_computation.1 | async-start | bytes 8912896 | tf_op jit(solution)/shard_map/all_to_all | solution.py:619
  155.5 2.3 copy-done
  159.0 1.2 copy-done.10
  160.2 1.2 copy-done.12
  161.5 4.4 %side.1 = (bf16[4096,128]{1,0:T(8,128)(2,1)}, bf16[4096,256]{1,0:T(8,128)(2,1)S(1)}, f32[4,128,128]{2,1,0:T(8,128)S(1)}) custom-call(s32[2]{0:T(128)S(1)} %pad_add_fusion.refs_0_, bf16[4096,128]{1,0:T(8,128)(2,1)S(1)} %copy-done.2, bf16[4096,128]{1,0:T(8,128)(2,1)S(1)} %copy-done.8, bf16[4096,128]{1,0:T(8,128)(2,1)S(1)} %copy-done.1, ...), custom_call_target="tpu_custom_call" | custom-call | tf_op jit(solution)/shard_map/side/pallas_call | solution.py:450
  165.9 2.8 collective-permute-start.6
  170.0 4.2 %collective-permute-done.6 = f32[128,128]{1,0:T(8,128)S(1)} collective-permute-done((f32[128,128]{1,0:T(8,128)S(1)}, f32[128,128]{1,0:T(8,128)S(1)}, u32[]{:S(2)}, u32[]{:S(2)}) %collective-permute-start.6) | collective-permute-done | bytes 65568 | tf_op jit(solution)/shard_map/ppermute | solution.py:629
  176.2 1.8 collective-permute-start.9
  178.0 3.2 %collective-permute-start.8 = (f32[128,128]{1,0:T(8,128)S(1)}, f32[128,128]{1,0:T(8,128)S(1)}, u32[]{:S(2)}, u32[]{:S(2)}) collective-permute-start(f32[128,128]{1,0:T(8,128)S(1)} %get-tuple-element.25), channel_id=1, source_target_pairs={{0,16},{2,18},{4,20},{6,22},{8,24},{10,26},{12,28},{14,30},{16,0},... | collective-permute-start | bytes 196616 | tf_op jit(solution)/shard_map/ppermute | solution.py:629
  181.2 2.1 collective-permute-done.9
  183.3 2.1 collective-permute-done.8
  185.4 1.7 collective-permute-done.7
  187.1 4.5 %collective-permute-start.12 = (f32[128,128]{1,0:T(8,128)S(1)}, f32[128,128]{1,0:T(8,128)S(1)}, u32[]{:S(2)}, u32[]{:S(2)}) collective-permute-start(f32[128,128]{1,0:T(8,128)S(1)} %add_add_fusion.1), channel_id=1, source_target_pairs={{0,96},{2,98},{4,100},{6,102},{8,104},{10,106},{12,108},{14,110},{... | collective-permute-start | bytes 196616 | tf_op jit(solution)/shard_map/ppermute | solution.py:629
  192.2 64.0 %collective-permute-done.12 = f32[128,128]{1,0:T(8,128)S(1)} collective-permute-done((f32[128,128]{1,0:T(8,128)S(1)}, f32[128,128]{1,0:T(8,128)S(1)}, u32[]{:S(2)}, u32[]{:S(2)}) %collective-permute-start.12) | collective-permute-done | bytes 65568 | tf_op jit(solution)/shard_map/ppermute | solution.py:629
  256.2 2.1 collective-permute-done.11
  258.4 4.1 %collective-permute-start.13 = (f32[128,128]{1,0:T(8,128)S(1)}, f32[128,128]{1,0:T(8,128)S(1)}, u32[]{:S(2)}, u32[]{:S(2)}) collective-permute-start(f32[128,128]{1,0:T(8,128)S(1)} %add_add_fusion.grads), channel_id=1, source_target_pairs={{0,128},{2,130},{4,132},{6,134},{8,136},{10,138},{12,140},{14,142}... | collective-permute-start | bytes 196616 | tf_op jit(solution)/shard_map/ppermute | solution.py:629
  262.5 4.4 %finish.1 = (f32[32,128,128]{2,1,0:T(8,128)}, f32[128,128]{1,0:T(8,128)S(1)}) custom-call(s32[128]{0:T(128)S(1)} %copy-done.20, s32[2]{0:T(128)S(1)} %copy-done.21, bf16[128,136,128]{2,1,0:T(8,128)(2,1)} %all-to-all-done.1.returned, f32[32,128,128]{2,1,0:T(8,128)S(1)} %bitcast.20, f32[128,128]{1,0:T(8,128)S(1)} %add_add_fusion.grads), custom_call_target="tpu_custom_call" | custom-call | tf_op jit(solution)/shard_map/finish/pallas_call | solution.py:531
  266.9 2.8 %collective-permute-start.16 = (f32[128,128]{1,0:T(8,128)S(1)}, f32[128,128]{1,0:T(8,128)S(1)}, u32[]{:S(2)}, u32[]{:S(2)}) collective-permute-start(f32[128,128]{1,0:T(8,128)S(1)} %add.91.refs_1_), channel_id=1, source_target_pairs={{0,6},{2,4},{4,2},{6,0},{8,14},{10,12},{12,10},{14,8},{16,22},{18,... | collective-permute-start | bytes 196616 | tf_op jit(solution)/shard_map/ppermute | solution.py:629
  271.1 1.4 collective-permute-done.16.refs_4_
  272.5 3.0 %collective-permute-done.15.refs_3_ = f32[128,128]{1,0:T(8,128)S(1)} collective-permute-done((f32[128,128]{1,0:T(8,128)S(1)}, f32[128,128]{1,0:T(8,128)S(1)}, u32[]{:S(2)}, u32[]{:S(2)}) %collective-permute-start.15) | collective-permute-done | bytes 65568 | tf_op jit(solution)/shard_map/ppermute | solution.py:629
  275.5 1.3 place.1
  (91 shorter events, 11.8 us)
Async XLA Ops:
  0.6 24.5 %collective-permute-start = (bf16[4096,128]{1,0:T(8,128)(2,1)}, bf16[4096,128]{1,0:T(8,128)(2,1)S(1)}, u32[]{:S(2)}, u32[]{:S(2)}) collective-permute-start(bf16[4096,128]{1,0:T(8,128)(2,1)} %refs_1_.1), channel_id=1, source_target_pairs={{0,1},{1,0},{2,3},{3,2},{4,5},{5,4},{6,7},{7,6},{8,9},{9,8},{10,11... | collective-permute-start | bytes 3145736 | tf_op jit(solution)/shard_map/ppermute | solution.py:623
  4.7 16.0 %copy-start.22 = (bf16[128,256]{1,0:T(8,128)(2,1)S(1)}, bf16[128,256]{1,0:T(8,128)(2,1)}, u32[]{:S(2)}) copy-start(bf16[128,256]{1,0:T(8,128)(2,1)} %param.12) | copy-start | bytes 196612
  4.7 16.1 %copy-start.23 = (bf16[128,256]{1,0:T(8,128)(2,1)S(1)}, bf16[128,256]{1,0:T(8,128)(2,1)}, u32[]{:S(2)}) copy-start(bf16[128,256]{1,0:T(8,128)(2,1)} %param.13) | copy-start | bytes 196612
  4.7 16.2 %copy-start.5 = (bf16[4096,128]{1,0:T(8,128)(2,1)S(1)}, bf16[4096,128]{1,0:T(8,128)(2,1)}, u32[]{:S(2)}) copy-start(bf16[4096,128]{1,0:T(8,128)(2,1)} %refs_5_.1) | copy-start | bytes 3145732
  4.7 17.4 %copy-start.19 = (s32[160]{0:T(256)S(1)}, s32[160]{0:T(256)}, u32[]{:S(2)}) copy-start(s32[160]{0:T(256)} %row.1) | copy-start | bytes 1924
  4.8 17.5 %copy-start.24 = (s32[160]{0:T(256)S(1)}, s32[160]{0:T(256)}, u32[]{:S(2)}) copy-start(s32[160]{0:T(256)} %param.16) | copy-start | bytes 1924
  4.8 118.3 %all-to-all-start = ((bf16[128,136,128]{2,1,0:T(8,128)(2,1)}), bf16[128,136,128]{2,1,0:T(8,128)(2,1)}, u32[]{:S(2)}, u32[]{:S(2)}) async-start(bf16[128,136,128]{2,1,0:T(8,128)(2,1)} %pack.1), calls=%async_computation | async-start | bytes 8912896 | tf_op jit(solution)/shard_map/all_to_all | solution.py:619
  20.9 4.1 %collective-permute-start.1 = (bf16[256,256]{1,0:T(8,128)(2,1)S(1)}, bf16[256,256]{1,0:T(8,128)(2,1)S(1)}, u32[]{:S(2)}, u32[]{:S(2)}) collective-permute-start(bf16[256,256]{1,0:T(8,128)(2,1)S(1)} %maximum_select_fusion), channel_id=1, source_target_pairs={{0,1},{1,0},{2,3},{3,2},{4,5},{5,4},{6,7},{7,6},{8,9},{9,8},{10,11... | collective-permute-start | bytes 393224 | tf_op jit(solution)/shard_map/ppermute | solution.py:623
  21.0 4.1 %collective-permute-start.2 = (bf16[4096,128]{1,0:T(8,128)(2,1)S(1)}, bf16[4096,128]{1,0:T(8,128)(2,1)S(1)}, u32[]{:S(2)}, u32[]{:S(2)}) collective-permute-start(bf16[4096,128]{1,0:T(8,128)(2,1)S(1)} %copy-done.5), channel_id=1, source_target_pairs={{0,1},{1,0},{2,3},{3,2},{4,5},{5,4},{6,7},{7,6},{8,9},{9,8},{10,11... | collective-permute-start | bytes 3145736 | tf_op jit(solution)/shard_map/ppermute | solution.py:623
  25.0 24.9 %copy-start.15 = (bf16[256,256]{1,0:T(8,128)(2,1)}, bf16[256,256]{1,0:T(8,128)(2,1)S(1)}, u32[]{:S(2)}) copy-start(bf16[256,256]{1,0:T(8,128)(2,1)S(1)} %get-tuple-element.54.rest_1_.nbr_w.refs_8_) | copy-start | bytes 393220
  25.1 24.9 %copy-start.17 = (bf16[256,256]{1,0:T(8,128)(2,1)}, bf16[256,256]{1,0:T(8,128)(2,1)S(1)}, u32[]{:S(2)}) copy-start(bf16[256,256]{1,0:T(8,128)(2,1)S(1)} %get-tuple-element.55.rest_0_.own_w.refs_7_) | copy-start | bytes 393220
  25.1 24.9 %copy-start.9 = (bf16[4096,128]{1,0:T(8,128)(2,1)}, bf16[4096,128]{1,0:T(8,128)(2,1)S(1)}, u32[]{:S(2)}) copy-start(bf16[4096,128]{1,0:T(8,128)(2,1)S(1)} %collective-permute-done.2.rest_3_.cot_peer.refs_6_) | copy-start | bytes 3145732
  25.1 24.8 %copy-start.7 = (bf16[4096,128]{1,0:T(8,128)(2,1)}, bf16[4096,128]{1,0:T(8,128)(2,1)S(1)}, u32[]{:S(2)}) copy-start(bf16[4096,128]{1,0:T(8,128)(2,1)S(1)} %collective-permute-done.rest_2_.feat_peer.refs_2_) | copy-start | bytes 3145732
  130.8 3.1 %collective-permute-start.3 = (bf16[4096,128]{1,0:T(8,128)(2,1)}, bf16[4096,128]{1,0:T(8,128)(2,1)S(1)}, u32[]{:S(2)}, u32[]{:S(2)}) collective-permute-start(bf16[4096,128]{1,0:T(8,128)(2,1)} %gather.1.agg.refs_3_), channel_id=1, source_target_pairs={{0,1},{1,0},{2,3},{3,2},{4,5},{5,4},{6,7},{7,6},{8,9},{9,8},{10,11... | collective-permute-start | bytes 3145736 | tf_op jit(solution)/shard_map/ppermute | solution.py:623
  145.4 10.1 %copy-start.1 = (bf16[4096,128]{1,0:T(8,128)(2,1)S(1)}, bf16[4096,128]{1,0:T(8,128)(2,1)}, u32[]{:S(2)}) copy-start(bf16[4096,128]{1,0:T(8,128)(2,1)} %gather.1.agg.refs_3_) | copy-start | bytes 3145732
  145.4 10.1 %copy-start.2 = (bf16[4096,128]{1,0:T(8,128)(2,1)S(1)}, bf16[4096,128]{1,0:T(8,128)(2,1)}, u32[]{:S(2)}) copy-start(bf16[4096,128]{1,0:T(8,128)(2,1)} %refs_1_.1) | copy-start | bytes 3145732
  145.5 117.0 %all-to-all-start.1 = ((bf16[128,136,128]{2,1,0:T(8,128)(2,1)}), bf16[128,136,128]{2,1,0:T(8,128)(2,1)}, u32[]{:S(2)}, u32[]{:S(2)}) async-start(bf16[128,136,128]{2,1,0:T(8,128)(2,1)} %middle.1.refs_9_), calls=%async_computation.1 | async-start | bytes 8912896 | tf_op jit(solution)/shard_map/all_to_all | solution.py:619
  161.4 101.0 %copy-start.20 = (s32[128]{0:T(128)S(1)}, s32[128]{0:T(128)}, u32[]{:S(2)}) copy-start(s32[128]{0:T(128)} %send.3) | copy-start | bytes 1540
  161.4 101.0 %copy-start.21 = (s32[2]{0:T(128)S(1)}, s32[2]{0:T(128)}, u32[]{:S(2)}) copy-start(s32[2]{0:T(128)} %hubs.3) | copy-start | bytes 28
  165.9 8.3 %collective-permute-start.6 = (f32[128,128]{1,0:T(8,128)S(1)}, f32[128,128]{1,0:T(8,128)S(1)}, u32[]{:S(2)}, u32[]{:S(2)}) collective-permute-start(f32[128,128]{1,0:T(8,128)S(1)} %get-tuple-element.45), channel_id=1, source_target_pairs={{0,6},{2,4},{4,2},{6,0},{8,14},{10,12},{12,10},{14,8},{16,22},{18,... | collective-permute-start | bytes 196616 | tf_op jit(solution)/shard_map/ppermute | solution.py:629
  168.6 6.5 %collective-permute-start.5 = (f32[128,128]{1,0:T(8,128)S(1)}, f32[128,128]{1,0:T(8,128)S(1)}, u32[]{:S(2)}, u32[]{:S(2)}) collective-permute-start(f32[128,128]{1,0:T(8,128)S(1)} %get-tuple-element.46), channel_id=1, source_target_pairs={{0,4},{2,6},{4,0},{6,2},{8,12},{10,14},{12,8},{14,10},{16,20},{18,... | collective-permute-start | bytes 196616 | tf_op jit(solution)/shard_map/ppermute | solution.py:629
  169.5 6.0 %collective-permute-start.4 = (f32[128,128]{1,0:T(8,128)S(1)}, f32[128,128]{1,0:T(8,128)S(1)}, u32[]{:S(2)}, u32[]{:S(2)}) collective-permute-start(f32[128,128]{1,0:T(8,128)S(1)} %get-tuple-element.47), channel_id=1, source_target_pairs={{0,2},{2,0},{4,6},{6,4},{8,10},{10,8},{12,14},{14,12},{16,18},{18,... | collective-permute-start | bytes 196616 | tf_op jit(solution)/shard_map/ppermute | solution.py:629
  176.2 7.0 %collective-permute-start.9 = (f32[128,128]{1,0:T(8,128)S(1)}, f32[128,128]{1,0:T(8,128)S(1)}, u32[]{:S(2)}, u32[]{:S(2)}) collective-permute-start(f32[128,128]{1,0:T(8,128)S(1)} %get-tuple-element.25), channel_id=1, source_target_pairs={{0,24},{2,26},{4,28},{6,30},{8,16},{10,18},{12,20},{14,22},{16,8},... | collective-permute-start | bytes 196616 | tf_op jit(solution)/shard_map/ppermute | solution.py:629
  178.0 7.4 %collective-permute-start.8 = (f32[128,128]{1,0:T(8,128)S(1)}, f32[128,128]{1,0:T(8,128)S(1)}, u32[]{:S(2)}, u32[]{:S(2)}) collective-permute-start(f32[128,128]{1,0:T(8,128)S(1)} %get-tuple-element.25), channel_id=1, source_target_pairs={{0,16},{2,18},{4,20},{6,22},{8,24},{10,26},{12,28},{14,30},{16,0},... | collective-permute-start | bytes 196616 | tf_op jit(solution)/shard_map/ppermute | solution.py:629
  181.2 5.9 %collective-permute-start.7 = (f32[128,128]{1,0:T(8,128)S(1)}, f32[128,128]{1,0:T(8,128)S(1)}, u32[]{:S(2)}, u32[]{:S(2)}) collective-permute-start(f32[128,128]{1,0:T(8,128)S(1)} %get-tuple-element.25), channel_id=1, source_target_pairs={{0,8},{2,10},{4,12},{6,14},{8,0},{10,2},{12,4},{14,6},{16,24},{18,... | collective-permute-start | bytes 196616 | tf_op jit(solution)/shard_map/ppermute | solution.py:629
  187.1 69.1 %collective-permute-start.12 = (f32[128,128]{1,0:T(8,128)S(1)}, f32[128,128]{1,0:T(8,128)S(1)}, u32[]{:S(2)}, u32[]{:S(2)}) collective-permute-start(f32[128,128]{1,0:T(8,128)S(1)} %add_add_fusion.1), channel_id=1, source_target_pairs={{0,96},{2,98},{4,100},{6,102},{8,104},{10,106},{12,108},{14,110},{... | collective-permute-start | bytes 196616 | tf_op jit(solution)/shard_map/ppermute | solution.py:629
  191.5 66.8 %collective-permute-start.11 = (f32[128,128]{1,0:T(8,128)S(1)}, f32[128,128]{1,0:T(8,128)S(1)}, u32[]{:S(2)}, u32[]{:S(2)}) collective-permute-start(f32[128,128]{1,0:T(8,128)S(1)} %add_add_fusion.1), channel_id=1, source_target_pairs={{0,64},{2,66},{4,68},{6,70},{8,72},{10,74},{12,76},{14,78},{16,80}... | collective-permute-start | bytes 196616 | tf_op jit(solution)/shard_map/ppermute | solution.py:629
  191.5 66.8 %collective-permute-start.10 = (f32[128,128]{1,0:T(8,128)S(1)}, f32[128,128]{1,0:T(8,128)S(1)}, u32[]{:S(2)}, u32[]{:S(2)}) collective-permute-start(f32[128,128]{1,0:T(8,128)S(1)} %add_add_fusion.1), channel_id=1, source_target_pairs={{0,32},{2,34},{4,36},{6,38},{8,40},{10,42},{12,44},{14,46},{16,48}... | collective-permute-start | bytes 196616 | tf_op jit(solution)/shard_map/ppermute | solution.py:629
  258.4 8.5 %collective-permute-start.13 = (f32[128,128]{1,0:T(8,128)S(1)}, f32[128,128]{1,0:T(8,128)S(1)}, u32[]{:S(2)}, u32[]{:S(2)}) collective-permute-start(f32[128,128]{1,0:T(8,128)S(1)} %add_add_fusion.grads), channel_id=1, source_target_pairs={{0,128},{2,130},{4,132},{6,134},{8,136},{10,138},{12,140},{14,142}... | collective-permute-start | bytes 196616 | tf_op jit(solution)/shard_map/ppermute | solution.py:629
  266.9 5.6 %collective-permute-start.16 = (f32[128,128]{1,0:T(8,128)S(1)}, f32[128,128]{1,0:T(8,128)S(1)}, u32[]{:S(2)}, u32[]{:S(2)}) collective-permute-start(f32[128,128]{1,0:T(8,128)S(1)} %add.91.refs_1_), channel_id=1, source_target_pairs={{0,6},{2,4},{4,2},{6,0},{8,14},{10,12},{12,10},{14,8},{16,22},{18,... | collective-permute-start | bytes 196616 | tf_op jit(solution)/shard_map/ppermute | solution.py:629
  269.7 5.8 %collective-permute-start.15 = (f32[128,128]{1,0:T(8,128)S(1)}, f32[128,128]{1,0:T(8,128)S(1)}, u32[]{:S(2)}, u32[]{:S(2)}) collective-permute-start(f32[128,128]{1,0:T(8,128)S(1)} %add.91.refs_1_), channel_id=1, source_target_pairs={{0,4},{2,6},{4,0},{6,2},{8,12},{10,14},{12,8},{14,10},{16,20},{18,... | collective-permute-start | bytes 196616 | tf_op jit(solution)/shard_map/ppermute | solution.py:629
  270.5 4.9 %collective-permute-start.14 = (f32[128,128]{1,0:T(8,128)S(1)}, f32[128,128]{1,0:T(8,128)S(1)}, u32[]{:S(2)}, u32[]{:S(2)}) collective-permute-start(f32[128,128]{1,0:T(8,128)S(1)} %add.91.refs_1_), channel_id=1, source_target_pairs={{0,2},{2,0},{4,6},{6,4},{8,10},{10,8},{12,14},{14,12},{16,18},{18,... | collective-permute-start | bytes 196616 | tf_op jit(solution)/shard_map/ppermute | solution.py:629
  (12 other events, 44.6 us)
